TPU v7x, 256 devices: a whole 4x4x8 slice. The times are simulated.
256 devices in a mesh: fac: 32 (over y, z), scn: 8 (over x, core).
Axes of the slice: x: 4, y: 4, z: 8, core: 2. Of those that a mesh axis runs over, the one named last changes fastest.
Arguments:
- loadings: bfloat16 [196608, 512], P('fac'), may hold values from -0.25 to 0.25
- draws: bfloat16 [512, 6144], P(None, 'scn'), may hold values from -6 to 6
- delta: float32 [196608], P('fac'), may hold values from -0.013671875 to 0.013671875
- gamma: bfloat16 [512, 128, 128], P('fac', 'scn'), may hold values from -0.0014648438 to 0.0014648438
- pair_rows: int32 [512], replicated, may hold values from 0 to 1535, as said below
- pair_cols: int32 [512], replicated, may hold values from 0 to 1535, as said below
- pair_count: int32 [32], replicated, may hold values from 4 to 16, as said below
Outputs:
- pnl: float32 [6144], P('scn')
Inputs may be any that keep to these rules, and one draw needn't show every extreme that they name: Block numbers of the slots; for every owner o, among the 32 entries pair_rows and pair_cols of its slots (live or not), the blocks of each index h of fac (blocks h * 48 to h * 48 + 47) are named at most 2 times, and for every owner some index h is named exactly 2 times. `pair_cols`: see pair_rows; the bound holds with both lists together. An owner's live slots are its first pair_count slots; some owner has all 16 slots live.
All inputs are finite; a program needn't handle non-finite values.
Results may differ from a plain program's by a relative error of at most 0.002.
Values may be sent and summed in bfloat16 or wider, within the bound.
No kernel may reach another device: no remote copies, remote signals or barrier semaphores. Data moves between devices by JAX's collectives and lax.ppermute only.
A program may use at most 128 MiB of HBM per device.

v0:
```python
import jax
import jax.numpy as jnp
from jax import lax
from jax.sharding import PartitionSpec as P


def on_device(loadings, draws, delta, gamma, pair_rows, pair_cols, pair_count):
    owners = lax.axis_size("fac")
    my_index = lax.axis_index("fac")
    capacity = gamma.shape[0]
    block_rows = gamma.shape[2]
    local_blocks = loadings.shape[0] // block_rows
    columns = draws.shape[1]
    per_source = 2 * capacity // owners + 1
    wanted = jnp.stack(
        [pair_rows.reshape(owners, capacity), pair_cols.reshape(owners, capacity)], axis=2
    ).reshape(owners, 2 * capacity)
    source = wanted // local_blocks
    offset = wanted - source * local_blocks
    request_order = jnp.arange(2 * capacity, dtype=jnp.int32)
    same_source = source[:, :, None] == source[:, None, :]
    earlier = request_order[None, :] < request_order[:, None]
    position = jnp.sum((same_source & earlier[None, :, :]).astype(jnp.int32), axis=2)
    slot_index = jnp.arange(per_source, dtype=jnp.int32)
    chosen = (source == my_index)[:, :, None] & (position[:, :, None] == slot_index[None, None, :])
    outgoing = jnp.sum(chosen.astype(jnp.int32) * offset[:, :, None], axis=1).reshape(-1)
    my_source = lax.dynamic_index_in_dim(source, my_index, 0, keepdims=False)
    my_position = lax.dynamic_index_in_dim(position, my_index, 0, keepdims=False)
    arrival = my_source * per_source + my_position
    exposure = jnp.dot(loadings, draws, preferred_element_type=jnp.float32)
    linear = jnp.sum(delta[:, None] * exposure, axis=0)
    shocks = exposure.astype(jnp.bfloat16).reshape(local_blocks, block_rows, columns)
    outbound = shocks[outgoing].reshape(owners, per_source, block_rows, columns)
    inbound = lax.all_to_all(outbound, "fac", split_axis=0, concat_axis=0, tiled=True)
    needed = inbound.reshape(owners * per_source, block_rows, columns)[arrival]
    paired = needed.reshape(capacity, 2, block_rows, columns)
    left_block = paired[:, 0]
    right_block = paired[:, 1]
    my_wanted = lax.dynamic_index_in_dim(wanted, my_index, 0, keepdims=False).reshape(capacity, 2)
    my_count = lax.dynamic_index_in_dim(pair_count, my_index, 0, keepdims=False)
    is_live = (jnp.arange(capacity, dtype=jnp.int32) < my_count).astype(jnp.float32)
    weight = jnp.where(my_wanted[:, 0] == my_wanted[:, 1], 1.0, 2.0).astype(jnp.float32) * is_live
    product = jnp.einsum(
        "cab,cbs->cas",
        lax.all_gather(gamma, "scn", axis=1, tiled=True),
        right_block,
        preferred_element_type=jnp.float32,
    )
    inner = jnp.sum(product * left_block, axis=1)
    quad = jnp.sum(weight[:, None] * inner, axis=0)
    return lax.psum(linear + 0.5 * quad, "fac")


def solution(mesh):
    in_specs = (P("fac", None), P(None, "scn"), P("fac"), P("fac", "scn", None), P(), P(), P())
    out_specs = P("scn")
    return jax.shard_map(
        on_device, mesh=mesh, in_specs=in_specs, out_specs=out_specs, check_vma=False
    )
```

profile of v0, /device:TPU:4, one launch (start us, length us, event | category | flops | bytes accessed | tf_op | source)
XLA Modules:
  0.0 416.4 jit_solution(12494564719701076189)
XLA Ops:
  0.0 0.0 copy-start
  0.0 0.8 stack_reshape.6
  0.8 0.8 stack_reshape.7
  1.6 0.1 copy.24
  1.7 0.1 copy.25
  1.8 0.8 convert_reduce_fusion
  2.6 0.1 select_reduce_fusion
  2.7 0.1 copy.29
  2.8 0.1 reshape.164
  3.0 0.0 copy-done
  3.0 9.3 %fusion.8 = (bf16[6144,768]{1,0:T(8,128)(2,1)}, f32[768]{0:T(1024)S(1)}) fusion(f32[6144]{0:T(1024)} %param.9, bf16[6144,512]{1,0:T(8,128)(2,1)} %param.7, bf16[512,768]{1,0:T(8,128)(2,1)S(1)} %copy-done), kind=kOutput, calls=%fused_computation.36 | convolution fusion | flops 4845992960 | bytes 16542720 | tf_op jit(solution)/shard_map/dot_general | solution.py:30
  12.3 10.8 %gather_fusion = bf16[64,128,768]{2,1,0:T(8,128)(2,1)} fusion(bf16[48,128,768]{2,1,0:T(8,128)(2,1)} %bitcast.32, s32[1024]{0:T(1024)S(1)} %pad_clamp_fusion.1), kind=kCustom, calls=%fused_computation | custom fusion | bytes 25166080 | tf_op jit(solution)/shard_map/gather | solution.py:33
  23.1 0.0 copy-start.2
  23.1 0.0 copy-start.1
  23.1 11.7 %all-to-all-start = ((bf16[32,2,128,768]{3,2,1,0:T(8,128)(2,1)}), bf16[32,2,128,768]{3,2,1,0:T(8,128)(2,1)}, u32[]{:S(2)}, u32[]{:S(2)}) async-start(bf16[32,2,128,768]{3,2,1,0:T(8,128)(2,1)} %bitcast.31), calls=%async_computation | async-start | bytes 25165824 | tf_op jit(solution)/shard_map/all_to_all | solution.py:34
  34.8 0.2 dynamic-slice_reduce_fusion
  35.0 0.1 reshape.162
  35.1 0.0 copy-done.2
  35.1 0.6 dynamic_slice.14
  35.7 0.8 select_reduce_fusion.1
  36.5 0.0 copy-done.1
  36.5 11.9 %all_gather.3 = bf16[16,128,128]{2,1,0:T(8,128)(2,1)S(1)} all-gather(bf16[16,16,128]{2,1,0:T(8,128)(2,1)S(1)} %copy-done.1), channel_id=1, replica_groups=mesh['fac'=32,'scn'=8] {'scn'}, dimensions={1}, use_global_device_ids=true | all-gather | bytes 589824 | tf_op jit(solution)/shard_map/all_gather | solution.py:45
  48.4 267.4 %all-to-all-done = bf16[32,2,128,768]{3,2,1,0:T(8,128)(2,1)} async-done(((bf16[32,2,128,768]{3,2,1,0:T(8,128)(2,1)}), bf16[32,2,128,768]{3,2,1,0:T(8,128)(2,1)}, u32[]{:S(2)}, u32[]{:S(2)}) %all-to-all-start) | async-done | bytes 12582944 | tf_op jit(solution)/shard_map/all_to_all | solution.py:34
  315.8 8.1 %gather_fusion.1 = bf16[32,128,768]{2,1,0:T(8,128)(2,1)} fusion(bf16[64,128,768]{2,1,0:T(8,128)(2,1)} %bitcast.5, s32[1024]{0:T(1024)S(1)} %pad_clamp_fusion), kind=kCustom, calls=%fused_computation.1 | custom fusion | bytes 12583040 | tf_op jit(solution)/shard_map/gather | solution.py:35
  323.9 3.9 fusion
  327.8 0.1 multiply_reduce_fusion.1
  327.9 88.5 %psum.7 = f32[768]{0:T(1024)} all-reduce(f32[768]{0:T(1024)S(1)} %multiply_add_fusion), channel_id=1, replica_groups=mesh['fac'=32,'scn'=8] {'fac'}, use_global_device_ids=true, to_apply=%region_5.6 | all-reduce | flops 768 | bytes 6144 | tf_op jit(solution)/shard_map/psum | solution.py:51
  (9 shorter events, 0.1 us)
Async XLA Ops:
  0.0 3.0 copy-start
  23.1 12.0 %copy-start.2 = (s32[32]{0:T(128)S(1)}, s32[32]{0:T(128)}, u32[]{:S(2)}) copy-start(s32[32]{0:T(128)} %param.13) | copy-start | bytes 388
  23.1 13.4 %copy-start.1 = (bf16[16,16,128]{2,1,0:T(8,128)(2,1)S(1)}, bf16[16,16,128]{2,1,0:T(8,128)(2,1)}, u32[]{:S(2)}) copy-start(bf16[16,16,128]{2,1,0:T(8,128)(2,1)} %param.10) | copy-start | bytes 196612
  23.1 292.7 %all-to-all-start = ((bf16[32,2,128,768]{3,2,1,0:T(8,128)(2,1)}), bf16[32,2,128,768]{3,2,1,0:T(8,128)(2,1)}, u32[]{:S(2)}, u32[]{:S(2)}) async-start(bf16[32,2,128,768]{3,2,1,0:T(8,128)(2,1)} %bitcast.31), calls=%async_computation | async-start | bytes 25165824 | tf_op jit(solution)/shard_map/all_to_all | solution.py:34
where the time goes:
time: 417 us; the launch traced here: 416 us
  waiting for transfers between devices  267 us (64%)
  blocking collectives  100 us (24%)
  local copies, waits for them, and re-layouts  21.7 us (5%)
  matrix products  13.2 us (3%)
  starting transfers between devices  11.7 us (3%)
    all_to_all x1, waiting for transfers between devices, on_device(): lax.all_to_all(outbound, 'fac', split_axis=0, concat_axis=0, tiled=True)  267 us
    psum x1, blocking collectives, on_device(): return lax.psum(linear + 0.5 * quad, 'fac')  88.5 us
    all_gather x1, blocking collectives, on_device(): lax.all_gather(gamma, 'scn', axis=1, tiled=True)  11.9 us
    all_to_all x1, starting transfers between devices, on_device(): lax.all_to_all(outbound, 'fac', split_axis=0, concat_axis=0, tiled=True)  11.7 us
    gather x1, local copies, waits for them, and re-layouts, on_device(): outbound = shocks[outgoing].reshape(owners, per_source, block_rows, columns)  10.8 us
    dot_general x1, matrix products, on_device(): exposure = jnp.dot(loadings, draws, preferred_element_type=jnp.float32)  9.35 us
  transfers between devices with their start and end apart: 1, of which 1 were waited for; matrix products, arithmetic and copies ran while one was open for 0% of the time, Pallas kernels for 0%

commit v1 on v0

v1 whole, which is shorter than its diff:
```python
import functools

import jax
import jax.numpy as jnp
from jax import lax
from jax.experimental import pallas as pl
from jax.experimental.pallas import tpu as pltpu
from jax.sharding import PartitionSpec as P

F32 = jnp.float32
BF16 = jnp.bfloat16
VMEM = pl.BlockSpec(memory_space=pltpu.VMEM)
SMEM = pl.BlockSpec(memory_space=pltpu.SMEM)
ANY = pl.BlockSpec(memory_space=pl.ANY)
LANES = 128
OWNERS = 32
PARTS = 8
CAP = 16
BLOCKS_DEV = 48
SLICE = 16
GROUPS = 4
UPPER = [(g, h) for g in range(GROUPS) for h in range(g, GROUPS)]


def holder_of(block):
    return (block * 1366) >> 16


def pick_kernel(ids, rows_s, cols_s, rows_v, cols_v, loadings, out, arrival, keys_v, keys_s, seen, sems, key_sem):
    me = ids[0]
    part = ids[1]
    lane = lax.broadcasted_iota(jnp.int32, rows_v.shape, 1) & (CAP - 1)

    def keyed(blocks, first_slot):
        holder = holder_of(blocks)
        key = (lane + first_slot) * 64 + (blocks - holder * BLOCKS_DEV)
        mine = holder == me
        return jnp.where(mine, key, 1 << 20), jnp.where(mine, -key, 1)

    low_r, high_r = keyed(rows_v[...], 0)
    low_c, high_c = keyed(cols_v[...], CAP)
    keys = jnp.concatenate([jnp.minimum(low_r, low_c), jnp.minimum(high_r, high_c)], axis=0)
    for shift in (1, 2, 4, 8):
        keys = jnp.minimum(keys, pltpu.roll(keys, LANES - shift, 1))
    keys_v[...] = keys
    copy = pltpu.make_async_copy(keys_v, keys_s, key_sem)
    copy.start()
    for h in range(OWNERS):
        seen[h] = 0
    for t in range(2 * CAP):
        block = rows_s[me * CAP + t] if t < CAP else cols_s[me * CAP + t - CAP]
        holder = holder_of(block)
        arrival[t] = 2 * holder + seen[holder]
        seen[holder] = 1
    copy.wait()

    def fetch(slot, offset):
        start = pl.multiple_of(offset * LANES + part * SLICE, SLICE)
        return pltpu.make_async_copy(loadings.at[pl.ds(start, SLICE), :], out.at[slot], sems.at[slot])

    for o in range(OWNERS):
        row, col = o // 8, (o % 8) * CAP
        fetch(2 * o, jnp.minimum(keys_s[row, col] & 63, BLOCKS_DEV - 1)).start()
        fetch(2 * o + 1, jnp.minimum((-keys_s[4 + row, col]) & 63, BLOCKS_DEV - 1)).start()
    for slot in range(2 * OWNERS):
        fetch(slot, 0).wait()


def regroup_kernel(arrival, recv, gamma, out):
    for t in range(2 * CAP):
        block = recv[arrival[t]]
        dest = (t % CAP) // 2
        first = ((t % 2) + 2 * (t // CAP)) * GROUPS
        for g in range(GROUPS):
            out[dest, first + g] = block[:, g * LANES : (g + 1) * LANES]
    for p in range(CAP):
        out[p // 2, 4 * GROUPS + p % 2] = gamma[p]


def pair_kernel(ids, rows_s, cols_s, count_s, recv, out):
    me = ids[0]
    part = ids[1]

    def block(b):
        tiles = [recv[:, b * GROUPS + g].reshape(LANES, LANES) for g in range(GROUPS)]
        return jnp.concatenate(tiles, axis=1)

    left = []
    high = []
    low = []
    for q in range(2):
        slot = 2 * part + q
        p = me * CAP + slot
        weight = jnp.where(rows_s[p] == cols_s[p], 0.5, 1.0)
        weight = jnp.where(slot < count_s[me], weight, 0.0)
        stored = recv[:, 4 * GROUPS + q].reshape(LANES, LANES)
        half = jnp.dot(stored, block(2 + q), preferred_element_type=F32) * weight
        top = half.astype(BF16)
        left.append(block(q))
        high.append(top)
        low.append((half - top.astype(F32)).astype(BF16))
    a = jnp.concatenate(left, axis=0)
    y = jnp.concatenate(high, axis=0)
    z = jnp.concatenate(low, axis=0)
    one = jnp.concatenate([a, a, y, z], axis=0)
    two = jnp.concatenate([y, z, a, a], axis=0)
    for k, (g, h) in enumerate(UPPER):
        summed = lax.dot_general(
            one[:, g * LANES : (g + 1) * LANES],
            two[:, h * LANES : (h + 1) * LANES],
            (((0,), (0,)), ((), ())),
            preferred_element_type=F32,
        )
        if g == h:
            summed = summed * 0.5
        out[:, k] = summed.astype(BF16).reshape(PARTS, SLICE, LANES)


def form_kernel(matrix, draws, slope, out):
    columns = draws.shape[1]
    total = jnp.zeros((1, columns), F32)
    for g in range(GROUPS):
        tiles = [
            matrix[:, k].reshape(LANES, LANES) for k, (i, _) in enumerate(UPPER) if i == g
        ]
        wide = jnp.concatenate(tiles, axis=1) if len(tiles) > 1 else tiles[0]
        image = jnp.dot(wide, draws[g * LANES :, :], preferred_element_type=F32)
        mine = draws[g * LANES : (g + 1) * LANES, :].astype(F32)
        total += jnp.sum(image * mine, axis=0, keepdims=True)
    v = slope[...]
    one = v.astype(BF16)
    v = v - one.astype(F32)
    two = v.astype(BF16)
    v = v - two.astype(F32)
    parts = jnp.concatenate(
        [one, two, v.astype(BF16), jnp.zeros((5, v.shape[1]), BF16)], axis=0
    )
    linear = jnp.dot(parts, draws[...], preferred_element_type=F32)
    total += jnp.sum(linear, axis=0, keepdims=True)
    rows = [total[:, i * LANES : (i + 1) * LANES] for i in range(columns // LANES)]
    rows += [jnp.zeros((8 - len(rows), LANES), F32)]
    tile = jnp.concatenate(rows, axis=0)
    for o in range(OWNERS):
        out[o] = tile


def on_device(loadings, draws, delta, gamma, pair_rows, pair_cols, pair_count):
    columns = draws.shape[1]
    depth = loadings.shape[1]
    ids = jnp.stack([lax.axis_index("fac"), lax.axis_index("scn")]).astype(jnp.int32)
    outgoing, arrival = pl.pallas_call(
        pick_kernel,
        out_shape=(
            jax.ShapeDtypeStruct((2 * OWNERS, SLICE, depth), BF16),
            jax.ShapeDtypeStruct((2 * CAP,), jnp.int32),
        ),
        in_specs=[SMEM, SMEM, SMEM, VMEM, VMEM, ANY],
        out_specs=(VMEM, SMEM),
        scratch_shapes=[
            pltpu.VMEM((8, LANES), jnp.int32),
            pltpu.SMEM((8, LANES), jnp.int32),
            pltpu.SMEM((OWNERS,), jnp.int32),
            pltpu.SemaphoreType.DMA((2 * OWNERS,)),
            pltpu.SemaphoreType.DMA,
        ],
        name="pick",
    )(ids, pair_rows, pair_cols, pair_rows.reshape(4, LANES), pair_cols.reshape(4, LANES), loadings)
    arrived = lax.all_to_all(outgoing, "fac", split_axis=0, concat_axis=0, tiled=True)
    slope = jnp.sum(delta[:, None] * loadings.astype(F32), axis=0)
    grouped = pl.pallas_call(
        regroup_kernel,
        out_shape=jax.ShapeDtypeStruct((PARTS, 18, SLICE, LANES), BF16),
        in_specs=[SMEM, VMEM, VMEM],
        out_specs=VMEM,
        name="regroup",
    )(arrival, arrived, gamma)
    pairs = lax.all_to_all(grouped, "scn", split_axis=0, concat_axis=0, tiled=True)
    partial = pl.pallas_call(
        pair_kernel,
        out_shape=jax.ShapeDtypeStruct((PARTS, len(UPPER), SLICE, LANES), BF16),
        in_specs=[SMEM, SMEM, SMEM, SMEM, VMEM],
        out_specs=VMEM,
        name="pair",
    )(ids, pair_rows, pair_cols, pair_count, pairs)
    partial = lax.all_to_all(partial, "scn", split_axis=0, concat_axis=0, tiled=True)
    rows = jnp.sum(partial.astype(F32), axis=0).astype(BF16)
    matrix = lax.all_gather(rows, "scn", axis=0, tiled=False)
    mine = pl.pallas_call(
        form_kernel,
        out_shape=jax.ShapeDtypeStruct((OWNERS, 8, LANES), F32),
        in_specs=[VMEM, VMEM, VMEM],
        out_specs=VMEM,
        name="form",
    )(matrix, draws, slope.reshape(1, depth))
    every = lax.all_to_all(mine, "fac", split_axis=0, concat_axis=0, tiled=True)
    return jnp.sum(every, axis=0).reshape(-1)[:columns]


def solution(mesh):
    in_specs = (P("fac", None), P(None, "scn"), P("fac"), P("fac", "scn", None), P(), P(), P())
    out_specs = P("scn")
    return jax.shard_map(
        on_device, mesh=mesh, in_specs=in_specs, out_specs=out_specs, check_vma=False
    )
```

time: 417 us -> 111 us (0.27)
  waiting for transfers between devices: 267 us -> 0.29 us
  local copies, waits for them, and re-layouts: 21.7 us -> 0.6 us
  blocking collectives: 100 us -> 84.5 us
  matrix products: 13.2 us -> 0 us
  Pallas kernels: 0 us -> 12.5 us
  starting transfers between devices: 11.7 us -> 5.89 us
    all_to_all x1, waiting for transfers between devices: 267 us -> 0.29 us  [on_device(): lax.all_to_all(partial, 'scn', split_axis=0, concat_axis=0, tiled=True)]
    psum x1 -> x0, blocking collectives: 88.5 us -> none  [on_device(): return lax.psum(linear + 0.5 * quad, 'fac')]
    all_to_all x0 -> x3, blocking collectives: none -> 69.5 us  [the longest x1 40.1 us: on_device(): lax.all_to_all(outgoing, 'fac', split_axis=0, concat_axis=0, tiled=True)]
    gather x2 -> x0, local copies, waits for them, and re-layouts: 18.9 us -> none  [the longest x1 10.8 us: on_device(): outbound = shocks[outgoing].reshape(owners, per_source, block_rows, columns)]
    dot_general x2 -> x0, matrix products: 13.2 us -> none  [the longest x1 9.35 us: on_device(): exposure = jnp.dot(loadings, draws, preferred_element_type=jnp.float32)]
    pallas_call x0 -> x4, Pallas kernels: none -> 12.5 us  [the longest x1 5.03 us: on_device(): pl.pallas_call(pick_kernel, out_shape=(jax.ShapeDtypeStruct((2 * OWNERS,...]
    all_to_all x1, starting transfers between devices: 11.7 us -> 5.89 us  [on_device(): lax.all_to_all(partial, 'scn', split_axis=0, concat_axis=0, tiled=True)]
  transfers between devices with their start and end apart: 1 -> 1, of which waited for: 1 -> 1; matrix products, arithmetic and copies ran while one was open for 0% -> 4% of each run, Pallas kernels for 0% -> 0%
where the time goes in v1:
time: 111 us; the launch traced here: 109 us
  blocking collectives  84.5 us (76%)
  Pallas kernels  12.5 us (11%)
  starting transfers between devices  5.89 us (5%)
  other arithmetic  5.44 us (5%)
    all_to_all x1, blocking collectives, on_device(): lax.all_to_all(outgoing, 'fac', split_axis=0, concat_axis=0, tiled=True)  40.1 us
    all_to_all x1, blocking collectives, on_device(): every = lax.all_to_all(mine, 'fac', split_axis=0, concat_axis=0, tiled=True)  15.9 us
    all_gather x1, blocking collectives, on_device(): matrix = lax.all_gather(rows, 'scn', axis=0, tiled=False)  15.1 us
    all_to_all x1, blocking collectives, on_device(): lax.all_to_all(grouped, 'scn', split_axis=0, concat_axis=0, tiled=True)  13.4 us
    all_to_all x1, starting transfers between devices, on_device(): lax.all_to_all(partial, 'scn', split_axis=0, concat_axis=0, tiled=True)  5.89 us
    pallas_call x1, Pallas kernels, on_device(): pl.pallas_call(pick_kernel, out_shape=(jax.ShapeDtypeStruct((2 * OWNERS,...  5.03 us
    reduce_sum x1, other arithmetic, on_device(): slope = jnp.sum(delta[:, None] * loadings.astype(F32), axis=0)  4.77 us
    pallas_call x1, Pallas kernels, on_device(): pl.pallas_call(pair_kernel, out_shape=jax.ShapeDtypeStruct((PARTS, len(UP...  2.87 us
  transfers between devices with their start and end apart: 1, of which 1 were waited for; matrix products, arithmetic and copies ran while one was open for 4% of the time, Pallas kernels for 0%

profile of v1, /device:TPU:4, one launch (start us, length us, event | category | flops | bytes accessed | tf_op | source)
XLA Modules:
  0.0 109.3 jit_solution(13037328301301251175)
XLA Ops:
  0.0 0.6 pad_add_fusion.ids
  0.6 0.0 copy-start
  0.6 5.0 %pick.1 = (bf16[64,16,512]{2,1,0:T(8,128)(2,1)}, s32[32]{0:T(128)}) custom-call(s32[2]{0:T(128)} %pad_add_fusion.ids, s32[512]{0:T(512)} %rows_s.3, s32[512]{0:T(512)} %cols_s.3, s32[4,128]{1,0:T(4,128)} %bitcast.9, s32[4,128]{1,0:T(4,128)} %bitcast.10, bf16[6144,512]{1,0:T(8,128)(2,1)} %loadings.1), custom_call_target="tpu_custom_call" | custom-call | tf_op jit(solution)/shard_map/pick/pallas_call | solution.py:151
  5.6 40.1 %all_to_all.20.recv = bf16[64,16,512]{2,1,0:T(8,128)(2,1)} all-to-all(bf16[64,16,512]{2,1,0:T(8,128)(2,1)} %get-tuple-element.8), channel_id=1, replica_groups=mesh['fac'=32,'scn'=8] {'fac'}, dimensions={0} | all-to-all | bytes 2097152 | tf_op jit(solution)/shard_map/all_to_all | solution.py:168
  45.8 2.1 %regroup.1 = bf16[8,18,16,128]{3,2,1,0:T(8,128)(2,1)} custom-call(s32[32]{0:T(128)} %get-tuple-element.7.arrival, bf16[64,16,512]{2,1,0:T(8,128)(2,1)} %all_to_all.20.recv, bf16[16,16,128]{2,1,0:T(8,128)(2,1)} %gamma.1), custom_call_target="tpu_custom_call" | custom-call | tf_op jit(solution)/shard_map/regroup/pallas_call | solution.py:170
  47.9 13.4 %all_to_all.21.recv = bf16[8,18,16,128]{3,2,1,0:T(8,128)(2,1)} all-to-all(bf16[8,18,16,128]{3,2,1,0:T(8,128)(2,1)} %regroup.1), channel_id=1, replica_groups=mesh['fac'=32,'scn'=8] {'scn'}, dimensions={0} | all-to-all | bytes 1179648 | tf_op jit(solution)/shard_map/all_to_all | solution.py:177
  61.3 2.9 %pair.1 = bf16[8,10,16,128]{3,2,1,0:T(8,128)(2,1)} custom-call(s32[2]{0:T(128)} %pad_add_fusion.ids, s32[512]{0:T(512)} %rows_s.3, s32[512]{0:T(512)} %cols_s.3, s32[32]{0:T(128)} %count_s.1, bf16[8,18,16,128]{3,2,1,0:T(8,128)(2,1)} %all_to_all.21.recv), custom_call_target="tpu_custom_call" | custom-call | tf_op jit(solution)/shard_map/pair/pallas_call | solution.py:178
  64.2 5.9 %all-to-all-start.2 = ((bf16[8,10,16,128]{3,2,1,0:T(8,128)(2,1)}), bf16[8,10,16,128]{3,2,1,0:T(8,128)(2,1)S(1)}, u32[]{:S(2)}, u32[]{:S(2)}) async-start(bf16[8,10,16,128]{3,2,1,0:T(8,128)(2,1)} %pair.1), calls=%async_computation.2 | async-start | bytes 655360 | tf_op jit(solution)/shard_map/all_to_all | solution.py:185
  70.1 0.0 copy-done
  70.1 4.8 %multiply_reduce_fusion = f32[512]{0:T(512)} fusion(bf16[6144,512]{1,0:T(8,128)(2,1)} %loadings.1, f32[6144]{0:T(1024)S(1)} %copy-done), kind=kLoop, calls=%fused_computation | loop fusion | flops 9436672 | bytes 6318080 | tf_op jit(solution)/shard_map/reduce_sum | solution.py:169
  74.9 0.3 all-to-all-done.2
  75.2 15.1 %all-gather = bf16[80,16,128]{2,1,0:T(8,128)(2,1)} all-gather(bf16[10,16,128]{2,1,0:T(8,128)(2,1)S(1)} %reduce_sum.30), channel_id=2, replica_groups=mesh['fac'=32,'scn'=8] {'scn'}, dimensions={0}, use_global_device_ids=true | all-gather | bytes 368640 | tf_op jit(solution)/shard_map/all_gather | solution.py:187
  90.3 2.4 %form.1 = f32[32,8,128]{2,1,0:T(8,128)} custom-call(bf16[8,10,16,128]{3,2,1,0:T(8,128)(2,1)} %bitcast.8, bf16[512,768]{1,0:T(8,128)(2,1)} %draws.1, f32[1,512]{1,0:T(1,128)} %bitcast.11), custom_call_target="tpu_custom_call" | custom-call | tf_op jit(solution)/shard_map/form/pallas_call | solution.py:188
  92.7 15.9 %all_to_all.22 = f32[32,8,128]{2,1,0:T(8,128)S(1)} all-to-all(f32[32,8,128]{2,1,0:T(8,128)} %form.1), channel_id=1, replica_groups=mesh['fac'=32,'scn'=8] {'fac'}, dimensions={0} | all-to-all | bytes 262144 | tf_op jit(solution)/shard_map/all_to_all | solution.py:195
  108.7 0.6 slice_bitcast_fusion
  (2 shorter events, 0.1 us)
Async XLA Ops:
  0.6 69.5 %copy-start = (f32[6144]{0:T(1024)S(1)}, f32[6144]{0:T(1024)}, u32[]{:S(2)}) copy-start(f32[6144]{0:T(1024)} %param.9) | copy-start | bytes 73732
  64.2 10.9 %all-to-all-start.2 = ((bf16[8,10,16,128]{3,2,1,0:T(8,128)(2,1)}), bf16[8,10,16,128]{3,2,1,0:T(8,128)(2,1)S(1)}, u32[]{:S(2)}, u32[]{:S(2)}) async-start(bf16[8,10,16,128]{3,2,1,0:T(8,128)(2,1)} %pair.1), calls=%async_computation.2 | async-start | bytes 655360 | tf_op jit(solution)/shard_map/all_to_all | solution.py:185

commit v2 on v1

--- a/solution.py
+++ b/solution.py
@@ -1,11 +1,10 @@
-import functools
-
 import jax
 import jax.numpy as jnp
 from jax import lax
 from jax.experimental import pallas as pl
 from jax.experimental.pallas import tpu as pltpu
 from jax.sharding import PartitionSpec as P
+
 
 F32 = jnp.float32
 BF16 = jnp.bfloat16
@@ -113,20 +112,31 @@
         )
         if g == h:
             summed = summed * 0.5
-        out[:, k] = summed.astype(BF16).reshape(PARTS, SLICE, LANES)
-
-
-def form_kernel(matrix, draws, slope, out):
-    columns = draws.shape[1]
-    total = jnp.zeros((1, columns), F32)
-    for g in range(GROUPS):
-        tiles = [
-            matrix[:, k].reshape(LANES, LANES) for k, (i, _) in enumerate(UPPER) if i == g
-        ]
-        wide = jnp.concatenate(tiles, axis=1) if len(tiles) > 1 else tiles[0]
-        image = jnp.dot(wide, draws[g * LANES :, :], preferred_element_type=F32)
-        mine = draws[g * LANES : (g + 1) * LANES, :].astype(F32)
-        total += jnp.sum(image * mine, axis=0, keepdims=True)
+        out[k] = summed
+
+
+def form_kernel(ids, own, other, here, left, right, far, slope, out):
+    columns = here.shape[1]
+    chip = ids[1] // 2
+    blocks = [(own[k] + other[k]).astype(BF16) for k in range(len(UPPER))]
+    wide = [
+        jnp.concatenate([b for b, (i, _) in zip(blocks, UPPER) if i == g], axis=1)
+        for g in range(GROUPS)
+    ]
+
+    def store(position, total):
+        rows = [total[:, i * LANES : (i + 1) * LANES] for i in range(columns // LANES)]
+        rows += [jnp.zeros((8 - len(rows), LANES), F32)]
+        out[position] = jnp.concatenate(rows, axis=0)
+
+    def quadratic(rows_of):
+        total = jnp.zeros((1, columns), F32)
+        for g in range(GROUPS):
+            image = jnp.dot(wide[g], rows_of(g * LANES, None), preferred_element_type=F32)
+            mine = rows_of(g * LANES, (g + 1) * LANES).astype(F32)
+            total += jnp.sum(image * mine, axis=0, keepdims=True)
+        return total
+
     v = slope[...]
     one = v.astype(BF16)
     v = v - one.astype(F32)
@@ -135,19 +145,25 @@
     parts = jnp.concatenate(
         [one, two, v.astype(BF16), jnp.zeros((5, v.shape[1]), BF16)], axis=0
     )
-    linear = jnp.dot(parts, draws[...], preferred_element_type=F32)
-    total += jnp.sum(linear, axis=0, keepdims=True)
-    rows = [total[:, i * LANES : (i + 1) * LANES] for i in range(columns // LANES)]
-    rows += [jnp.zeros((8 - len(rows), LANES), F32)]
-    tile = jnp.concatenate(rows, axis=0)
-    for o in range(OWNERS):
-        out[o] = tile
-
-
-def on_device(loadings, draws, delta, gamma, pair_rows, pair_cols, pair_count):
+    linear = jnp.dot(parts, here[...], preferred_element_type=F32)
+    linear = jnp.sum(linear, axis=0, keepdims=True)
+    store(chip, quadratic(lambda a, b: here[a:b, :]) + linear)
+    store((chip + 3) & 3, quadratic(lambda a, b: left[a:b, :]))
+    store((chip + 1) & 3, quadratic(lambda a, b: right[a:b, :]))
+    store((chip + 2) & 3, quadratic(lambda a, b: far[a:b, :]))
+
+
+def ring(step):
+    return [(i, (i + step) % PARTS) for i in range(PARTS)]
+
+
+def body(loadings, draws, delta, gamma, pair_rows, pair_cols, pair_count):
     columns = draws.shape[1]
     depth = loadings.shape[1]
     ids = jnp.stack([lax.axis_index("fac"), lax.axis_index("scn")]).astype(jnp.int32)
+    left = lax.ppermute(draws, "scn", ring(2))
+    right = lax.ppermute(draws, "scn", ring(-2))
+    far = lax.ppermute(draws, "scn", ring(4))
     outgoing, arrival = pl.pallas_call(
         pick_kernel,
         out_shape=(
@@ -175,23 +191,26 @@
         name="regroup",
     )(arrival, arrived, gamma)
     pairs = lax.all_to_all(grouped, "scn", split_axis=0, concat_axis=0, tiled=True)
-    partial = pl.pallas_call(
+    own = pl.pallas_call(
         pair_kernel,
-        out_shape=jax.ShapeDtypeStruct((PARTS, len(UPPER), SLICE, LANES), BF16),
+        out_shape=jax.ShapeDtypeStruct((len(UPPER), LANES, LANES), F32),
         in_specs=[SMEM, SMEM, SMEM, SMEM, VMEM],
         out_specs=VMEM,
         name="pair",
     )(ids, pair_rows, pair_cols, pair_count, pairs)
-    partial = lax.all_to_all(partial, "scn", split_axis=0, concat_axis=0, tiled=True)
-    rows = jnp.sum(partial.astype(F32), axis=0).astype(BF16)
-    matrix = lax.all_gather(rows, "scn", axis=0, tiled=False)
-    mine = pl.pallas_call(
+    other = lax.ppermute(own, "scn", [(i, i ^ 1) for i in range(PARTS)])
+    spread = pl.pallas_call(
         form_kernel,
-        out_shape=jax.ShapeDtypeStruct((OWNERS, 8, LANES), F32),
-        in_specs=[VMEM, VMEM, VMEM],
+        out_shape=jax.ShapeDtypeStruct((PARTS // 2, 8, LANES), F32),
+        in_specs=[SMEM] + [VMEM] * 7,
         out_specs=VMEM,
         name="form",
-    )(matrix, draws, slope.reshape(1, depth))
+    )(ids, own, other, draws, left, right, far, slope.reshape(1, depth))
+    chips = [[c + 2 * x for x in range(PARTS // 2)] for c in range(2)]
+    along = lax.all_to_all(
+        spread, "scn", split_axis=0, concat_axis=0, tiled=True, axis_index_groups=chips
+    )
+    mine = jnp.broadcast_to(jnp.sum(along, axis=0)[None], (OWNERS, 8, LANES))
     every = lax.all_to_all(mine, "fac", split_axis=0, concat_axis=0, tiled=True)
     return jnp.sum(every, axis=0).reshape(-1)[:columns]
 
@@ -199,6 +218,4 @@
 def solution(mesh):
     in_specs = (P("fac", None), P(None, "scn"), P("fac"), P("fac", "scn", None), P(), P(), P())
     out_specs = P("scn")
-    return jax.shard_map(
-        on_device, mesh=mesh, in_specs=in_specs, out_specs=out_specs, check_vma=False
-    )
+    return jax.shard_map(body, mesh=mesh, in_specs=in_specs, out_specs=out_specs, check_vma=False)

time: 111 us -> 126 us (1.14)
  waiting for transfers between devices: 0.29 us -> 29.8 us
  blocking collectives: 84.5 us -> 64.7 us
  starting transfers between devices: 5.89 us -> 8.13 us
  Pallas kernels: 12.5 us -> 14.2 us
    ppermute x0 -> x4, waiting for transfers between devices: none -> 25 us  [the longest x1 15.6 us: body(): far = lax.ppermute(draws, 'scn', ring(4))]
    all_gather x1 -> x0, blocking collectives: 15.1 us -> none  [on_device(): matrix = lax.all_gather(rows, 'scn', axis=0, tiled=False)]
    all_to_all x3, blocking collectives: 69.5 us -> 64.7 us  [the longest x1 40.1 us: body(): lax.all_to_all(outgoing, 'fac', split_axis=0, concat_axis=0, tiled=True)]
    all_to_all x1, waiting for transfers between devices: 0.29 us -> 4.83 us  [body(): lax.all_to_all(grouped, 'scn', split_axis=0, concat_axis=0, tiled=True)]
    ppermute x0 -> x4, starting transfers between devices: none -> 3.32 us  [the longest x1 1.29 us: body(): far = lax.ppermute(draws, 'scn', ring(4))]
    pallas_call x4, Pallas kernels: 12.5 us -> 14.2 us  [the longest x1 4.74 us: body(): pl.pallas_call(pick_kernel, out_shape=(jax.ShapeDtypeStruct((2 * OWNERS,...]
  transfers between devices with their start and end apart: 1 -> 5, of which waited for: 1 -> 4; matrix products, arithmetic and copies ran while one was open for 4% -> 4% of each run, Pallas kernels for 0% -> 2%
where the time goes in v2:
time: 126 us; the launch traced here: 124 us
  blocking collectives  64.7 us (51%)
  waiting for transfers between devices  29.8 us (24%)
  Pallas kernels  14.2 us (11%)
  starting transfers between devices  8.13 us (6%)
  other arithmetic  5.47 us (4%)
  local copies, waits for them, and re-layouts  1.44 us (1%)
    all_to_all x1, blocking collectives, body(): lax.all_to_all(outgoing, 'fac', split_axis=0, concat_axis=0, tiled=True)  40.1 us
    ppermute x1, waiting for transfers between devices, body(): far = lax.ppermute(draws, 'scn', ring(4))  15.6 us
    all_to_all x1, blocking collectives, body(): every = lax.all_to_all(mine, 'fac', split_axis=0, concat_axis=0, tiled=True)  15.3 us
    all_to_all x1, blocking collectives, body(): lax.all_to_all(spread, 'scn', split_axis=0, concat_axis=0, tiled=True, ax...  9.31 us
    ppermute x1, waiting for transfers between devices, body(): left = lax.ppermute(draws, 'scn', ring(2))  8.15 us
    all_to_all x1, waiting for transfers between devices, body(): lax.all_to_all(grouped, 'scn', split_axis=0, concat_axis=0, tiled=True)  4.83 us
    all_to_all x1, starting transfers between devices, body(): lax.all_to_all(grouped, 'scn', split_axis=0, concat_axis=0, tiled=True)  4.8 us
    reduce_sum x1, other arithmetic, body(): slope = jnp.sum(delta[:, None] * loadings.astype(F32), axis=0)  4.77 us
  transfers between devices with their start and end apart: 5, of which 4 were waited for; matrix products, arithmetic and copies ran while one was open for 4% of the time, Pallas kernels for 2%

profile of v2, /device:TPU:4, one launch (start us, length us, event | category | flops | bytes accessed | tf_op | source)
XLA Modules:
  0.0 123.8 jit_solution(17636267929402357483)
XLA Ops:
  0.0 0.0 copy-start.1
  0.0 0.0 copy-start.4
  0.0 0.7 pad_add_fusion.ids
  0.7 4.7 %pick.1 = (bf16[64,16,512]{2,1,0:T(8,128)(2,1)}, s32[32]{0:T(128)}) custom-call(s32[2]{0:T(128)} %pad_add_fusion.ids, s32[512]{0:T(512)} %rows_s.3, s32[512]{0:T(512)} %cols_s.3, s32[4,128]{1,0:T(4,128)} %bitcast.7, s32[4,128]{1,0:T(4,128)} %bitcast.8, bf16[6144,512]{1,0:T(8,128)(2,1)} %loadings.1), custom_call_target="tpu_custom_call" | custom-call | tf_op jit(solution)/shard_map/pick/pallas_call | solution.py:167
  5.4 40.1 %all_to_all.20.recv = bf16[64,16,512]{2,1,0:T(8,128)(2,1)} all-to-all(bf16[64,16,512]{2,1,0:T(8,128)(2,1)} %get-tuple-element.8), channel_id=1, replica_groups=mesh['fac'=32,'scn'=8] {'fac'}, dimensions={0} | all-to-all | bytes 2097152 | tf_op jit(solution)/shard_map/all_to_all | solution.py:184
  45.5 2.1 %regroup.1 = bf16[8,18,16,128]{3,2,1,0:T(8,128)(2,1)} custom-call(s32[32]{0:T(128)} %get-tuple-element.7.arrival, bf16[64,16,512]{2,1,0:T(8,128)(2,1)} %all_to_all.20.recv, bf16[16,16,128]{2,1,0:T(8,128)(2,1)} %gamma.1), custom_call_target="tpu_custom_call" | custom-call | tf_op jit(solution)/shard_map/regroup/pallas_call | solution.py:186
  47.7 4.8 %all-to-all-start.1 = ((bf16[8,18,16,128]{3,2,1,0:T(8,128)(2,1)}), bf16[8,18,16,128]{3,2,1,0:T(8,128)(2,1)S(1)}, u32[]{:S(2)}, u32[]{:S(2)}) async-start(bf16[8,18,16,128]{3,2,1,0:T(8,128)(2,1)} %regroup.1), calls=%async_computation.1 | async-start | bytes 1179648 | tf_op jit(solution)/shard_map/all_to_all | solution.py:193
  52.5 0.0 copy-done.1
  52.5 1.2 collective-permute-start.1
  53.7 0.9 collective-permute-start.2
  54.5 1.3 %collective-permute-start.3 = (bf16[512,768]{1,0:T(8,128)(2,1)S(1)}, bf16[512,768]{1,0:T(8,128)(2,1)}, u32[]{:S(2)}, u32[]{:S(2)}) collective-permute-start(bf16[512,768]{1,0:T(8,128)(2,1)S(1)} %copy-done.1), channel_id=1, source_target_pairs={{0,4},{1,5},{2,6},{3,7},{4,0},{5,1},{6,2},{7,3},{8,12},{9,13},{10,... | collective-permute-start | bytes 2359304 | tf_op jit(solution)/shard_map/ppermute | solution.py:166
  55.8 4.8 %all-to-all-done.1.recv = bf16[8,18,16,128]{3,2,1,0:T(8,128)(2,1)S(1)} async-done(((bf16[8,18,16,128]{3,2,1,0:T(8,128)(2,1)}), bf16[8,18,16,128]{3,2,1,0:T(8,128)(2,1)S(1)}, u32[]{:S(2)}, u32[]{:S(2)}) %all-to-all-start.1) | async-done | bytes 589856 | tf_op jit(solution)/shard_map/all_to_all | solution.py:193
  60.7 0.0 copy-start
  60.7 0.8 copy-done
  61.5 3.0 %pair.1.own = f32[10,128,128]{2,1,0:T(8,128)} custom-call(s32[2]{0:T(128)} %pad_add_fusion.ids, s32[512]{0:T(512)} %rows_s.3, s32[512]{0:T(512)} %cols_s.3, s32[32]{0:T(128)} %count_s.1, bf16[8,18,16,128]{3,2,1,0:T(8,128)(2,1)} %copy-done), custom_call_target="tpu_custom_call" | custom-call | tf_op jit(solution)/shard_map/pair/pallas_call | solution.py:194
  64.5 0.0 collective-permute-start
  64.5 0.0 copy-done.4
  64.5 4.8 %multiply_reduce_fusion = f32[512]{0:T(512)} fusion(bf16[6144,512]{1,0:T(8,128)(2,1)} %loadings.1, f32[6144]{0:T(1024)S(1)} %copy-done.4), kind=kLoop, calls=%fused_computation | loop fusion | flops 9436672 | bytes 6318080 | tf_op jit(solution)/shard_map/reduce_sum | solution.py:185
  69.2 8.1 %collective-permute-done.1.left = bf16[512,768]{1,0:T(8,128)(2,1)S(1)} collective-permute-done((bf16[512,768]{1,0:T(8,128)(2,1)S(1)}, bf16[512,768]{1,0:T(8,128)(2,1)S(1)}, u32[]{:S(2)}, u32[]{:S(2)}) %collective-permute-start.1) | collective-permute-done | bytes 786464 | tf_op jit(solution)/shard_map/ppermute | solution.py:164
  77.4 0.0 copy-start.2
  77.4 1.3 %collective-permute-done.2.right = bf16[512,768]{1,0:T(8,128)(2,1)S(1)} collective-permute-done((bf16[512,768]{1,0:T(8,128)(2,1)S(1)}, bf16[512,768]{1,0:T(8,128)(2,1)S(1)}, u32[]{:S(2)}, u32[]{:S(2)}) %collective-permute-start.2) | collective-permute-done | bytes 786464 | tf_op jit(solution)/shard_map/ppermute | solution.py:165
  78.6 0.0 copy-start.3
  78.6 15.6 %collective-permute-done.3.far = bf16[512,768]{1,0:T(8,128)(2,1)} collective-permute-done((bf16[512,768]{1,0:T(8,128)(2,1)S(1)}, bf16[512,768]{1,0:T(8,128)(2,1)}, u32[]{:S(2)}, u32[]{:S(2)}) %collective-permute-start.3) | collective-permute-done | bytes 786464 | tf_op jit(solution)/shard_map/ppermute | solution.py:166
  94.2 0.0 collective-permute-done.other
  94.2 0.0 copy-done.2
  94.2 0.0 copy-done.3
  94.3 4.4 %form.1 = f32[4,8,128]{2,1,0:T(8,128)} custom-call(s32[2]{0:T(128)} %pad_add_fusion.ids, f32[10,128,128]{2,1,0:T(8,128)} %pair.1.own, f32[10,128,128]{2,1,0:T(8,128)} %collective-permute-done.other, bf16[512,768]{1,0:T(8,128)(2,1)} %here.1, bf16[512,768]{1,0:T(8,128)(2,1)} %copy-done.2, bf16[512,768]{1,0:T(8,128)(2,1)} %copy-done.3, ...), custom_call_target="tpu_custom_call" | custom-call | tf_op jit(solution)/shard_map/form/pallas_call | solution.py:202
  98.6 9.3 %all_to_all.21 = f32[4,8,128]{2,1,0:T(8,128)S(1)} all-to-all(f32[4,8,128]{2,1,0:T(8,128)} %form.1), channel_id=1, replica_groups={{0,2,4,6},{1,3,5,7},{8,10,12,14},{9,11,13,15},{16,18,20,22},{17,19,21,2..., dimensions={0} | all-to-all | bytes 32768 | tf_op jit(solution)/shard_map/all_to_all | solution.py:210
  107.9 15.3 %all_to_all.22 = f32[32,8,128]{2,1,0:T(8,128)S(1)} all-to-all(f32[32,8,128]{2,1,0:T(8,128)S(1)} %broadcast_in_dim.2), channel_id=1, replica_groups=mesh['fac'=32,'scn'=8] {'fac'}, dimensions={0} | all-to-all | bytes 262144 | tf_op jit(solution)/shard_map/all_to_all | solution.py:214
  123.2 0.6 slice_bitcast_fusion
  (3 shorter events, 0.1 us)
Async XLA Ops:
  0.0 52.5 %copy-start.1 = (bf16[512,768]{1,0:T(8,128)(2,1)S(1)}, bf16[512,768]{1,0:T(8,128)(2,1)}, u32[]{:S(2)}) copy-start(bf16[512,768]{1,0:T(8,128)(2,1)} %here.1) | copy-start | bytes 2359300
  0.0 64.5 %copy-start.4 = (f32[6144]{0:T(1024)S(1)}, f32[6144]{0:T(1024)}, u32[]{:S(2)}) copy-start(f32[6144]{0:T(1024)} %param.9) | copy-start | bytes 73732
  47.7 13.0 %all-to-all-start.1 = ((bf16[8,18,16,128]{3,2,1,0:T(8,128)(2,1)}), bf16[8,18,16,128]{3,2,1,0:T(8,128)(2,1)S(1)}, u32[]{:S(2)}, u32[]{:S(2)}) async-start(bf16[8,18,16,128]{3,2,1,0:T(8,128)(2,1)} %regroup.1), calls=%async_computation.1 | async-start | bytes 1179648 | tf_op jit(solution)/shard_map/all_to_all | solution.py:193
  52.5 24.9 %collective-permute-start.1 = (bf16[512,768]{1,0:T(8,128)(2,1)S(1)}, bf16[512,768]{1,0:T(8,128)(2,1)S(1)}, u32[]{:S(2)}, u32[]{:S(2)}) collective-permute-start(bf16[512,768]{1,0:T(8,128)(2,1)S(1)} %copy-done.1), channel_id=1, source_target_pairs={{0,2},{1,3},{2,4},{3,5},{4,6},{5,7},{6,0},{7,1},{8,10},{9,11},{10,... | collective-permute-start | bytes 2359304 | tf_op jit(solution)/shard_map/ppermute | solution.py:164
  53.7 25.0 %collective-permute-start.2 = (bf16[512,768]{1,0:T(8,128)(2,1)S(1)}, bf16[512,768]{1,0:T(8,128)(2,1)S(1)}, u32[]{:S(2)}, u32[]{:S(2)}) collective-permute-start(bf16[512,768]{1,0:T(8,128)(2,1)S(1)} %copy-done.1), channel_id=1, source_target_pairs={{0,6},{1,7},{2,0},{3,1},{4,2},{5,3},{6,4},{7,5},{8,14},{9,15},{10,... | collective-permute-start | bytes 2359304 | tf_op jit(solution)/shard_map/ppermute | solution.py:165
  54.5 39.7 %collective-permute-start.3 = (bf16[512,768]{1,0:T(8,128)(2,1)S(1)}, bf16[512,768]{1,0:T(8,128)(2,1)}, u32[]{:S(2)}, u32[]{:S(2)}) collective-permute-start(bf16[512,768]{1,0:T(8,128)(2,1)S(1)} %copy-done.1), channel_id=1, source_target_pairs={{0,4},{1,5},{2,6},{3,7},{4,0},{5,1},{6,2},{7,3},{8,12},{9,13},{10,... | collective-permute-start | bytes 2359304 | tf_op jit(solution)/shard_map/ppermute | solution.py:166
  60.7 0.8 copy-start
  64.5 29.8 %collective-permute-start = (f32[10,128,128]{2,1,0:T(8,128)}, f32[10,128,128]{2,1,0:T(8,128)}, u32[]{:S(2)}, u32[]{:S(2)}) collective-permute-start(f32[10,128,128]{2,1,0:T(8,128)} %pair.1.own), channel_id=1, source_target_pairs={{0,1},{1,0},{2,3},{3,2},{4,5},{5,4},{6,7},{7,6},{8,9},{9,8},{10,11... | collective-permute-start | bytes 1966088 | tf_op jit(solution)/shard_map/ppermute | solution.py:201
  77.4 16.9 %copy-start.2 = (bf16[512,768]{1,0:T(8,128)(2,1)}, bf16[512,768]{1,0:T(8,128)(2,1)S(1)}, u32[]{:S(2)}) copy-start(bf16[512,768]{1,0:T(8,128)(2,1)S(1)} %collective-permute-done.1.left) | copy-start | bytes 2359300
  78.6 15.6 %copy-start.3 = (bf16[512,768]{1,0:T(8,128)(2,1)}, bf16[512,768]{1,0:T(8,128)(2,1)S(1)}, u32[]{:S(2)}) copy-start(bf16[512,768]{1,0:T(8,128)(2,1)S(1)} %collective-permute-done.2.right) | copy-start | bytes 2359300

commit v3 on v2

--- a/solution.py
+++ b/solution.py
@@ -10,7 +10,8 @@
 BF16 = jnp.bfloat16
 VMEM = pl.BlockSpec(memory_space=pltpu.VMEM)
 SMEM = pl.BlockSpec(memory_space=pltpu.SMEM)
-ANY = pl.BlockSpec(memory_space=pl.ANY)
+HBM = pl.BlockSpec(memory_space=pltpu.HBM)
+GRANT = pltpu.CompilerParams(vmem_limit_bytes=24 * 1024 * 1024)
 LANES = 128
 OWNERS = 32
 PARTS = 8
@@ -21,13 +22,21 @@
 UPPER = [(g, h) for g in range(GROUPS) for h in range(g, GROUPS)]
 
 
+def near(x):
+    return pltpu.with_memory_space_constraint(x, pltpu.VMEM)
+
+
+def away(x):
+    return pltpu.with_memory_space_constraint(x, pltpu.HBM)
+
+
 def holder_of(block):
     return (block * 1366) >> 16
 
 
-def pick_kernel(ids, rows_s, cols_s, rows_v, cols_v, loadings, out, arrival, keys_v, keys_s, seen, sems, key_sem):
-    me = ids[0]
-    part = ids[1]
+def pick_kernel(rows_s, cols_s, rows_v, cols_v, loadings, out, arrival, keys_v, keys_s, seen, sems, key_sem):
+    me = lax.axis_index("fac")
+    part = lax.axis_index("scn")
     lane = lax.broadcasted_iota(jnp.int32, rows_v.shape, 1) & (CAP - 1)
 
     def keyed(blocks, first_slot):
@@ -44,6 +53,16 @@
     keys_v[...] = keys
     copy = pltpu.make_async_copy(keys_v, keys_s, key_sem)
     copy.start()
+    copy.wait()
+
+    def fetch(slot, offset):
+        start = pl.multiple_of(offset * LANES + part * SLICE, SLICE)
+        return pltpu.make_async_copy(loadings.at[pl.ds(start, SLICE), :], out.at[slot], sems.at[slot])
+
+    for o in range(OWNERS):
+        row, col = o // 8, (o % 8) * CAP
+        fetch(2 * o, jnp.minimum(keys_s[row, col] & 63, BLOCKS_DEV - 1)).start()
+        fetch(2 * o + 1, jnp.minimum((-keys_s[4 + row, col]) & 63, BLOCKS_DEV - 1)).start()
     for h in range(OWNERS):
         seen[h] = 0
     for t in range(2 * CAP):
@@ -51,16 +70,6 @@
         holder = holder_of(block)
         arrival[t] = 2 * holder + seen[holder]
         seen[holder] = 1
-    copy.wait()
-
-    def fetch(slot, offset):
-        start = pl.multiple_of(offset * LANES + part * SLICE, SLICE)
-        return pltpu.make_async_copy(loadings.at[pl.ds(start, SLICE), :], out.at[slot], sems.at[slot])
-
-    for o in range(OWNERS):
-        row, col = o // 8, (o % 8) * CAP
-        fetch(2 * o, jnp.minimum(keys_s[row, col] & 63, BLOCKS_DEV - 1)).start()
-        fetch(2 * o + 1, jnp.minimum((-keys_s[4 + row, col]) & 63, BLOCKS_DEV - 1)).start()
     for slot in range(2 * OWNERS):
         fetch(slot, 0).wait()
 
@@ -76,9 +85,9 @@
         out[p // 2, 4 * GROUPS + p % 2] = gamma[p]
 
 
-def pair_kernel(ids, rows_s, cols_s, count_s, recv, out):
-    me = ids[0]
-    part = ids[1]
+def pair_kernel(rows_s, cols_s, count_s, recv, out):
+    me = lax.axis_index("fac")
+    part = lax.axis_index("scn")
 
     def block(b):
         tiles = [recv[:, b * GROUPS + g].reshape(LANES, LANES) for g in range(GROUPS)]
@@ -115,9 +124,9 @@
         out[k] = summed
 
 
-def form_kernel(ids, own, other, here, left, right, far, slope, out):
+def form_kernel(own, other, here, left, right, far, slope, out):
     columns = here.shape[1]
-    chip = ids[1] // 2
+    chip = lax.axis_index("scn") // 2
     blocks = [(own[k] + other[k]).astype(BF16) for k in range(len(UPPER))]
     wide = [
         jnp.concatenate([b for b, (i, _) in zip(blocks, UPPER) if i == g], axis=1)
@@ -145,12 +154,10 @@
     parts = jnp.concatenate(
         [one, two, v.astype(BF16), jnp.zeros((5, v.shape[1]), BF16)], axis=0
     )
-    linear = jnp.dot(parts, here[...], preferred_element_type=F32)
-    linear = jnp.sum(linear, axis=0, keepdims=True)
-    store(chip, quadratic(lambda a, b: here[a:b, :]) + linear)
-    store((chip + 3) & 3, quadratic(lambda a, b: left[a:b, :]))
-    store((chip + 1) & 3, quadratic(lambda a, b: right[a:b, :]))
-    store((chip + 2) & 3, quadratic(lambda a, b: far[a:b, :]))
+    for step, rows_of in enumerate((here, right, far, left)):
+        linear = jnp.dot(parts, rows_of[...], preferred_element_type=F32)
+        linear = jnp.sum(linear, axis=0, keepdims=True)
+        store((chip + step) & 3, quadratic(lambda a, b: rows_of[a:b, :]) + linear)
 
 
 def ring(step):
@@ -160,17 +167,17 @@
 def body(loadings, draws, delta, gamma, pair_rows, pair_cols, pair_count):
     columns = draws.shape[1]
     depth = loadings.shape[1]
-    ids = jnp.stack([lax.axis_index("fac"), lax.axis_index("scn")]).astype(jnp.int32)
+    rows, cols = away(pair_rows), away(pair_cols)
     left = lax.ppermute(draws, "scn", ring(2))
     right = lax.ppermute(draws, "scn", ring(-2))
     far = lax.ppermute(draws, "scn", ring(4))
     outgoing, arrival = pl.pallas_call(
         pick_kernel,
         out_shape=(
-            jax.ShapeDtypeStruct((2 * OWNERS, SLICE, depth), BF16),
+            pltpu.VMEM((2 * OWNERS, SLICE, depth), BF16),
             jax.ShapeDtypeStruct((2 * CAP,), jnp.int32),
         ),
-        in_specs=[SMEM, SMEM, SMEM, VMEM, VMEM, ANY],
+        in_specs=[SMEM, SMEM, VMEM, VMEM, HBM],
         out_specs=(VMEM, SMEM),
         scratch_shapes=[
             pltpu.VMEM((8, LANES), jnp.int32),
@@ -179,33 +186,41 @@
             pltpu.SemaphoreType.DMA((2 * OWNERS,)),
             pltpu.SemaphoreType.DMA,
         ],
+        compiler_params=GRANT,
         name="pick",
-    )(ids, pair_rows, pair_cols, pair_rows.reshape(4, LANES), pair_cols.reshape(4, LANES), loadings)
+    )(rows, cols, away(pair_rows.reshape(4, LANES)), away(pair_cols.reshape(4, LANES)), away(loadings))
     arrived = lax.all_to_all(outgoing, "fac", split_axis=0, concat_axis=0, tiled=True)
-    slope = jnp.sum(delta[:, None] * loadings.astype(F32), axis=0)
+    chip = lax.axis_index("scn") // 2
+    quarter = loadings.shape[0] // (PARTS // 2)
+    some = lax.dynamic_slice_in_dim(loadings, chip * quarter, quarter)
+    shares = lax.dynamic_slice_in_dim(delta, chip * quarter, quarter)
+    slope = jnp.sum(shares[:, None] * some.astype(F32), axis=0)
     grouped = pl.pallas_call(
         regroup_kernel,
-        out_shape=jax.ShapeDtypeStruct((PARTS, 18, SLICE, LANES), BF16),
+        out_shape=pltpu.VMEM((PARTS, 18, SLICE, LANES), BF16),
         in_specs=[SMEM, VMEM, VMEM],
         out_specs=VMEM,
+        compiler_params=GRANT,
         name="regroup",
-    )(arrival, arrived, gamma)
+    )(arrival, near(arrived), gamma)
     pairs = lax.all_to_all(grouped, "scn", split_axis=0, concat_axis=0, tiled=True)
     own = pl.pallas_call(
         pair_kernel,
-        out_shape=jax.ShapeDtypeStruct((len(UPPER), LANES, LANES), F32),
-        in_specs=[SMEM, SMEM, SMEM, SMEM, VMEM],
+        out_shape=pltpu.VMEM((len(UPPER), LANES, LANES), F32),
+        in_specs=[SMEM, SMEM, SMEM, VMEM],
         out_specs=VMEM,
+        compiler_params=GRANT,
         name="pair",
-    )(ids, pair_rows, pair_cols, pair_count, pairs)
+    )(rows, cols, away(pair_count), near(pairs))
     other = lax.ppermute(own, "scn", [(i, i ^ 1) for i in range(PARTS)])
     spread = pl.pallas_call(
         form_kernel,
-        out_shape=jax.ShapeDtypeStruct((PARTS // 2, 8, LANES), F32),
-        in_specs=[SMEM] + [VMEM] * 7,
+        out_shape=pltpu.VMEM((PARTS // 2, 8, LANES), F32),
+        in_specs=[VMEM] * 7,
         out_specs=VMEM,
+        compiler_params=GRANT,
         name="form",
-    )(ids, own, other, draws, left, right, far, slope.reshape(1, depth))
+    )(near(own), near(other), draws, near(left), near(right), near(far), slope.reshape(1, depth))
     chips = [[c + 2 * x for x in range(PARTS // 2)] for c in range(2)]
     along = lax.all_to_all(
         spread, "scn", split_axis=0, concat_axis=0, tiled=True, axis_index_groups=chips

time: 126 us -> 122 us (0.968)
  waiting for transfers between devices: 29.8 us -> 33.9 us
  other arithmetic: 5.47 us -> 1.83 us
  Pallas kernels: 14.2 us -> 10.8 us
    ppermute x1, waiting for transfers between devices: 8.15 us -> 12.2 us  [body(): left = lax.ppermute(draws, 'scn', ring(2))]
    pallas_call x4, Pallas kernels: 14.2 us -> 10.8 us  [the longest x1 4.42 us: body(): pl.pallas_call(pick_kernel, out_shape=(pltpu.VMEM((2 * OWNERS, SLICE, dep...]
    reduce_sum x1, other arithmetic: 4.77 us -> 1.79 us  [body(): slope = jnp.sum(shares[:, None] * some.astype(F32), axis=0)]
  transfers between devices with their start and end apart: 5 -> 5, of which waited for: 4 -> 4; matrix products, arithmetic and copies ran while one was open for 4% -> 2% of each run, Pallas kernels for 2% -> 1%
where the time goes in v3:
time: 122 us; the launch traced here: 120 us
  blocking collectives  63.7 us (52%)
  waiting for transfers between devices  33.9 us (28%)
  Pallas kernels  10.8 us (9%)
  starting transfers between devices  8.22 us (7%)
  other arithmetic  1.83 us (2%)
  local copies, waits for them, and re-layouts  1.41 us (1%)
    all_to_all x1, blocking collectives, body(): lax.all_to_all(outgoing, 'fac', split_axis=0, concat_axis=0, tiled=True)  40 us
    ppermute x1, waiting for transfers between devices, body(): far = lax.ppermute(draws, 'scn', ring(4))  15.5 us
    all_to_all x1, blocking collectives, body(): every = lax.all_to_all(mine, 'fac', split_axis=0, concat_axis=0, tiled=True)  15.3 us
    ppermute x1, waiting for transfers between devices, body(): left = lax.ppermute(draws, 'scn', ring(2))  12.2 us
    all_to_all x1, blocking collectives, body(): lax.all_to_all(spread, 'scn', split_axis=0, concat_axis=0, tiled=True, ax...  8.45 us
    all_to_all x1, waiting for transfers between devices, body(): lax.all_to_all(grouped, 'scn', split_axis=0, concat_axis=0, tiled=True)  4.83 us
    all_to_all x1, starting transfers between devices, body(): lax.all_to_all(grouped, 'scn', split_axis=0, concat_axis=0, tiled=True)  4.8 us
    pallas_call x1, Pallas kernels, body(): pl.pallas_call(pick_kernel, out_shape=(pltpu.VMEM((2 * OWNERS, SLICE, dep...  4.42 us
  transfers between devices with their start and end apart: 5, of which 4 were waited for; matrix products, arithmetic and copies ran while one was open for 2% of the time, Pallas kernels for 1%

profile of v3, /device:TPU:4, one launch (start us, length us, event | category | flops | bytes accessed | tf_op | source)
XLA Modules:
  0.0 120.0 jit_solution(4297483954626541978)
XLA Ops:
  0.0 0.0 copy-start.1
  0.0 4.4 %pick.1 = (bf16[64,16,512]{2,1,0:T(8,128)(2,1)S(1)}, s32[32]{0:T(128)S(1)}) custom-call(s32[512]{0:T(512)} %rows_s.3, s32[512]{0:T(512)} %cols_s.3, s32[4,128]{1,0:T(4,128)} %bitcast.6, s32[4,128]{1,0:T(4,128)} %bitcast.7, bf16[6144,512]{1,0:T(8,128)(2,1)} %loadings.1), custom_call_target="tpu_custom_call" | custom-call | tf_op jit(solution)/shard_map/pick/pallas_call | solution.py:174
  4.4 0.0 copy-start
  4.4 40.0 %all_to_all.20.recv = bf16[64,16,512]{2,1,0:T(8,128)(2,1)S(1)} all-to-all(bf16[64,16,512]{2,1,0:T(8,128)(2,1)S(1)} %get-tuple-element.8), channel_id=1, replica_groups=mesh['fac'=32,'scn'=8] {'fac'}, dimensions={0} | all-to-all | bytes 2097152 | tf_op jit(solution)/shard_map/all_to_all | solution.py:192
  44.4 0.0 copy-done.1
  44.4 1.4 %regroup.1 = bf16[8,18,16,128]{3,2,1,0:T(8,128)(2,1)} custom-call(s32[32]{0:T(128)S(1)} %get-tuple-element.7.arrival, bf16[64,16,512]{2,1,0:T(8,128)(2,1)S(1)} %all_to_all.20.recv, bf16[16,16,128]{2,1,0:T(8,128)(2,1)S(1)} %copy-done.1), custom_call_target="tpu_custom_call" | custom-call | tf_op jit(solution)/shard_map/regroup/pallas_call | solution.py:198
  45.8 4.8 %all-to-all-start.1 = ((bf16[8,18,16,128]{3,2,1,0:T(8,128)(2,1)}), bf16[8,18,16,128]{3,2,1,0:T(8,128)(2,1)S(1)}, u32[]{:S(2)}, u32[]{:S(2)}) async-start(bf16[8,18,16,128]{3,2,1,0:T(8,128)(2,1)} %regroup.1), calls=%async_computation.1 | async-start | bytes 1179648 | tf_op jit(solution)/shard_map/all_to_all | solution.py:206
  50.6 0.0 copy-done
  50.6 1.2 collective-permute-start.1
  51.8 0.9 collective-permute-start.2
  52.7 1.3 %collective-permute-start.3 = (bf16[512,768]{1,0:T(8,128)(2,1)S(1)}, bf16[512,768]{1,0:T(8,128)(2,1)}, u32[]{:S(2)}, u32[]{:S(2)}) collective-permute-start(bf16[512,768]{1,0:T(8,128)(2,1)S(1)} %copy-done), channel_id=1, source_target_pairs={{0,4},{1,5},{2,6},{3,7},{4,0},{5,1},{6,2},{7,3},{8,12},{9,13},{10,... | collective-permute-start | bytes 2359304 | tf_op jit(solution)/shard_map/ppermute | solution.py:173
  53.9 4.8 %all-to-all-done.1.recv = bf16[8,18,16,128]{3,2,1,0:T(8,128)(2,1)S(1)} async-done(((bf16[8,18,16,128]{3,2,1,0:T(8,128)(2,1)}), bf16[8,18,16,128]{3,2,1,0:T(8,128)(2,1)S(1)}, u32[]{:S(2)}, u32[]{:S(2)}) %all-to-all-start.1) | async-done | bytes 589856 | tf_op jit(solution)/shard_map/all_to_all | solution.py:206
  58.8 1.8 %pair.1.own = f32[10,128,128]{2,1,0:T(8,128)S(1)} custom-call(s32[512]{0:T(512)} %rows_s.3, s32[512]{0:T(512)} %cols_s.3, s32[32]{0:T(128)} %count_s.1, bf16[8,18,16,128]{3,2,1,0:T(8,128)(2,1)S(1)} %all-to-all-done.1.recv), custom_call_target="tpu_custom_call" | custom-call | tf_op jit(solution)/shard_map/pair/pallas_call | solution.py:207
  60.6 0.1 collective-permute-start
  60.7 0.8 dynamic_slice.6
  61.5 1.8 %multiply_reduce_fusion = f32[512]{0:T(512)S(1)} fusion(bf16[6144,512]{1,0:T(8,128)(2,1)} %loadings.1, s32[]{:T(128)S(6)} %select_n.10, f32[1536]{0:T(1024)S(1)} %dynamic_slice.6), kind=kLoop, calls=%fused_computation | loop fusion | flops 2358784 | bytes 1581060 | tf_op jit(solution)/shard_map/reduce_sum | solution.py:197
  63.3 12.2 %collective-permute-done.1.left = bf16[512,768]{1,0:T(8,128)(2,1)S(1)} collective-permute-done((bf16[512,768]{1,0:T(8,128)(2,1)S(1)}, bf16[512,768]{1,0:T(8,128)(2,1)S(1)}, u32[]{:S(2)}, u32[]{:S(2)}) %collective-permute-start.1) | collective-permute-done | bytes 786464 | tf_op jit(solution)/shard_map/ppermute | solution.py:171
  75.5 1.4 %collective-permute-done.2.right = bf16[512,768]{1,0:T(8,128)(2,1)} collective-permute-done((bf16[512,768]{1,0:T(8,128)(2,1)S(1)}, bf16[512,768]{1,0:T(8,128)(2,1)}, u32[]{:S(2)}, u32[]{:S(2)}) %collective-permute-start.2) | collective-permute-done | bytes 786464 | tf_op jit(solution)/shard_map/ppermute | solution.py:172
  76.9 15.5 %collective-permute-done.3.far = bf16[512,768]{1,0:T(8,128)(2,1)} collective-permute-done((bf16[512,768]{1,0:T(8,128)(2,1)S(1)}, bf16[512,768]{1,0:T(8,128)(2,1)}, u32[]{:S(2)}, u32[]{:S(2)}) %collective-permute-start.3) | collective-permute-done | bytes 786464 | tf_op jit(solution)/shard_map/ppermute | solution.py:173
  92.4 0.0 collective-permute-done.other
  92.4 3.2 %form.1 = f32[4,8,128]{2,1,0:T(8,128)S(1)} custom-call(f32[10,128,128]{2,1,0:T(8,128)S(1)} %pair.1.own, f32[10,128,128]{2,1,0:T(8,128)S(1)} %collective-permute-done.other, bf16[512,768]{1,0:T(8,128)(2,1)S(1)} %copy-done, bf16[512,768]{1,0:T(8,128)(2,1)S(1)} %collective-permute-done.1.left, bf16[512,768]{1,0:T(8,128)(2,1)} %collective-permute-done.2.right, ...), custom_call_target="tpu_custom_call" | custom-call | tf_op jit(solution)/shard_map/form/pallas_call | solution.py:216
  95.6 8.4 %all_to_all.21 = f32[4,8,128]{2,1,0:T(8,128)S(1)} all-to-all(f32[4,8,128]{2,1,0:T(8,128)S(1)} %form.1), channel_id=1, replica_groups={{0,2,4,6},{1,3,5,7},{8,10,12,14},{9,11,13,15},{16,18,20,22},{17,19,21,2..., dimensions={0} | all-to-all | bytes 32768 | tf_op jit(solution)/shard_map/all_to_all | solution.py:225
  104.1 15.3 %all_to_all.22 = f32[32,8,128]{2,1,0:T(8,128)S(1)} all-to-all(f32[32,8,128]{2,1,0:T(8,128)S(1)} %broadcast_in_dim.2), channel_id=1, replica_groups=mesh['fac'=32,'scn'=8] {'fac'}, dimensions={0} | all-to-all | bytes 262144 | tf_op jit(solution)/shard_map/all_to_all | solution.py:229
  119.4 0.6 slice_bitcast_fusion
  (3 shorter events, 0.1 us)
Async XLA Ops:
  0.0 44.4 %copy-start.1 = (bf16[16,16,128]{2,1,0:T(8,128)(2,1)S(1)}, bf16[16,16,128]{2,1,0:T(8,128)(2,1)}, u32[]{:S(2)}) copy-start(bf16[16,16,128]{2,1,0:T(8,128)(2,1)} %gamma.1) | copy-start | bytes 196612
  4.4 46.2 %copy-start = (bf16[512,768]{1,0:T(8,128)(2,1)S(1)}, bf16[512,768]{1,0:T(8,128)(2,1)}, u32[]{:S(2)}) copy-start(bf16[512,768]{1,0:T(8,128)(2,1)} %here.1) | copy-start | bytes 2359300
  45.8 13.0 %all-to-all-start.1 = ((bf16[8,18,16,128]{3,2,1,0:T(8,128)(2,1)}), bf16[8,18,16,128]{3,2,1,0:T(8,128)(2,1)S(1)}, u32[]{:S(2)}, u32[]{:S(2)}) async-start(bf16[8,18,16,128]{3,2,1,0:T(8,128)(2,1)} %regroup.1), calls=%async_computation.1 | async-start | bytes 1179648 | tf_op jit(solution)/shard_map/all_to_all | solution.py:206
  50.6 24.9 %collective-permute-start.1 = (bf16[512,768]{1,0:T(8,128)(2,1)S(1)}, bf16[512,768]{1,0:T(8,128)(2,1)S(1)}, u32[]{:S(2)}, u32[]{:S(2)}) collective-permute-start(bf16[512,768]{1,0:T(8,128)(2,1)S(1)} %copy-done), channel_id=1, source_target_pairs={{0,2},{1,3},{2,4},{3,5},{4,6},{5,7},{6,0},{7,1},{8,10},{9,11},{10,... | collective-permute-start | bytes 2359304 | tf_op jit(solution)/shard_map/ppermute | solution.py:171
  51.8 25.1 %collective-permute-start.2 = (bf16[512,768]{1,0:T(8,128)(2,1)S(1)}, bf16[512,768]{1,0:T(8,128)(2,1)}, u32[]{:S(2)}, u32[]{:S(2)}) collective-permute-start(bf16[512,768]{1,0:T(8,128)(2,1)S(1)} %copy-done), channel_id=1, source_target_pairs={{0,6},{1,7},{2,0},{3,1},{4,2},{5,3},{6,4},{7,5},{8,14},{9,15},{10,... | collective-permute-start | bytes 2359304 | tf_op jit(solution)/shard_map/ppermute | solution.py:172
  52.7 39.7 %collective-permute-start.3 = (bf16[512,768]{1,0:T(8,128)(2,1)S(1)}, bf16[512,768]{1,0:T(8,128)(2,1)}, u32[]{:S(2)}, u32[]{:S(2)}) collective-permute-start(bf16[512,768]{1,0:T(8,128)(2,1)S(1)} %copy-done), channel_id=1, source_target_pairs={{0,4},{1,5},{2,6},{3,7},{4,0},{5,1},{6,2},{7,3},{8,12},{9,13},{10,... | collective-permute-start | bytes 2359304 | tf_op jit(solution)/shard_map/ppermute | solution.py:173
  60.6 31.8 %collective-permute-start = (f32[10,128,128]{2,1,0:T(8,128)S(1)}, f32[10,128,128]{2,1,0:T(8,128)S(1)}, u32[]{:S(2)}, u32[]{:S(2)}) collective-permute-start(f32[10,128,128]{2,1,0:T(8,128)S(1)} %pair.1.own), channel_id=1, source_target_pairs={{0,1},{1,0},{2,3},{3,2},{4,5},{5,4},{6,7},{7,6},{8,9},{9,8},{10,11... | collective-permute-start | bytes 1966088 | tf_op jit(solution)/shard_map/ppermute | solution.py:215

commit v4 on v3

v4 whole, which is shorter than its diff:
```python
import jax
import jax.numpy as jnp
from jax import lax
from jax.experimental import pallas as pl
from jax.experimental.pallas import tpu as pltpu
from jax.sharding import PartitionSpec as P


F32 = jnp.float32
BF16 = jnp.bfloat16
VMEM = pl.BlockSpec(memory_space=pltpu.VMEM)
SMEM = pl.BlockSpec(memory_space=pltpu.SMEM)
HBM = pl.BlockSpec(memory_space=pltpu.HBM)
GRANT = pltpu.CompilerParams(vmem_limit_bytes=24 * 1024 * 1024)
LANES = 128
OWNERS = 32
PARTS = 8
CAP = 16
BLOCKS_DEV = 48
SLICE = 16
GROUPS = 4
WIDE = 256


def near(x):
    return pltpu.with_memory_space_constraint(x, pltpu.VMEM)


def away(x):
    return pltpu.with_memory_space_constraint(x, pltpu.HBM)


def holder_of(block):
    return (block * 1366) >> 16


def pick_kernel(
    rows, cols, count, loadings, out, table,
    rows_v, cols_v, rows_s, cols_s, count_s, keys_v, keys_s, seen, sems, small,
):
    me = lax.axis_index("fac")
    part = lax.axis_index("scn")
    pairs = ((rows, rows_v), (cols, cols_v), (rows, rows_s), (cols, cols_s), (count, count_s))
    moves = [pltpu.make_async_copy(a, b, small.at[i]) for i, (a, b) in enumerate(pairs)]
    for move in moves:
        move.start()
    moves[0].wait()
    moves[1].wait()
    lane = lax.broadcasted_iota(jnp.int32, rows_v.shape, 1) & (CAP - 1)

    def keyed(blocks, first_slot):
        holder = holder_of(blocks)
        key = (lane + first_slot) * 64 + (blocks - holder * BLOCKS_DEV)
        mine = holder == me
        return jnp.where(mine, key, 1 << 20), jnp.where(mine, -key, 1)

    low_r, high_r = keyed(rows_v[...], 0)
    low_c, high_c = keyed(cols_v[...], CAP)
    keys = jnp.concatenate([jnp.minimum(low_r, low_c), jnp.minimum(high_r, high_c)], axis=0)
    for shift in (1, 2, 4, 8):
        keys = jnp.minimum(keys, pltpu.roll(keys, LANES - shift, 1))
    keys_v[...] = keys
    copy = pltpu.make_async_copy(keys_v, keys_s, small.at[5])
    copy.start()
    copy.wait()

    def fetch(slot, offset):
        start = pl.multiple_of(offset * LANES + part * SLICE, SLICE)
        return pltpu.make_async_copy(loadings.at[pl.ds(start, SLICE), :], out.at[slot], sems.at[slot])

    for o in range(OWNERS):
        row, col = o // 8, (o % 8) * CAP
        fetch(2 * o, jnp.minimum(keys_s[row, col] & 63, BLOCKS_DEV - 1)).start()
        fetch(2 * o + 1, jnp.minimum((-keys_s[4 + row, col]) & 63, BLOCKS_DEV - 1)).start()
    for move in moves[2:]:
        move.wait()
    for h in range(OWNERS):
        seen[h] = 0
    row = me // 8
    col = (me % 8) * CAP
    for t in range(2 * CAP):
        block = rows_s[row, col + t] if t < CAP else cols_s[row, col + t - CAP]
        holder = holder_of(block)
        table[t] = 2 * holder + seen[holder]
        seen[holder] = 1
    live = count_s[me]
    for p in range(CAP):
        weight = jnp.where(rows_s[row, col + p] == cols_s[row, col + p], 1, 2)
        table[2 * CAP + p] = jnp.where(p < live, weight, 0)
    for slot in range(2 * OWNERS):
        fetch(slot, 0).wait()


def regroup_kernel(table, recv, gamma, out):
    for t in range(2 * CAP):
        block = recv[table[t]]
        dest = (t % CAP) // 2
        first = ((t % 2) + 2 * (t // CAP)) * GROUPS
        for g in range(GROUPS):
            out[dest, first + g] = block[:, g * LANES : (g + 1) * LANES]
    for p in range(CAP):
        weight = table[2 * CAP + p].astype(F32)
        out[p // 2, 4 * GROUPS + p % 2] = (gamma[p].astype(F32) * weight).astype(BF16)


def pair_kernel(recv, out):
    def block(b):
        tiles = [recv[:, b * GROUPS + g].reshape(LANES, LANES) for g in range(GROUPS)]
        return jnp.concatenate(tiles, axis=1)

    left = []
    high = []
    low = []
    for q in range(2):
        stored = recv[:, 4 * GROUPS + q].reshape(LANES, LANES)
        half = jnp.dot(stored, block(2 + q), preferred_element_type=F32)
        top = half.astype(BF16)
        left.append(block(q))
        high.append(top)
        low.append((half - top.astype(F32)).astype(BF16))
    a = jnp.concatenate(left, axis=0)
    y = jnp.concatenate(high, axis=0)
    z = jnp.concatenate(low, axis=0)
    turned = jnp.concatenate([a.T, a.T, y.T, z.T], axis=1)
    other = jnp.concatenate([y, z, a, a], axis=0)
    out[0] = 0.25 * jnp.dot(turned[:WIDE], other[:, :WIDE], preferred_element_type=F32)
    right = jnp.dot(turned, other[:, WIDE:], preferred_element_type=F32)
    out[1] = 0.5 * right[:WIDE]
    out[2] = 0.25 * right[WIDE:]


def form_kernel(own, other, here, left, right, far, slope, out):
    chip = lax.axis_index("scn") // 2
    v = slope[...]
    one = v.astype(BF16)
    v = v - one.astype(F32)
    two = v.astype(BF16)
    v = v - two.astype(F32)
    fill = jnp.zeros((13, v.shape[1]), BF16)
    parts = jnp.concatenate([one, two, v.astype(BF16), fill], axis=0)
    first = (own[0] + other[0]).astype(BF16)
    cross = (own[1] + other[1]).astype(BF16)
    last = (own[2] + other[2]).astype(BF16)
    top = jnp.concatenate([first, parts[:, :WIDE]], axis=0)
    low = jnp.concatenate([cross, parts[:, WIDE:], last], axis=0)
    extra = WIDE + parts.shape[0]
    for step, group in enumerate((here, right, far, left)):
        upper = group[:WIDE, :]
        lower = group[WIDE:, :]
        image = jnp.dot(low, lower, preferred_element_type=F32)
        more = image[:extra] + jnp.dot(top, upper, preferred_element_type=F32)
        total = jnp.sum(more[:WIDE] * upper.astype(F32) + image[extra:] * lower.astype(F32), axis=0, keepdims=True)
        out[(chip + step) & 3] = total + jnp.sum(more[WIDE:], axis=0, keepdims=True)


def ring(step):
    return [(i, (i + step) % PARTS) for i in range(PARTS)]


def body(loadings, draws, delta, gamma, pair_rows, pair_cols, pair_count):
    columns = draws.shape[1]
    depth = loadings.shape[1]
    left = lax.ppermute(draws, "scn", ring(2))
    right = lax.ppermute(draws, "scn", ring(-2))
    far = lax.ppermute(draws, "scn", ring(4))
    outgoing, table = pl.pallas_call(
        pick_kernel,
        out_shape=(
            pltpu.VMEM((2 * OWNERS, SLICE, depth), BF16),
            jax.ShapeDtypeStruct((3 * CAP,), jnp.int32),
        ),
        in_specs=[HBM, HBM, HBM, HBM],
        out_specs=(VMEM, SMEM),
        scratch_shapes=[
            pltpu.VMEM((4, LANES), jnp.int32),
            pltpu.VMEM((4, LANES), jnp.int32),
            pltpu.SMEM((4, LANES), jnp.int32),
            pltpu.SMEM((4, LANES), jnp.int32),
            pltpu.SMEM((OWNERS,), jnp.int32),
            pltpu.VMEM((8, LANES), jnp.int32),
            pltpu.SMEM((8, LANES), jnp.int32),
            pltpu.SMEM((OWNERS,), jnp.int32),
            pltpu.SemaphoreType.DMA((2 * OWNERS,)),
            pltpu.SemaphoreType.DMA((6,)),
        ],
        compiler_params=GRANT,
        name="pick",
    )(
        away(pair_rows.reshape(4, LANES)),
        away(pair_cols.reshape(4, LANES)),
        away(pair_count),
        away(loadings),
    )
    arrived = lax.all_to_all(outgoing, "fac", split_axis=0, concat_axis=0, tiled=True)
    chip = lax.axis_index("scn") // 2
    quarter = loadings.shape[0] // (PARTS // 2)
    some = lax.dynamic_slice_in_dim(loadings, chip * quarter, quarter)
    shares = lax.dynamic_slice_in_dim(delta, chip * quarter, quarter)
    slope = jnp.sum(shares[:, None] * some.astype(F32), axis=0)
    grouped = pl.pallas_call(
        regroup_kernel,
        out_shape=pltpu.VMEM((PARTS, 18, SLICE, LANES), BF16),
        in_specs=[SMEM, VMEM, VMEM],
        out_specs=VMEM,
        compiler_params=GRANT,
        name="regroup",
    )(table, near(arrived), gamma)
    pairs = lax.all_to_all(grouped, "scn", split_axis=0, concat_axis=0, tiled=True)
    own = pl.pallas_call(
        pair_kernel,
        out_shape=pltpu.VMEM((3, WIDE, WIDE), F32),
        in_specs=[VMEM],
        out_specs=VMEM,
        compiler_params=GRANT,
        name="pair",
    )(near(pairs))
    other = lax.ppermute(own, "scn", [(i, i ^ 1) for i in range(PARTS)])
    spread = pl.pallas_call(
        form_kernel,
        out_shape=pltpu.VMEM((PARTS // 2, 1, columns), F32),
        in_specs=[VMEM] * 7,
        out_specs=VMEM,
        compiler_params=GRANT,
        name="form",
    )(near(own), near(other), draws, near(left), near(right), near(far), slope.reshape(1, depth))
    chips = [[c + 2 * x for x in range(PARTS // 2)] for c in range(2)]
    along = lax.all_to_all(
        spread, "scn", split_axis=0, concat_axis=0, tiled=True, axis_index_groups=chips
    )
    mine = jnp.broadcast_to(jnp.sum(along, axis=0)[None], (OWNERS, 1, columns))
    every = lax.all_to_all(mine, "fac", split_axis=0, concat_axis=0, tiled=True)
    return jnp.sum(every, axis=0).reshape(-1)


def solution(mesh):
    in_specs = (P("fac", None), P(None, "scn"), P("fac"), P("fac", "scn", None), P(), P(), P())
    out_specs = P("scn")
    return jax.shard_map(body, mesh=mesh, in_specs=in_specs, out_specs=out_specs, check_vma=False)
```

time: 122 us -> 121 us (level)
  no operation moved by 1% of the time
where the time goes in v4:
time: 121 us; the launch traced here: 120 us
  blocking collectives  63.5 us (52%)
  waiting for transfers between devices  34.9 us (29%)
  Pallas kernels  9.66 us (8%)
  starting transfers between devices  8.22 us (7%)
  other arithmetic  2.48 us (2%)
    all_to_all x1, blocking collectives, body(): lax.all_to_all(outgoing, 'fac', split_axis=0, concat_axis=0, tiled=True)  40 us
    ppermute x1, waiting for transfers between devices, body(): far = lax.ppermute(draws, 'scn', ring(4))  15.5 us
    all_to_all x1, blocking collectives, body(): every = lax.all_to_all(mine, 'fac', split_axis=0, concat_axis=0, tiled=True)  15.1 us
    ppermute x1, waiting for transfers between devices, body(): left = lax.ppermute(draws, 'scn', ring(2))  13.2 us
    all_to_all x1, blocking collectives, body(): lax.all_to_all(spread, 'scn', split_axis=0, concat_axis=0, tiled=True, ax...  8.43 us
    all_to_all x1, waiting for transfers between devices, body(): lax.all_to_all(grouped, 'scn', split_axis=0, concat_axis=0, tiled=True)  4.83 us
    all_to_all x1, starting transfers between devices, body(): lax.all_to_all(grouped, 'scn', split_axis=0, concat_axis=0, tiled=True)  4.8 us
    pallas_call x1, Pallas kernels, body(): pl.pallas_call(pick_kernel, out_shape=(pltpu.VMEM((2 * OWNERS, SLICE, dep...  4.32 us
  transfers between devices with their start and end apart: 5, of which 4 were waited for; matrix products, arithmetic and copies ran while one was open for 2% of the time, Pallas kernels for 1%

profile of v4, /device:TPU:4, one launch (start us, length us, event | category | flops | bytes accessed | tf_op | source)
XLA Modules:
  0.0 119.7 jit_solution(17363566477796908136)
XLA Ops:
  0.0 0.0 copy-start.1
  0.0 4.3 %pick.1 = (bf16[64,16,512]{2,1,0:T(8,128)(2,1)S(1)}, s32[48]{0:T(128)S(1)}) custom-call(s32[4,128]{1,0:T(4,128)} %bitcast.4, s32[4,128]{1,0:T(4,128)} %bitcast.5, s32[32]{0:T(128)} %count.1, bf16[6144,512]{1,0:T(8,128)(2,1)} %loadings.1), custom_call_target="tpu_custom_call" | custom-call | tf_op jit(solution)/shard_map/pick/pallas_call | solution.py:166
  4.3 0.0 copy-start
  4.3 40.0 %all_to_all.20.recv = bf16[64,16,512]{2,1,0:T(8,128)(2,1)S(1)} all-to-all(bf16[64,16,512]{2,1,0:T(8,128)(2,1)S(1)} %get-tuple-element.8), channel_id=1, replica_groups=mesh['fac'=32,'scn'=8] {'fac'}, dimensions={0} | all-to-all | bytes 2097152 | tf_op jit(solution)/shard_map/all_to_all | solution.py:194
  44.3 0.0 copy-done.1
  44.3 1.4 %regroup.1 = bf16[8,18,16,128]{3,2,1,0:T(8,128)(2,1)} custom-call(s32[48]{0:T(128)S(1)} %get-tuple-element.7.table, bf16[64,16,512]{2,1,0:T(8,128)(2,1)S(1)} %all_to_all.20.recv, bf16[16,16,128]{2,1,0:T(8,128)(2,1)S(1)} %copy-done.1), custom_call_target="tpu_custom_call" | custom-call | tf_op jit(solution)/shard_map/regroup/pallas_call | solution.py:200
  45.7 4.8 %all-to-all-start.1 = ((bf16[8,18,16,128]{3,2,1,0:T(8,128)(2,1)}), bf16[8,18,16,128]{3,2,1,0:T(8,128)(2,1)S(1)}, u32[]{:S(2)}, u32[]{:S(2)}) async-start(bf16[8,18,16,128]{3,2,1,0:T(8,128)(2,1)} %regroup.1), calls=%async_computation.1 | async-start | bytes 1179648 | tf_op jit(solution)/shard_map/all_to_all | solution.py:208
  50.5 0.0 copy-done
  50.5 1.2 collective-permute-start.1
  51.7 0.9 collective-permute-start.2
  52.6 1.3 %collective-permute-start.3 = (bf16[512,768]{1,0:T(8,128)(2,1)S(1)}, bf16[512,768]{1,0:T(8,128)(2,1)}, u32[]{:S(2)}, u32[]{:S(2)}) collective-permute-start(bf16[512,768]{1,0:T(8,128)(2,1)S(1)} %copy-done), channel_id=1, source_target_pairs={{0,4},{1,5},{2,6},{3,7},{4,0},{5,1},{6,2},{7,3},{8,12},{9,13},{10,... | collective-permute-start | bytes 2359304 | tf_op jit(solution)/shard_map/ppermute | solution.py:165
  53.9 4.8 %all-to-all-done.1.recv = bf16[8,18,16,128]{3,2,1,0:T(8,128)(2,1)S(1)} async-done(((bf16[8,18,16,128]{3,2,1,0:T(8,128)(2,1)}), bf16[8,18,16,128]{3,2,1,0:T(8,128)(2,1)S(1)}, u32[]{:S(2)}, u32[]{:S(2)}) %all-to-all-start.1) | async-done | bytes 589856 | tf_op jit(solution)/shard_map/all_to_all | solution.py:208
  58.7 0.8 pair.1.own
  59.5 0.1 collective-permute-start
  59.6 0.8 dynamic_slice.6
  60.4 1.8 %multiply_reduce_fusion = f32[512]{0:T(512)S(1)} fusion(bf16[6144,512]{1,0:T(8,128)(2,1)} %loadings.1, s32[]{:T(128)S(6)} %select_n.10, f32[1536]{0:T(1024)S(1)} %dynamic_slice.6), kind=kLoop, calls=%fused_computation | loop fusion | flops 2358784 | bytes 1581060 | tf_op jit(solution)/shard_map/reduce_sum | solution.py:199
  62.2 13.2 %collective-permute-done.1.left = bf16[512,768]{1,0:T(8,128)(2,1)S(1)} collective-permute-done((bf16[512,768]{1,0:T(8,128)(2,1)S(1)}, bf16[512,768]{1,0:T(8,128)(2,1)S(1)}, u32[]{:S(2)}, u32[]{:S(2)}) %collective-permute-start.1) | collective-permute-done | bytes 786464 | tf_op jit(solution)/shard_map/ppermute | solution.py:163
  75.4 1.4 %collective-permute-done.2.right = bf16[512,768]{1,0:T(8,128)(2,1)} collective-permute-done((bf16[512,768]{1,0:T(8,128)(2,1)S(1)}, bf16[512,768]{1,0:T(8,128)(2,1)}, u32[]{:S(2)}, u32[]{:S(2)}) %collective-permute-start.2) | collective-permute-done | bytes 786464 | tf_op jit(solution)/shard_map/ppermute | solution.py:164
  76.8 15.5 %collective-permute-done.3.far = bf16[512,768]{1,0:T(8,128)(2,1)} collective-permute-done((bf16[512,768]{1,0:T(8,128)(2,1)S(1)}, bf16[512,768]{1,0:T(8,128)(2,1)}, u32[]{:S(2)}, u32[]{:S(2)}) %collective-permute-start.3) | collective-permute-done | bytes 786464 | tf_op jit(solution)/shard_map/ppermute | solution.py:165
  92.3 0.0 collective-permute-done.other
  92.3 3.1 %form.1 = f32[4,1,768]{2,1,0:T(1,128)S(1)} custom-call(f32[3,256,256]{2,1,0:T(8,128)S(1)} %pair.1.own, f32[3,256,256]{2,1,0:T(8,128)} %collective-permute-done.other, bf16[512,768]{1,0:T(8,128)(2,1)S(1)} %copy-done, bf16[512,768]{1,0:T(8,128)(2,1)S(1)} %collective-permute-done.1.left, bf16[512,768]{1,0:T(8,128)(2,1)} %collective-permute-done.2.right, ...), custom_call_target="tpu_custom_call" | custom-call | tf_op jit(solution)/shard_map/form/pallas_call | solution.py:218
  95.4 8.4 %all_to_all.21 = f32[4,1,768]{2,1,0:T(1,128)S(1)} all-to-all(f32[4,1,768]{2,1,0:T(1,128)S(1)} %form.1), channel_id=1, replica_groups={{0,2,4,6},{1,3,5,7},{8,10,12,14},{9,11,13,15},{16,18,20,22},{17,19,21,2..., dimensions={0} | all-to-all | bytes 24576 | tf_op jit(solution)/shard_map/all_to_all | solution.py:227
  103.9 0.1 broadcast_in_dim.2
  103.9 15.1 %all_to_all.22 = f32[32,1,768]{2,1,0:T(1,128)S(1)} all-to-all(f32[32,1,768]{2,1,0:T(1,128)S(1)} %broadcast_in_dim.2), channel_id=1, replica_groups=mesh['fac'=32,'scn'=8] {'fac'}, dimensions={0} | all-to-all | bytes 196608 | tf_op jit(solution)/shard_map/all_to_all | solution.py:231
  119.0 0.7 reduce_sum.29
  (1 shorter events, 0.0 us)
Async XLA Ops:
  0.0 44.3 %copy-start.1 = (bf16[16,16,128]{2,1,0:T(8,128)(2,1)S(1)}, bf16[16,16,128]{2,1,0:T(8,128)(2,1)}, u32[]{:S(2)}) copy-start(bf16[16,16,128]{2,1,0:T(8,128)(2,1)} %gamma.1) | copy-start | bytes 196612
  4.3 46.2 %copy-start = (bf16[512,768]{1,0:T(8,128)(2,1)S(1)}, bf16[512,768]{1,0:T(8,128)(2,1)}, u32[]{:S(2)}) copy-start(bf16[512,768]{1,0:T(8,128)(2,1)} %here.1) | copy-start | bytes 2359300
  45.7 13.0 %all-to-all-start.1 = ((bf16[8,18,16,128]{3,2,1,0:T(8,128)(2,1)}), bf16[8,18,16,128]{3,2,1,0:T(8,128)(2,1)S(1)}, u32[]{:S(2)}, u32[]{:S(2)}) async-start(bf16[8,18,16,128]{3,2,1,0:T(8,128)(2,1)} %regroup.1), calls=%async_computation.1 | async-start | bytes 1179648 | tf_op jit(solution)/shard_map/all_to_all | solution.py:208
  50.5 24.9 %collective-permute-start.1 = (bf16[512,768]{1,0:T(8,128)(2,1)S(1)}, bf16[512,768]{1,0:T(8,128)(2,1)S(1)}, u32[]{:S(2)}, u32[]{:S(2)}) collective-permute-start(bf16[512,768]{1,0:T(8,128)(2,1)S(1)} %copy-done), channel_id=1, source_target_pairs={{0,2},{1,3},{2,4},{3,5},{4,6},{5,7},{6,0},{7,1},{8,10},{9,11},{10,... | collective-permute-start | bytes 2359304 | tf_op jit(solution)/shard_map/ppermute | solution.py:163
  51.7 25.1 %collective-permute-start.2 = (bf16[512,768]{1,0:T(8,128)(2,1)S(1)}, bf16[512,768]{1,0:T(8,128)(2,1)}, u32[]{:S(2)}, u32[]{:S(2)}) collective-permute-start(bf16[512,768]{1,0:T(8,128)(2,1)S(1)} %copy-done), channel_id=1, source_target_pairs={{0,6},{1,7},{2,0},{3,1},{4,2},{5,3},{6,4},{7,5},{8,14},{9,15},{10,... | collective-permute-start | bytes 2359304 | tf_op jit(solution)/shard_map/ppermute | solution.py:164
  52.6 39.7 %collective-permute-start.3 = (bf16[512,768]{1,0:T(8,128)(2,1)S(1)}, bf16[512,768]{1,0:T(8,128)(2,1)}, u32[]{:S(2)}, u32[]{:S(2)}) collective-permute-start(bf16[512,768]{1,0:T(8,128)(2,1)S(1)} %copy-done), channel_id=1, source_target_pairs={{0,4},{1,5},{2,6},{3,7},{4,0},{5,1},{6,2},{7,3},{8,12},{9,13},{10,... | collective-permute-start | bytes 2359304 | tf_op jit(solution)/shard_map/ppermute | solution.py:165
  59.5 32.8 %collective-permute-start = (f32[3,256,256]{2,1,0:T(8,128)S(1)}, f32[3,256,256]{2,1,0:T(8,128)}, u32[]{:S(2)}, u32[]{:S(2)}) collective-permute-start(f32[3,256,256]{2,1,0:T(8,128)S(1)} %pair.1.own), channel_id=1, source_target_pairs={{0,1},{1,0},{2,3},{3,2},{4,5},{5,4},{6,7},{7,6},{8,9},{9,8},{10,11... | collective-permute-start | bytes 2359304 | tf_op jit(solution)/shard_map/ppermute | solution.py:217

commit v5 on v4

--- a/solution.py
+++ b/solution.py
@@ -20,6 +20,8 @@
 SLICE = 16
 GROUPS = 4
 WIDE = 256
+CHIPS = 4
+TILES = 18
 
 
 def near(x):
@@ -91,28 +93,45 @@
         fetch(slot, 0).wait()
 
 
-def regroup_kernel(table, recv, gamma, out):
-    for t in range(2 * CAP):
-        block = recv[table[t]]
-        dest = (t % CAP) // 2
-        first = ((t % 2) + 2 * (t // CAP)) * GROUPS
-        for g in range(GROUPS):
-            out[dest, first + g] = block[:, g * LANES : (g + 1) * LANES]
-    for p in range(CAP):
-        weight = table[2 * CAP + p].astype(F32)
-        out[p // 2, 4 * GROUPS + p % 2] = (gamma[p].astype(F32) * weight).astype(BF16)
-
-
-def pair_kernel(recv, out):
+def regroup_kernel(table, recv, gamma, keep, send):
+    part = lax.axis_index("scn")
+    chip = part // 2
+    core = part % 2
+    for step in range(CHIPS):
+        for out, column in ((keep, core), (send, 1 - core)):
+            first = 4 * ((chip + step) & 3) + 2 * column
+            for q in range(2):
+                for side in range(2):
+                    block = recv[table[first + q + side * CAP]]
+                    for g in range(GROUPS):
+                        out[step, (q + 2 * side) * GROUPS + g] = block[:, g * LANES : (g + 1) * LANES]
+                weight = table[2 * CAP + first + q].astype(F32)
+                out[step, 4 * GROUPS + q] = (gamma[first + q].astype(F32) * weight).astype(BF16)
+
+
+def merge_kernel(keep, swapped, *outs):
+    core = lax.axis_index("scn") % 2
+    for step, out in enumerate(outs):
+        out[core] = keep[step]
+        out[1 - core] = swapped[step]
+
+
+def pair_kernel(here, one_off, two_off, three_off, out, recv):
+    chip = lax.axis_index("scn") // 2
+    for step, chunk in enumerate((here, one_off, two_off, three_off)):
+        source = (chip + CHIPS - step) & 3
+        for core in range(2):
+            recv[:, 2 * source + core] = chunk[core]
+
     def block(b):
-        tiles = [recv[:, b * GROUPS + g].reshape(LANES, LANES) for g in range(GROUPS)]
+        tiles = [recv[b * GROUPS + g].reshape(LANES, LANES) for g in range(GROUPS)]
         return jnp.concatenate(tiles, axis=1)
 
     left = []
     high = []
     low = []
     for q in range(2):
-        stored = recv[:, 4 * GROUPS + q].reshape(LANES, LANES)
+        stored = recv[4 * GROUPS + q].reshape(LANES, LANES)
         half = jnp.dot(stored, block(2 + q), preferred_element_type=F32)
         top = half.astype(BF16)
         left.append(block(q))
@@ -129,8 +148,7 @@
     out[2] = 0.25 * right[WIDE:]
 
 
-def form_kernel(own, other, here, left, right, far, slope, out):
-    chip = lax.axis_index("scn") // 2
+def form_kernel(own, other, here, left, right, far, slope, *outs):
     v = slope[...]
     one = v.astype(BF16)
     v = v - one.astype(F32)
@@ -144,13 +162,13 @@
     top = jnp.concatenate([first, parts[:, :WIDE]], axis=0)
     low = jnp.concatenate([cross, parts[:, WIDE:], last], axis=0)
     extra = WIDE + parts.shape[0]
-    for step, group in enumerate((here, right, far, left)):
+    for group, out in zip((here, right, far, left), outs):
         upper = group[:WIDE, :]
         lower = group[WIDE:, :]
         image = jnp.dot(low, lower, preferred_element_type=F32)
         more = image[:extra] + jnp.dot(top, upper, preferred_element_type=F32)
         total = jnp.sum(more[:WIDE] * upper.astype(F32) + image[extra:] * lower.astype(F32), axis=0, keepdims=True)
-        out[(chip + step) & 3] = total + jnp.sum(more[WIDE:], axis=0, keepdims=True)
+        out[...] = total + jnp.sum(more[WIDE:], axis=0, keepdims=True)
 
 
 def ring(step):
@@ -197,37 +215,48 @@
     some = lax.dynamic_slice_in_dim(loadings, chip * quarter, quarter)
     shares = lax.dynamic_slice_in_dim(delta, chip * quarter, quarter)
     slope = jnp.sum(shares[:, None] * some.astype(F32), axis=0)
-    grouped = pl.pallas_call(
+    tiles = (TILES, SLICE, LANES)
+    keep, send = pl.pallas_call(
         regroup_kernel,
-        out_shape=pltpu.VMEM((PARTS, 18, SLICE, LANES), BF16),
+        out_shape=(pltpu.VMEM((CHIPS, *tiles), BF16), pltpu.VMEM((CHIPS, *tiles), BF16)),
         in_specs=[SMEM, VMEM, VMEM],
-        out_specs=VMEM,
+        out_specs=(VMEM, VMEM),
         compiler_params=GRANT,
         name="regroup",
     )(table, near(arrived), gamma)
-    pairs = lax.all_to_all(grouped, "scn", split_axis=0, concat_axis=0, tiled=True)
+    partner = [(i, i ^ 1) for i in range(PARTS)]
+    swapped = lax.ppermute(send, "scn", partner)
+    chunks = pl.pallas_call(
+        merge_kernel,
+        out_shape=(pltpu.VMEM((2, *tiles), BF16),) * CHIPS,
+        in_specs=[VMEM, VMEM],
+        out_specs=(VMEM,) * CHIPS,
+        compiler_params=GRANT,
+        name="merge",
+    )(near(keep), near(swapped))
+    moved = [lax.ppermute(chunks[k], "scn", ring(2 * k)) for k in range(1, CHIPS)]
     own = pl.pallas_call(
         pair_kernel,
         out_shape=pltpu.VMEM((3, WIDE, WIDE), F32),
-        in_specs=[VMEM],
+        in_specs=[VMEM] * CHIPS,
         out_specs=VMEM,
+        scratch_shapes=[pltpu.VMEM((TILES, PARTS, SLICE, LANES), BF16)],
         compiler_params=GRANT,
         name="pair",
-    )(near(pairs))
-    other = lax.ppermute(own, "scn", [(i, i ^ 1) for i in range(PARTS)])
+    )(near(chunks[0]), *[near(x) for x in moved])
+    other = lax.ppermute(own, "scn", partner)
     spread = pl.pallas_call(
         form_kernel,
-        out_shape=pltpu.VMEM((PARTS // 2, 1, columns), F32),
+        out_shape=(pltpu.VMEM((1, columns), F32),) * CHIPS,
         in_specs=[VMEM] * 7,
-        out_specs=VMEM,
+        out_specs=(VMEM,) * CHIPS,
         compiler_params=GRANT,
         name="form",
     )(near(own), near(other), draws, near(left), near(right), near(far), slope.reshape(1, depth))
-    chips = [[c + 2 * x for x in range(PARTS // 2)] for c in range(2)]
-    along = lax.all_to_all(
-        spread, "scn", split_axis=0, concat_axis=0, tiled=True, axis_index_groups=chips
-    )
-    mine = jnp.broadcast_to(jnp.sum(along, axis=0)[None], (OWNERS, 1, columns))
+    total = spread[0]
+    for k in range(1, CHIPS):
+        total = total + lax.ppermute(spread[k], "scn", ring(2 * k))
+    mine = jnp.broadcast_to(total[None], (OWNERS, 1, columns))
     every = lax.all_to_all(mine, "fac", split_axis=0, concat_axis=0, tiled=True)
     return jnp.sum(every, axis=0).reshape(-1)
 

time: 121 us -> 119 us (0.983)
  blocking collectives: 63.5 us -> 55 us
  waiting for transfers between devices: 34.9 us -> 39.1 us
  starting transfers between devices: 8.22 us -> 10.5 us
    ppermute x1 -> x8, waiting for transfers between devices: 0.01 us -> 11.7 us  [the longest x3 6.7 us: body(): lax.ppermute(chunks[k], 'scn', ring(2 * k))]
    all_to_all x1 -> x0, blocking collectives: 8.43 us -> none  [body(): lax.all_to_all(spread, 'scn', split_axis=0, concat_axis=0, tiled=True, ax...]
    ppermute x1 -> x8, starting transfers between devices: 0.09 us -> 8.39 us  [the longest x3 5.01 us: body(): total = total + lax.ppermute(spread[k], 'scn', ring(2 * k))]
    all_to_all x1 -> x0, waiting for transfers between devices: 4.83 us -> none  [body(): lax.all_to_all(grouped, 'scn', split_axis=0, concat_axis=0, tiled=True)]
    all_to_all x1 -> x0, starting transfers between devices: 4.8 us -> none  [body(): lax.all_to_all(grouped, 'scn', split_axis=0, concat_axis=0, tiled=True)]
    ppermute x1, waiting for transfers between devices: 13.2 us -> 11.2 us  [body(): left = lax.ppermute(draws, 'scn', ring(2))]
    ppermute x1, waiting for transfers between devices: 15.5 us -> 14.1 us  [body(): far = lax.ppermute(draws, 'scn', ring(4))]
    ppermute x1, starting transfers between devices: 1.29 us -> 0.01 us  [body(): far = lax.ppermute(draws, 'scn', ring(4))]
  transfers between devices with their start and end apart: 5 -> 11, of which waited for: 4 -> 9; matrix products, arithmetic and copies ran while one was open for 2% -> 2% of each run, Pallas kernels for 1% -> 1%
where the time goes in v5:
time: 119 us; the launch traced here: 117 us
  blocking collectives  55 us (46%)
  waiting for transfers between devices  39.1 us (33%)
  starting transfers between devices  10.5 us (9%)
  Pallas kernels  8.75 us (7%)
  other arithmetic  2.48 us (2%)
    all_to_all x1, blocking collectives, body(): lax.all_to_all(outgoing, 'fac', split_axis=0, concat_axis=0, tiled=True)  40 us
    all_to_all x1, blocking collectives, body(): every = lax.all_to_all(mine, 'fac', split_axis=0, concat_axis=0, tiled=True)  15.1 us
    ppermute x1, waiting for transfers between devices, body(): far = lax.ppermute(draws, 'scn', ring(4))  14.1 us
    ppermute x1, waiting for transfers between devices, body(): left = lax.ppermute(draws, 'scn', ring(2))  11.2 us
    ppermute x3, waiting for transfers between devices, body(): lax.ppermute(chunks[k], 'scn', ring(2 * k))  6.7 us
    ppermute x3, starting transfers between devices, body(): total = total + lax.ppermute(spread[k], 'scn', ring(2 * k))  5.01 us
    pallas_call x1, Pallas kernels, body(): pl.pallas_call(pick_kernel, out_shape=(pltpu.VMEM((2 * OWNERS, SLICE, dep...  4.32 us
    ppermute x3, waiting for transfers between devices, body(): total = total + lax.ppermute(spread[k], 'scn', ring(2 * k))  3.46 us
  transfers between devices with their start and end apart: 11, of which 9 were waited for; matrix products, arithmetic and copies ran while one was open for 2% of the time, Pallas kernels for 1%

profile of v5, /device:TPU:4, one launch (start us, length us, event | category | flops | bytes accessed | tf_op | source)
XLA Modules:
  0.0 116.8 jit_solution(9368972015573470670)
XLA Ops:
  0.0 4.3 %pick.1 = (bf16[64,16,512]{2,1,0:T(8,128)(2,1)S(1)}, s32[48]{0:T(128)S(1)}) custom-call(s32[4,128]{1,0:T(4,128)} %bitcast.4, s32[4,128]{1,0:T(4,128)} %bitcast.5, s32[32]{0:T(128)} %count.1, bf16[6144,512]{1,0:T(8,128)(2,1)} %loadings.1), custom_call_target="tpu_custom_call" | custom-call | tf_op jit(solution)/shard_map/pick/pallas_call | solution.py:184
  4.3 0.0 copy-start
  4.3 40.0 %all_to_all.10.recv = bf16[64,16,512]{2,1,0:T(8,128)(2,1)S(1)} all-to-all(bf16[64,16,512]{2,1,0:T(8,128)(2,1)S(1)} %get-tuple-element.18), channel_id=1, replica_groups=mesh['fac'=32,'scn'=8] {'fac'}, dimensions={0} | all-to-all | bytes 2097152 | tf_op jit(solution)/shard_map/all_to_all | solution.py:212
  44.3 0.6 regroup.1
  45.0 0.1 collective-permute-start
  45.1 1.6 %collective-permute-done.swapped = bf16[4,18,16,128]{3,2,1,0:T(8,128)(2,1)S(1)} collective-permute-done((bf16[4,18,16,128]{3,2,1,0:T(8,128)(2,1)S(1)}, bf16[4,18,16,128]{3,2,1,0:T(8,128)(2,1)S(1)}, u32[]{:S(2)}, u32[]{:S(2)}) %collective-permute-start) | collective-permute-done | bytes 294944 | tf_op jit(solution)/shard_map/ppermute | solution.py:228
  46.6 0.1 merge.1
  46.7 1.2 %collective-permute-start.1 = (bf16[2,18,16,128]{3,2,1,0:T(8,128)(2,1)S(1)}, bf16[2,18,16,128]{3,2,1,0:T(8,128)(2,1)S(1)}, u32[]{:S(2)}, u32[]{:S(2)}) collective-permute-start(bf16[2,18,16,128]{3,2,1,0:T(8,128)(2,1)S(1)} %get-tuple-element.22), channel_id=1, source_target_pairs={{0,2},{1,3},{2,4},{3,5},{4,6},{5,7},{6,0},{7,1},{8,10},{9,11},{10,... | collective-permute-start | bytes 442376 | tf_op jit(solution)/shard_map/ppermute | solution.py:237
  47.9 0.8 collective-permute-start.2
  48.8 1.1 collective-permute-start.3
  49.9 1.0 collective-permute-start.5
  50.9 1.1 collective-permute-start.6
  52.0 4.3 %collective-permute-done.1.one_off = bf16[2,18,16,128]{3,2,1,0:T(8,128)(2,1)S(1)} collective-permute-done((bf16[2,18,16,128]{3,2,1,0:T(8,128)(2,1)S(1)}, bf16[2,18,16,128]{3,2,1,0:T(8,128)(2,1)S(1)}, u32[]{:S(2)}, u32[]{:S(2)}) %collective-permute-start.1) | collective-permute-done | bytes 147488 | tf_op jit(solution)/shard_map/ppermute | solution.py:237
  56.3 0.0 collective-permute-start.7
  56.3 0.2 collective-permute-done.2.two_off
  56.6 2.1 %collective-permute-done.3.three_off = bf16[2,18,16,128]{3,2,1,0:T(8,128)(2,1)S(1)} collective-permute-done((bf16[2,18,16,128]{3,2,1,0:T(8,128)(2,1)S(1)}, bf16[2,18,16,128]{3,2,1,0:T(8,128)(2,1)S(1)}, u32[]{:S(2)}, u32[]{:S(2)}) %collective-permute-start.3) | collective-permute-done | bytes 147488 | tf_op jit(solution)/shard_map/ppermute | solution.py:237
  58.7 0.8 pair.1.own
  59.6 0.1 collective-permute-start.4
  59.7 0.8 dynamic_slice.6
  60.5 1.8 %multiply_reduce_fusion = f32[512]{0:T(512)S(1)} fusion(bf16[6144,512]{1,0:T(8,128)(2,1)} %loadings.1, s32[]{:T(128)S(6)} %select_n.10, f32[1536]{0:T(1024)S(1)} %dynamic_slice.6), kind=kLoop, calls=%fused_computation | loop fusion | flops 2358784 | bytes 1581060 | tf_op jit(solution)/shard_map/reduce_sum | solution.py:217
  62.3 11.2 %collective-permute-done.5.left = bf16[512,768]{1,0:T(8,128)(2,1)S(1)} collective-permute-done((bf16[512,768]{1,0:T(8,128)(2,1)S(1)}, bf16[512,768]{1,0:T(8,128)(2,1)S(1)}, u32[]{:S(2)}, u32[]{:S(2)}) %collective-permute-start.5) | collective-permute-done | bytes 786464 | tf_op jit(solution)/shard_map/ppermute | solution.py:181
  73.4 2.2 %collective-permute-done.6.right = bf16[512,768]{1,0:T(8,128)(2,1)S(1)} collective-permute-done((bf16[512,768]{1,0:T(8,128)(2,1)S(1)}, bf16[512,768]{1,0:T(8,128)(2,1)S(1)}, u32[]{:S(2)}, u32[]{:S(2)}) %collective-permute-start.6) | collective-permute-done | bytes 786464 | tf_op jit(solution)/shard_map/ppermute | solution.py:182
  75.6 14.1 %collective-permute-done.7.far = bf16[512,768]{1,0:T(8,128)(2,1)} collective-permute-done((bf16[512,768]{1,0:T(8,128)(2,1)S(1)}, bf16[512,768]{1,0:T(8,128)(2,1)}, u32[]{:S(2)}, u32[]{:S(2)}) %collective-permute-start.7) | collective-permute-done | bytes 786464 | tf_op jit(solution)/shard_map/ppermute | solution.py:183
  89.6 0.0 collective-permute-done.4.other
  89.6 2.9 %form.1 = (f32[1,768]{1,0:T(1,128)S(1)}, f32[1,768]{1,0:T(1,128)S(1)}, f32[1,768]{1,0:T(1,128)S(1)}, f32[1,768]{1,0:T(1,128)S(1)}) custom-call(f32[3,256,256]{2,1,0:T(8,128)S(1)} %pair.1.own, f32[3,256,256]{2,1,0:T(8,128)} %collective-permute-done.4.other, bf16[512,768]{1,0:T(8,128)(2,1)S(1)} %copy-done, bf16[512,768]{1,0:T(8,128)(2,1)S(1)} %collective-permute-done.5.left, ...), custom_call_target="tpu_custom_call" | custom-call | tf_op jit(solution)/shard_map/form/pallas_call | solution.py:248
  92.5 3.4 %collective-permute-start.10 = (f32[1,768]{1,0:T(1,128)S(1)}, f32[1,768]{1,0:T(1,128)S(1)}, u32[]{:S(2)}, u32[]{:S(2)}) collective-permute-start(f32[1,768]{1,0:T(1,128)S(1)} %get-tuple-element.28), channel_id=1, source_target_pairs={{0,6},{1,7},{2,0},{3,1},{4,2},{5,3},{6,4},{7,5},{8,14},{9,15},{10,... | collective-permute-start | bytes 9224 | tf_op jit(solution)/shard_map/ppermute | solution.py:258
  95.9 1.6 %collective-permute-start.9 = (f32[1,768]{1,0:T(1,128)S(1)}, f32[1,768]{1,0:T(1,128)S(1)}, u32[]{:S(2)}, u32[]{:S(2)}) collective-permute-start(f32[1,768]{1,0:T(1,128)S(1)} %get-tuple-element.27), channel_id=1, source_target_pairs={{0,4},{1,5},{2,6},{3,7},{4,0},{5,1},{6,2},{7,3},{8,12},{9,13},{10,... | collective-permute-start | bytes 9224 | tf_op jit(solution)/shard_map/ppermute | solution.py:258
  97.6 1.9 %collective-permute-done.8 = f32[1,768]{1,0:T(1,128)S(1)} collective-permute-done((f32[1,768]{1,0:T(1,128)S(1)}, f32[1,768]{1,0:T(1,128)S(1)}, u32[]{:S(2)}, u32[]{:S(2)}) %collective-permute-start.8) | collective-permute-done | bytes 3104 | tf_op jit(solution)/shard_map/ppermute | solution.py:258
  99.5 1.5 %collective-permute-done.9 = f32[1,768]{1,0:T(1,128)S(1)} collective-permute-done((f32[1,768]{1,0:T(1,128)S(1)}, f32[1,768]{1,0:T(1,128)S(1)}, u32[]{:S(2)}, u32[]{:S(2)}) %collective-permute-start.9) | collective-permute-done | bytes 3104 | tf_op jit(solution)/shard_map/ppermute | solution.py:258
  101.0 0.1 broadcast_in_dim.10
  101.1 15.1 %all_to_all.11 = f32[32,1,768]{2,1,0:T(1,128)S(1)} all-to-all(f32[32,1,768]{2,1,0:T(1,128)S(1)} %broadcast_in_dim.10), channel_id=1, replica_groups=mesh['fac'=32,'scn'=8] {'fac'}, dimensions={0} | all-to-all | bytes 196608 | tf_op jit(solution)/shard_map/all_to_all | solution.py:260
  116.2 0.7 reduce_sum.19
  (6 shorter events, 0.0 us)
Async XLA Ops:
  0.0 44.3 %copy-start.1 = (bf16[16,16,128]{2,1,0:T(8,128)(2,1)S(1)}, bf16[16,16,128]{2,1,0:T(8,128)(2,1)}, u32[]{:S(2)}) copy-start(bf16[16,16,128]{2,1,0:T(8,128)(2,1)} %gamma.1) | copy-start | bytes 196612
  4.3 45.5 %copy-start = (bf16[512,768]{1,0:T(8,128)(2,1)S(1)}, bf16[512,768]{1,0:T(8,128)(2,1)}, u32[]{:S(2)}) copy-start(bf16[512,768]{1,0:T(8,128)(2,1)} %here.1) | copy-start | bytes 2359300
  45.0 1.7 %collective-permute-start = (bf16[4,18,16,128]{3,2,1,0:T(8,128)(2,1)S(1)}, bf16[4,18,16,128]{3,2,1,0:T(8,128)(2,1)S(1)}, u32[]{:S(2)}, u32[]{:S(2)}) collective-permute-start(bf16[4,18,16,128]{3,2,1,0:T(8,128)(2,1)S(1)} %get-tuple-element.20), channel_id=1, source_target_pairs={{0,1},{1,0},{2,3},{3,2},{4,5},{5,4},{6,7},{7,6},{8,9},{9,8},{10,11... | collective-permute-start | bytes 884744 | tf_op jit(solution)/shard_map/ppermute | solution.py:228
  46.7 9.6 %collective-permute-start.1 = (bf16[2,18,16,128]{3,2,1,0:T(8,128)(2,1)S(1)}, bf16[2,18,16,128]{3,2,1,0:T(8,128)(2,1)S(1)}, u32[]{:S(2)}, u32[]{:S(2)}) collective-permute-start(bf16[2,18,16,128]{3,2,1,0:T(8,128)(2,1)S(1)} %get-tuple-element.22), channel_id=1, source_target_pairs={{0,2},{1,3},{2,4},{3,5},{4,6},{5,7},{6,0},{7,1},{8,10},{9,11},{10,... | collective-permute-start | bytes 442376 | tf_op jit(solution)/shard_map/ppermute | solution.py:237
  47.9 8.7 %collective-permute-start.2 = (bf16[2,18,16,128]{3,2,1,0:T(8,128)(2,1)S(1)}, bf16[2,18,16,128]{3,2,1,0:T(8,128)(2,1)S(1)}, u32[]{:S(2)}, u32[]{:S(2)}) collective-permute-start(bf16[2,18,16,128]{3,2,1,0:T(8,128)(2,1)S(1)} %get-tuple-element.23), channel_id=1, source_target_pairs={{0,4},{1,5},{2,6},{3,7},{4,0},{5,1},{6,2},{7,3},{8,12},{9,13},{10,... | collective-permute-start | bytes 442376 | tf_op jit(solution)/shard_map/ppermute | solution.py:237
  48.8 10.0 %collective-permute-start.3 = (bf16[2,18,16,128]{3,2,1,0:T(8,128)(2,1)S(1)}, bf16[2,18,16,128]{3,2,1,0:T(8,128)(2,1)S(1)}, u32[]{:S(2)}, u32[]{:S(2)}) collective-permute-start(bf16[2,18,16,128]{3,2,1,0:T(8,128)(2,1)S(1)} %get-tuple-element.24), channel_id=1, source_target_pairs={{0,6},{1,7},{2,0},{3,1},{4,2},{5,3},{6,4},{7,5},{8,14},{9,15},{10,... | collective-permute-start | bytes 442376 | tf_op jit(solution)/shard_map/ppermute | solution.py:237
  49.9 23.5 %collective-permute-start.5 = (bf16[512,768]{1,0:T(8,128)(2,1)S(1)}, bf16[512,768]{1,0:T(8,128)(2,1)S(1)}, u32[]{:S(2)}, u32[]{:S(2)}) collective-permute-start(bf16[512,768]{1,0:T(8,128)(2,1)S(1)} %copy-done), channel_id=1, source_target_pairs={{0,2},{1,3},{2,4},{3,5},{4,6},{5,7},{6,0},{7,1},{8,10},{9,11},{10,... | collective-permute-start | bytes 2359304 | tf_op jit(solution)/shard_map/ppermute | solution.py:181
  50.9 24.7 %collective-permute-start.6 = (bf16[512,768]{1,0:T(8,128)(2,1)S(1)}, bf16[512,768]{1,0:T(8,128)(2,1)S(1)}, u32[]{:S(2)}, u32[]{:S(2)}) collective-permute-start(bf16[512,768]{1,0:T(8,128)(2,1)S(1)} %copy-done), channel_id=1, source_target_pairs={{0,6},{1,7},{2,0},{3,1},{4,2},{5,3},{6,4},{7,5},{8,14},{9,15},{10,... | collective-permute-start | bytes 2359304 | tf_op jit(solution)/shard_map/ppermute | solution.py:182
  56.3 33.3 %collective-permute-start.7 = (bf16[512,768]{1,0:T(8,128)(2,1)S(1)}, bf16[512,768]{1,0:T(8,128)(2,1)}, u32[]{:S(2)}, u32[]{:S(2)}) collective-permute-start(bf16[512,768]{1,0:T(8,128)(2,1)S(1)} %copy-done), channel_id=1, source_target_pairs={{0,4},{1,5},{2,6},{3,7},{4,0},{5,1},{6,2},{7,3},{8,12},{9,13},{10,... | collective-permute-start | bytes 2359304 | tf_op jit(solution)/shard_map/ppermute | solution.py:183
  59.6 30.1 %collective-permute-start.4 = (f32[3,256,256]{2,1,0:T(8,128)S(1)}, f32[3,256,256]{2,1,0:T(8,128)}, u32[]{:S(2)}, u32[]{:S(2)}) collective-permute-start(f32[3,256,256]{2,1,0:T(8,128)S(1)} %pair.1.own), channel_id=1, source_target_pairs={{0,1},{1,0},{2,3},{3,2},{4,5},{5,4},{6,7},{7,6},{8,9},{9,8},{10,11... | collective-permute-start | bytes 2359304 | tf_op jit(solution)/shard_map/ppermute | solution.py:247
  92.5 5.0 %collective-permute-start.10 = (f32[1,768]{1,0:T(1,128)S(1)}, f32[1,768]{1,0:T(1,128)S(1)}, u32[]{:S(2)}, u32[]{:S(2)}) collective-permute-start(f32[1,768]{1,0:T(1,128)S(1)} %get-tuple-element.28), channel_id=1, source_target_pairs={{0,6},{1,7},{2,0},{3,1},{4,2},{5,3},{6,4},{7,5},{8,14},{9,15},{10,... | collective-permute-start | bytes 9224 | tf_op jit(solution)/shard_map/ppermute | solution.py:258
  95.9 3.6 %collective-permute-start.8 = (f32[1,768]{1,0:T(1,128)S(1)}, f32[1,768]{1,0:T(1,128)S(1)}, u32[]{:S(2)}, u32[]{:S(2)}) collective-permute-start(f32[1,768]{1,0:T(1,128)S(1)} %get-tuple-element.26), channel_id=1, source_target_pairs={{0,2},{1,3},{2,4},{3,5},{4,6},{5,7},{6,0},{7,1},{8,10},{9,11},{10,... | collective-permute-start | bytes 9224 | tf_op jit(solution)/shard_map/ppermute | solution.py:258
  95.9 5.1 %collective-permute-start.9 = (f32[1,768]{1,0:T(1,128)S(1)}, f32[1,768]{1,0:T(1,128)S(1)}, u32[]{:S(2)}, u32[]{:S(2)}) collective-permute-start(f32[1,768]{1,0:T(1,128)S(1)} %get-tuple-element.27), channel_id=1, source_target_pairs={{0,4},{1,5},{2,6},{3,7},{4,0},{5,1},{6,2},{7,3},{8,12},{9,13},{10,... | collective-permute-start | bytes 9224 | tf_op jit(solution)/shard_map/ppermute | solution.py:258

commit v6 on v4

--- a/solution.py
+++ b/solution.py
@@ -103,7 +103,7 @@
         out[p // 2, 4 * GROUPS + p % 2] = (gamma[p].astype(F32) * weight).astype(BF16)
 
 
-def pair_kernel(recv, out):
+def pair_kernel(recv, out, sent):
     def block(b):
         tiles = [recv[:, b * GROUPS + g].reshape(LANES, LANES) for g in range(GROUPS)]
         return jnp.concatenate(tiles, axis=1)
@@ -127,9 +127,11 @@
     right = jnp.dot(turned, other[:, WIDE:], preferred_element_type=F32)
     out[1] = 0.5 * right[:WIDE]
     out[2] = 0.25 * right[WIDE:]
-
-
-def form_kernel(own, other, here, left, right, far, slope, out):
+    for k in range(3):
+        sent[k] = out[k].astype(BF16)
+
+
+def form_kernel(own, other, here, left, right, far_top, far_low, slope, out):
     chip = lax.axis_index("scn") // 2
     v = slope[...]
     one = v.astype(BF16)
@@ -138,15 +140,15 @@
     v = v - two.astype(F32)
     fill = jnp.zeros((13, v.shape[1]), BF16)
     parts = jnp.concatenate([one, two, v.astype(BF16), fill], axis=0)
-    first = (own[0] + other[0]).astype(BF16)
-    cross = (own[1] + other[1]).astype(BF16)
-    last = (own[2] + other[2]).astype(BF16)
+    first = (own[0] + other[0].astype(F32)).astype(BF16)
+    cross = (own[1] + other[1].astype(F32)).astype(BF16)
+    last = (own[2] + other[2].astype(F32)).astype(BF16)
     top = jnp.concatenate([first, parts[:, :WIDE]], axis=0)
     low = jnp.concatenate([cross, parts[:, WIDE:], last], axis=0)
     extra = WIDE + parts.shape[0]
-    for step, group in enumerate((here, right, far, left)):
-        upper = group[:WIDE, :]
-        lower = group[WIDE:, :]
+    for step, group in enumerate((here, right, None, left)):
+        upper = far_top[...] if group is None else group[:WIDE, :]
+        lower = far_low[...] if group is None else group[WIDE:, :]
         image = jnp.dot(low, lower, preferred_element_type=F32)
         more = image[:extra] + jnp.dot(top, upper, preferred_element_type=F32)
         total = jnp.sum(more[:WIDE] * upper.astype(F32) + image[extra:] * lower.astype(F32), axis=0, keepdims=True)
@@ -162,7 +164,8 @@
     depth = loadings.shape[1]
     left = lax.ppermute(draws, "scn", ring(2))
     right = lax.ppermute(draws, "scn", ring(-2))
-    far = lax.ppermute(draws, "scn", ring(4))
+    far_top = lax.ppermute(left[: depth // 2], "scn", ring(2))
+    far_low = lax.ppermute(right[depth // 2 :], "scn", ring(-2))
     outgoing, table = pl.pallas_call(
         pick_kernel,
         out_shape=(
@@ -206,23 +209,23 @@
         name="regroup",
     )(table, near(arrived), gamma)
     pairs = lax.all_to_all(grouped, "scn", split_axis=0, concat_axis=0, tiled=True)
-    own = pl.pallas_call(
+    own, sent = pl.pallas_call(
         pair_kernel,
-        out_shape=pltpu.VMEM((3, WIDE, WIDE), F32),
+        out_shape=(pltpu.VMEM((3, WIDE, WIDE), F32), pltpu.VMEM((3, WIDE, WIDE), BF16)),
         in_specs=[VMEM],
-        out_specs=VMEM,
+        out_specs=(VMEM, VMEM),
         compiler_params=GRANT,
         name="pair",
     )(near(pairs))
-    other = lax.ppermute(own, "scn", [(i, i ^ 1) for i in range(PARTS)])
+    other = lax.ppermute(sent, "scn", [(i, i ^ 1) for i in range(PARTS)])
     spread = pl.pallas_call(
         form_kernel,
         out_shape=pltpu.VMEM((PARTS // 2, 1, columns), F32),
-        in_specs=[VMEM] * 7,
+        in_specs=[VMEM] * 8,
         out_specs=VMEM,
         compiler_params=GRANT,
         name="form",
-    )(near(own), near(other), draws, near(left), near(right), near(far), slope.reshape(1, depth))
+    )(near(own), near(other), draws, near(left), near(right), near(far_top), near(far_low), slope.reshape(1, depth))
     chips = [[c + 2 * x for x in range(PARTS // 2)] for c in range(2)]
     along = lax.all_to_all(
         spread, "scn", split_axis=0, concat_axis=0, tiled=True, axis_index_groups=chips

time: 121 us -> 97 us (0.80)
  blocking collectives: 63.5 us -> 22.7 us
  starting transfers between devices: 8.22 us -> 20.4 us
  local copies, waits for them, and re-layouts: 0.85 us -> 4.44 us
    all_to_all x1 -> x0, blocking collectives: 40 us -> none  [body(): lax.all_to_all(outgoing, 'fac', split_axis=0, concat_axis=0, tiled=True)]
    all_to_all x0 -> x1, waiting for transfers between devices: none -> 26.5 us  [body(): lax.all_to_all(outgoing, 'fac', split_axis=0, concat_axis=0, tiled=True)]
    ppermute x1, waiting for transfers between devices: 13.2 us -> 0.01 us  [body(): left = lax.ppermute(draws, 'scn', ring(2))]
    ppermute x2 -> x3, waiting for transfers between devices: 15.5 us -> 4.06 us  [the longest x1 3.13 us: body(): far_top = lax.ppermute(left[:depth // 2], 'scn', ring(2))]
    all_to_all x0 -> x1, starting transfers between devices: none -> 11.4 us  [body(): lax.all_to_all(outgoing, 'fac', split_axis=0, concat_axis=0, tiled=True)]
    unnamed x4 -> x8, local copies, waits for them, and re-layouts: 0.01 us -> 2.03 us
    slice x0 -> x2, local copies, waits for them, and re-layouts: none -> 1.58 us  [the longest x1 0.79 us: body(): far_low = lax.ppermute(right[depth // 2:], 'scn', ring(-2))]
    ppermute x1, waiting for transfers between devices: 1.36 us -> 0.01 us  [body(): right = lax.ppermute(draws, 'scn', ring(-2))]
  transfers between devices with their start and end apart: 5 -> 7, of which waited for: 4 -> 4; matrix products, arithmetic and copies ran while one was open for 2% -> 4% of each run, Pallas kernels for 1% -> 3%
where the time goes in v6:
time: 97 us; the launch traced here: 95.4 us
  waiting for transfers between devices  35.1 us (36%)
  blocking collectives  22.7 us (23%)
  starting transfers between devices  20.4 us (21%)
  Pallas kernels  10.3 us (11%)
  local copies, waits for them, and re-layouts  4.44 us (5%)
  other arithmetic  2.48 us (3%)
    all_to_all x1, waiting for transfers between devices, body(): lax.all_to_all(outgoing, 'fac', split_axis=0, concat_axis=0, tiled=True)  26.5 us
    all_to_all x1, blocking collectives, body(): every = lax.all_to_all(mine, 'fac', split_axis=0, concat_axis=0, tiled=True)  15.1 us
    all_to_all x1, starting transfers between devices, body(): lax.all_to_all(outgoing, 'fac', split_axis=0, concat_axis=0, tiled=True)  11.4 us
    all_to_all x1, blocking collectives, body(): lax.all_to_all(spread, 'scn', split_axis=0, concat_axis=0, tiled=True, ax...  7.55 us
    all_to_all x1, starting transfers between devices, body(): lax.all_to_all(grouped, 'scn', split_axis=0, concat_axis=0, tiled=True)  4.8 us
    pallas_call x1, Pallas kernels, body(): pl.pallas_call(pick_kernel, out_shape=(pltpu.VMEM((2 * OWNERS, SLICE, dep...  4.76 us
    all_to_all x1, waiting for transfers between devices, body(): lax.all_to_all(grouped, 'scn', split_axis=0, concat_axis=0, tiled=True)  4.55 us
    ppermute x1, waiting for transfers between devices, body(): far_top = lax.ppermute(left[:depth // 2], 'scn', ring(2))  3.13 us
  transfers between devices with their start and end apart: 7, of which 4 were waited for; matrix products, arithmetic and copies ran while one was open for 4% of the time, Pallas kernels for 3%

profile of v6, /device:TPU:4, one launch (start us, length us, event | category | flops | bytes accessed | tf_op | source)
XLA Modules:
  0.0 95.4 jit_solution(3084810376207209894)
XLA Ops:
  0.0 0.0 copy-start
  0.0 4.8 %pick.1 = (bf16[64,16,512]{2,1,0:T(8,128)(2,1)}, s32[48]{0:T(128)S(1)}) custom-call(s32[4,128]{1,0:T(4,128)} %bitcast.4, s32[4,128]{1,0:T(4,128)} %bitcast.5, s32[32]{0:T(128)} %count.1, bf16[6144,512]{1,0:T(8,128)(2,1)} %loadings.1), custom_call_target="tpu_custom_call" | custom-call | tf_op jit(solution)/shard_map/pick/pallas_call | solution.py:169
  4.8 11.4 %all-to-all-start = ((bf16[64,16,512]{2,1,0:T(8,128)(2,1)}), bf16[64,16,512]{2,1,0:T(8,128)(2,1)S(1)}, u32[]{:S(2)}, u32[]{:S(2)}) async-start(bf16[64,16,512]{2,1,0:T(8,128)(2,1)} %get-tuple-element.10), calls=%async_computation | async-start | bytes 2097152 | tf_op jit(solution)/shard_map/all_to_all | solution.py:197
  16.2 0.0 copy-done
  16.2 1.2 %collective-permute-start.1 = (bf16[512,768]{1,0:T(8,128)(2,1)S(1)}, bf16[512,768]{1,0:T(8,128)(2,1)S(1)}, u32[]{:S(2)}, u32[]{:S(2)}) collective-permute-start(bf16[512,768]{1,0:T(8,128)(2,1)S(1)} %copy-done), channel_id=1, source_target_pairs={{0,2},{1,3},{2,4},{3,5},{4,6},{5,7},{6,0},{7,1},{8,10},{9,11},{10,... | collective-permute-start | bytes 2359304 | tf_op jit(solution)/shard_map/ppermute | solution.py:165
  17.4 0.9 collective-permute-start.2
  18.3 26.5 %all-to-all-done.recv = bf16[64,16,512]{2,1,0:T(8,128)(2,1)S(1)} async-done(((bf16[64,16,512]{2,1,0:T(8,128)(2,1)}), bf16[64,16,512]{2,1,0:T(8,128)(2,1)S(1)}, u32[]{:S(2)}, u32[]{:S(2)}) %all-to-all-start) | async-done | bytes 1048608 | tf_op jit(solution)/shard_map/all_to_all | solution.py:197
  44.8 0.0 copy-done.3
  44.8 1.5 %regroup.1 = bf16[8,18,16,128]{3,2,1,0:T(8,128)(2,1)} custom-call(s32[48]{0:T(128)S(1)} %get-tuple-element.9.table, bf16[64,16,512]{2,1,0:T(8,128)(2,1)S(1)} %all-to-all-done.recv, bf16[16,16,128]{2,1,0:T(8,128)(2,1)S(1)} %copy-done.3), custom_call_target="tpu_custom_call" | custom-call | tf_op jit(solution)/shard_map/regroup/pallas_call | solution.py:203
  46.3 4.8 %all-to-all-start.1 = ((bf16[8,18,16,128]{3,2,1,0:T(8,128)(2,1)}), bf16[8,18,16,128]{3,2,1,0:T(8,128)(2,1)S(1)}, u32[]{:S(2)}, u32[]{:S(2)}) async-start(bf16[8,18,16,128]{3,2,1,0:T(8,128)(2,1)} %regroup.1), calls=%async_computation.1 | async-start | bytes 1179648 | tf_op jit(solution)/shard_map/all_to_all | solution.py:211
  51.1 0.0 collective-permute-done.1.left
  51.1 0.8 slice.8
  51.9 1.2 %collective-permute-start.3 = (bf16[256,768]{1,0:T(8,128)(2,1)}, bf16[256,768]{1,0:T(8,128)(2,1)S(1)}, u32[]{:S(2)}, u32[]{:S(2)}) collective-permute-start(bf16[256,768]{1,0:T(8,128)(2,1)} %slice.8), channel_id=1, source_target_pairs={{0,2},{1,3},{2,4},{3,5},{4,6},{5,7},{6,0},{7,1},{8,10},{9,11},{10,... | collective-permute-start | bytes 1179656 | tf_op jit(solution)/shard_map/ppermute | solution.py:167
  53.0 0.0 collective-permute-done.2.right
  53.0 0.8 slice.9
  53.8 0.9 collective-permute-start.4
  54.7 4.5 %all-to-all-done.1.recv = bf16[8,18,16,128]{3,2,1,0:T(8,128)(2,1)S(1)} async-done(((bf16[8,18,16,128]{3,2,1,0:T(8,128)(2,1)}), bf16[8,18,16,128]{3,2,1,0:T(8,128)(2,1)S(1)}, u32[]{:S(2)}, u32[]{:S(2)}) %all-to-all-start.1) | async-done | bytes 589856 | tf_op jit(solution)/shard_map/all_to_all | solution.py:211
  59.2 1.6 %pair.1 = (f32[3,256,256]{2,1,0:T(8,128)S(1)}, bf16[3,256,256]{2,1,0:T(8,128)(2,1)}) custom-call(bf16[8,18,16,128]{3,2,1,0:T(8,128)(2,1)S(1)} %all-to-all-done.1.recv), custom_call_target="tpu_custom_call" | custom-call | tf_op jit(solution)/shard_map/pair/pallas_call | solution.py:212
  60.8 0.0 copy-start.1
  60.8 0.9 copy-done.1
  61.7 0.0 collective-permute-start
  61.7 0.8 dynamic_slice.6
  62.5 1.8 %multiply_reduce_fusion = f32[512]{0:T(512)S(1)} fusion(bf16[6144,512]{1,0:T(8,128)(2,1)} %loadings.1, s32[]{:T(128)S(6)} %select_n.10, f32[1536]{0:T(1024)S(1)} %dynamic_slice.6), kind=kLoop, calls=%fused_computation | loop fusion | flops 2358784 | bytes 1581060 | tf_op jit(solution)/shard_map/reduce_sum | solution.py:202
  64.2 3.1 %collective-permute-done.3.far_top = bf16[256,768]{1,0:T(8,128)(2,1)S(1)} collective-permute-done((bf16[256,768]{1,0:T(8,128)(2,1)}, bf16[256,768]{1,0:T(8,128)(2,1)S(1)}, u32[]{:S(2)}, u32[]{:S(2)}) %collective-permute-start.3) | collective-permute-done | bytes 393248 | tf_op jit(solution)/shard_map/ppermute | solution.py:167
  67.4 0.9 collective-permute-done.4.far_low
  68.3 0.0 collective-permute-done.other
  68.3 1.1 %copy-done.2 = f32[3,256,256]{2,1,0:T(8,128)S(1)} copy-done((f32[3,256,256]{2,1,0:T(8,128)S(1)}, f32[3,256,256]{2,1,0:T(8,128)}, u32[]{:S(2)}) %copy-start.2) | copy-done | bytes 786456
  69.4 2.5 %form.1 = f32[4,1,768]{2,1,0:T(1,128)S(1)} custom-call(f32[3,256,256]{2,1,0:T(8,128)S(1)} %copy-done.2, bf16[3,256,256]{2,1,0:T(8,128)(2,1)S(1)} %collective-permute-done.other, bf16[512,768]{1,0:T(8,128)(2,1)S(1)} %copy-done, bf16[512,768]{1,0:T(8,128)(2,1)S(1)} %collective-permute-done.1.left, bf16[512,768]{1,0:T(8,128)(2,1)S(1)} %collective-permute-done.2.right, ...), custom_call_target="tpu_custom_call" | custom-call | tf_op jit(solution)/shard_map/form/pallas_call | solution.py:221
  72.0 7.5 %all_to_all.20 = f32[4,1,768]{2,1,0:T(1,128)S(1)} all-to-all(f32[4,1,768]{2,1,0:T(1,128)S(1)} %form.1), channel_id=1, replica_groups={{0,2,4,6},{1,3,5,7},{8,10,12,14},{9,11,13,15},{16,18,20,22},{17,19,21,2..., dimensions={0} | all-to-all | bytes 24576 | tf_op jit(solution)/shard_map/all_to_all | solution.py:230
  79.5 0.1 broadcast_in_dim.2
  79.6 15.1 %all_to_all.21 = f32[32,1,768]{2,1,0:T(1,128)S(1)} all-to-all(f32[32,1,768]{2,1,0:T(1,128)S(1)} %broadcast_in_dim.2), channel_id=1, replica_groups=mesh['fac'=32,'scn'=8] {'fac'}, dimensions={0} | all-to-all | bytes 196608 | tf_op jit(solution)/shard_map/all_to_all | solution.py:234
  94.7 0.7 reduce_sum.29
  (3 shorter events, 0.0 us)
Async XLA Ops:
  0.0 16.2 %copy-start = (bf16[512,768]{1,0:T(8,128)(2,1)S(1)}, bf16[512,768]{1,0:T(8,128)(2,1)}, u32[]{:S(2)}) copy-start(bf16[512,768]{1,0:T(8,128)(2,1)} %here.1) | copy-start | bytes 2359300
  0.0 44.8 %copy-start.3 = (bf16[16,16,128]{2,1,0:T(8,128)(2,1)S(1)}, bf16[16,16,128]{2,1,0:T(8,128)(2,1)}, u32[]{:S(2)}) copy-start(bf16[16,16,128]{2,1,0:T(8,128)(2,1)} %gamma.1) | copy-start | bytes 196612
  4.8 40.0 %all-to-all-start = ((bf16[64,16,512]{2,1,0:T(8,128)(2,1)}), bf16[64,16,512]{2,1,0:T(8,128)(2,1)S(1)}, u32[]{:S(2)}, u32[]{:S(2)}) async-start(bf16[64,16,512]{2,1,0:T(8,128)(2,1)} %get-tuple-element.10), calls=%async_computation | async-start | bytes 2097152 | tf_op jit(solution)/shard_map/all_to_all | solution.py:197
  16.2 34.9 %collective-permute-start.1 = (bf16[512,768]{1,0:T(8,128)(2,1)S(1)}, bf16[512,768]{1,0:T(8,128)(2,1)S(1)}, u32[]{:S(2)}, u32[]{:S(2)}) collective-permute-start(bf16[512,768]{1,0:T(8,128)(2,1)S(1)} %copy-done), channel_id=1, source_target_pairs={{0,2},{1,3},{2,4},{3,5},{4,6},{5,7},{6,0},{7,1},{8,10},{9,11},{10,... | collective-permute-start | bytes 2359304 | tf_op jit(solution)/shard_map/ppermute | solution.py:165
  17.4 35.6 %collective-permute-start.2 = (bf16[512,768]{1,0:T(8,128)(2,1)S(1)}, bf16[512,768]{1,0:T(8,128)(2,1)S(1)}, u32[]{:S(2)}, u32[]{:S(2)}) collective-permute-start(bf16[512,768]{1,0:T(8,128)(2,1)S(1)} %copy-done), channel_id=1, source_target_pairs={{0,6},{1,7},{2,0},{3,1},{4,2},{5,3},{6,4},{7,5},{8,14},{9,15},{10,... | collective-permute-start | bytes 2359304 | tf_op jit(solution)/shard_map/ppermute | solution.py:166
  46.3 13.0 %all-to-all-start.1 = ((bf16[8,18,16,128]{3,2,1,0:T(8,128)(2,1)}), bf16[8,18,16,128]{3,2,1,0:T(8,128)(2,1)S(1)}, u32[]{:S(2)}, u32[]{:S(2)}) async-start(bf16[8,18,16,128]{3,2,1,0:T(8,128)(2,1)} %regroup.1), calls=%async_computation.1 | async-start | bytes 1179648 | tf_op jit(solution)/shard_map/all_to_all | solution.py:211
  51.9 15.5 %collective-permute-start.3 = (bf16[256,768]{1,0:T(8,128)(2,1)}, bf16[256,768]{1,0:T(8,128)(2,1)S(1)}, u32[]{:S(2)}, u32[]{:S(2)}) collective-permute-start(bf16[256,768]{1,0:T(8,128)(2,1)} %slice.8), channel_id=1, source_target_pairs={{0,2},{1,3},{2,4},{3,5},{4,6},{5,7},{6,0},{7,1},{8,10},{9,11},{10,... | collective-permute-start | bytes 1179656 | tf_op jit(solution)/shard_map/ppermute | solution.py:167
  53.8 14.5 %collective-permute-start.4 = (bf16[256,768]{1,0:T(8,128)(2,1)}, bf16[256,768]{1,0:T(8,128)(2,1)}, u32[]{:S(2)}, u32[]{:S(2)}) collective-permute-start(bf16[256,768]{1,0:T(8,128)(2,1)} %slice.9), channel_id=1, source_target_pairs={{0,6},{1,7},{2,0},{3,1},{4,2},{5,3},{6,4},{7,5},{8,14},{9,15},{10,... | collective-permute-start | bytes 1179656 | tf_op jit(solution)/shard_map/ppermute | solution.py:168
  60.8 0.9 copy-start.1
  61.7 6.6 %collective-permute-start = (bf16[3,256,256]{2,1,0:T(8,128)(2,1)}, bf16[3,256,256]{2,1,0:T(8,128)(2,1)S(1)}, u32[]{:S(2)}, u32[]{:S(2)}) collective-permute-start(bf16[3,256,256]{2,1,0:T(8,128)(2,1)} %get-tuple-element.12), channel_id=1, source_target_pairs={{0,1},{1,0},{2,3},{3,2},{4,5},{5,4},{6,7},{7,6},{8,9},{9,8},{10,11... | collective-permute-start | bytes 1179656 | tf_op jit(solution)/shard_map/ppermute | solution.py:220
  68.3 1.1 %copy-start.2 = (f32[3,256,256]{2,1,0:T(8,128)S(1)}, f32[3,256,256]{2,1,0:T(8,128)}, u32[]{:S(2)}) copy-start(f32[3,256,256]{2,1,0:T(8,128)} %copy-done.1) | copy-start | bytes 2359300

commit v7 on v6

--- a/solution.py
+++ b/solution.py
@@ -131,7 +131,11 @@
         sent[k] = out[k].astype(BF16)
 
 
-def form_kernel(own, other, here, left, right, far_top, far_low, slope, out):
+def form_kernel(own, other, here, left, right, top_far, low_far, slope, out, far_top, far_low, sems):
+    first_half = pltpu.make_async_copy(top_far, far_top, sems.at[0])
+    second_half = pltpu.make_async_copy(low_far, far_low, sems.at[1])
+    first_half.start()
+    second_half.start()
     chip = lax.axis_index("scn") // 2
     v = slope[...]
     one = v.astype(BF16)
@@ -146,7 +150,10 @@
     top = jnp.concatenate([first, parts[:, :WIDE]], axis=0)
     low = jnp.concatenate([cross, parts[:, WIDE:], last], axis=0)
     extra = WIDE + parts.shape[0]
-    for step, group in enumerate((here, right, None, left)):
+    for step, group in ((0, here), (1, right), (3, left), (2, None)):
+        if group is None:
+            first_half.wait()
+            second_half.wait()
         upper = far_top[...] if group is None else group[:WIDE, :]
         lower = far_low[...] if group is None else group[WIDE:, :]
         image = jnp.dot(low, lower, preferred_element_type=F32)
@@ -221,11 +228,16 @@
     spread = pl.pallas_call(
         form_kernel,
         out_shape=pltpu.VMEM((PARTS // 2, 1, columns), F32),
-        in_specs=[VMEM] * 8,
+        in_specs=[VMEM] * 5 + [HBM, HBM, VMEM],
         out_specs=VMEM,
+        scratch_shapes=[
+            pltpu.VMEM((depth // 2, columns), BF16),
+            pltpu.VMEM((depth // 2, columns), BF16),
+            pltpu.SemaphoreType.DMA((2,)),
+        ],
         compiler_params=GRANT,
         name="form",
-    )(near(own), near(other), draws, near(left), near(right), near(far_top), near(far_low), slope.reshape(1, depth))
+    )(near(own), near(other), draws, near(left), near(right), away(far_top), away(far_low), slope.reshape(1, depth))
     chips = [[c + 2 * x for x in range(PARTS // 2)] for c in range(2)]
     along = lax.all_to_all(
         spread, "scn", split_axis=0, concat_axis=0, tiled=True, axis_index_groups=chips

time: 97 us -> 96.8 us (level)
  Pallas kernels: 10.3 us -> 9.31 us
  transfers between devices with their start and end apart: 7 -> 7, of which waited for: 4 -> 4; matrix products, arithmetic and copies ran while one was open for 4% -> 4% of each run, Pallas kernels for 3% -> 2%
where the time goes in v7:
time: 96.8 us; the launch traced here: 95.2 us
  waiting for transfers between devices  35.9 us (37%)
  blocking collectives  22.6 us (23%)
  starting transfers between devices  20.4 us (21%)
  Pallas kernels  9.31 us (10%)
  local copies, waits for them, and re-layouts  4.46 us (5%)
  other arithmetic  2.48 us (3%)
    all_to_all x1, waiting for transfers between devices, body(): lax.all_to_all(outgoing, 'fac', split_axis=0, concat_axis=0, tiled=True)  26.5 us
    all_to_all x1, blocking collectives, body(): every = lax.all_to_all(mine, 'fac', split_axis=0, concat_axis=0, tiled=True)  15.1 us
    all_to_all x1, starting transfers between devices, body(): lax.all_to_all(outgoing, 'fac', split_axis=0, concat_axis=0, tiled=True)  11.4 us
    all_to_all x1, blocking collectives, body(): lax.all_to_all(spread, 'scn', split_axis=0, concat_axis=0, tiled=True, ax...  7.55 us
    all_to_all x1, starting transfers between devices, body(): lax.all_to_all(grouped, 'scn', split_axis=0, concat_axis=0, tiled=True)  4.8 us
    pallas_call x1, Pallas kernels, body(): pl.pallas_call(pick_kernel, out_shape=(pltpu.VMEM((2 * OWNERS, SLICE, dep...  4.76 us
    all_to_all x1, waiting for transfers between devices, body(): lax.all_to_all(grouped, 'scn', split_axis=0, concat_axis=0, tiled=True)  4.53 us
    ppermute x1, waiting for transfers between devices, body(): far_top = lax.ppermute(left[:depth // 2], 'scn', ring(2))  4.01 us
  transfers between devices with their start and end apart: 7, of which 4 were waited for; matrix products, arithmetic and copies ran while one was open for 4% of the time, Pallas kernels for 2%

profile of v7, /device:TPU:4, one launch (start us, length us, event | category | flops | bytes accessed | tf_op | source)
XLA Modules:
  0.0 95.2 jit_solution(13134324862830950923)
XLA Ops:
  0.0 0.0 copy-start
  0.0 4.8 %pick.1 = (bf16[64,16,512]{2,1,0:T(8,128)(2,1)}, s32[48]{0:T(128)S(1)}) custom-call(s32[4,128]{1,0:T(4,128)} %bitcast.4, s32[4,128]{1,0:T(4,128)} %bitcast.5, s32[32]{0:T(128)} %count.1, bf16[6144,512]{1,0:T(8,128)(2,1)} %loadings.1), custom_call_target="tpu_custom_call" | custom-call | tf_op jit(solution)/shard_map/pick/pallas_call | solution.py:176
  4.8 11.4 %all-to-all-start = ((bf16[64,16,512]{2,1,0:T(8,128)(2,1)}), bf16[64,16,512]{2,1,0:T(8,128)(2,1)S(1)}, u32[]{:S(2)}, u32[]{:S(2)}) async-start(bf16[64,16,512]{2,1,0:T(8,128)(2,1)} %get-tuple-element.10), calls=%async_computation | async-start | bytes 2097152 | tf_op jit(solution)/shard_map/all_to_all | solution.py:204
  16.2 0.0 copy-done
  16.2 1.2 %collective-permute-start.1 = (bf16[512,768]{1,0:T(8,128)(2,1)S(1)}, bf16[512,768]{1,0:T(8,128)(2,1)S(1)}, u32[]{:S(2)}, u32[]{:S(2)}) collective-permute-start(bf16[512,768]{1,0:T(8,128)(2,1)S(1)} %copy-done), channel_id=1, source_target_pairs={{0,2},{1,3},{2,4},{3,5},{4,6},{5,7},{6,0},{7,1},{8,10},{9,11},{10,... | collective-permute-start | bytes 2359304 | tf_op jit(solution)/shard_map/ppermute | solution.py:172
  17.4 0.9 collective-permute-start.2
  18.3 26.5 %all-to-all-done.recv = bf16[64,16,512]{2,1,0:T(8,128)(2,1)S(1)} async-done(((bf16[64,16,512]{2,1,0:T(8,128)(2,1)}), bf16[64,16,512]{2,1,0:T(8,128)(2,1)S(1)}, u32[]{:S(2)}, u32[]{:S(2)}) %all-to-all-start) | async-done | bytes 1048608 | tf_op jit(solution)/shard_map/all_to_all | solution.py:204
  44.8 0.0 copy-done.3
  44.8 1.5 %regroup.1 = bf16[8,18,16,128]{3,2,1,0:T(8,128)(2,1)} custom-call(s32[48]{0:T(128)S(1)} %get-tuple-element.9.table, bf16[64,16,512]{2,1,0:T(8,128)(2,1)S(1)} %all-to-all-done.recv, bf16[16,16,128]{2,1,0:T(8,128)(2,1)S(1)} %copy-done.3), custom_call_target="tpu_custom_call" | custom-call | tf_op jit(solution)/shard_map/regroup/pallas_call | solution.py:210
  46.3 4.8 %all-to-all-start.1 = ((bf16[8,18,16,128]{3,2,1,0:T(8,128)(2,1)}), bf16[8,18,16,128]{3,2,1,0:T(8,128)(2,1)S(1)}, u32[]{:S(2)}, u32[]{:S(2)}) async-start(bf16[8,18,16,128]{3,2,1,0:T(8,128)(2,1)} %regroup.1), calls=%async_computation.1 | async-start | bytes 1179648 | tf_op jit(solution)/shard_map/all_to_all | solution.py:218
  51.1 0.0 collective-permute-done.1.left
  51.1 0.8 slice.8
  51.9 1.2 %collective-permute-start.3 = (bf16[256,768]{1,0:T(8,128)(2,1)}, bf16[256,768]{1,0:T(8,128)(2,1)}, u32[]{:S(2)}, u32[]{:S(2)}) collective-permute-start(bf16[256,768]{1,0:T(8,128)(2,1)} %slice.8), channel_id=1, source_target_pairs={{0,2},{1,3},{2,4},{3,5},{4,6},{5,7},{6,0},{7,1},{8,10},{9,11},{10,... | collective-permute-start | bytes 1179656 | tf_op jit(solution)/shard_map/ppermute | solution.py:174
  53.0 0.0 collective-permute-done.2.right
  53.0 0.8 slice.9
  53.8 0.9 collective-permute-start.4
  54.7 4.5 %all-to-all-done.1.recv = bf16[8,18,16,128]{3,2,1,0:T(8,128)(2,1)S(1)} async-done(((bf16[8,18,16,128]{3,2,1,0:T(8,128)(2,1)}), bf16[8,18,16,128]{3,2,1,0:T(8,128)(2,1)S(1)}, u32[]{:S(2)}, u32[]{:S(2)}) %all-to-all-start.1) | async-done | bytes 589856 | tf_op jit(solution)/shard_map/all_to_all | solution.py:218
  59.2 0.8 pair.1
  60.0 0.0 copy-start.1
  60.0 0.9 copy-done.1
  60.9 0.0 collective-permute-start
  60.9 0.8 dynamic_slice.6
  61.7 1.8 %multiply_reduce_fusion = f32[512]{0:T(512)S(1)} fusion(bf16[6144,512]{1,0:T(8,128)(2,1)} %loadings.1, s32[]{:T(128)S(6)} %select_n.10, f32[1536]{0:T(1024)S(1)} %dynamic_slice.6), kind=kLoop, calls=%fused_computation | loop fusion | flops 2358784 | bytes 1581060 | tf_op jit(solution)/shard_map/reduce_sum | solution.py:209
  63.5 4.0 %collective-permute-done.3.top_far = bf16[256,768]{1,0:T(8,128)(2,1)} collective-permute-done((bf16[256,768]{1,0:T(8,128)(2,1)}, bf16[256,768]{1,0:T(8,128)(2,1)}, u32[]{:S(2)}, u32[]{:S(2)}) %collective-permute-start.3) | collective-permute-done | bytes 393248 | tf_op jit(solution)/shard_map/ppermute | solution.py:174
  67.5 0.8 collective-permute-done.4.low_far
  68.3 0.0 collective-permute-done.other
  68.3 1.1 %copy-done.2 = f32[3,256,256]{2,1,0:T(8,128)S(1)} copy-done((f32[3,256,256]{2,1,0:T(8,128)S(1)}, f32[3,256,256]{2,1,0:T(8,128)}, u32[]{:S(2)}) %copy-start.2) | copy-done | bytes 786456
  69.4 2.3 %form.1 = f32[4,1,768]{2,1,0:T(1,128)S(1)} custom-call(f32[3,256,256]{2,1,0:T(8,128)S(1)} %copy-done.2, bf16[3,256,256]{2,1,0:T(8,128)(2,1)S(1)} %collective-permute-done.other, bf16[512,768]{1,0:T(8,128)(2,1)S(1)} %copy-done, bf16[512,768]{1,0:T(8,128)(2,1)S(1)} %collective-permute-done.1.left, bf16[512,768]{1,0:T(8,128)(2,1)S(1)} %collective-permute-done.2.right, ...), custom_call_target="tpu_custom_call" | custom-call | tf_op jit(solution)/shard_map/form/pallas_call | solution.py:228
  71.8 7.5 %all_to_all.20 = f32[4,1,768]{2,1,0:T(1,128)S(1)} all-to-all(f32[4,1,768]{2,1,0:T(1,128)S(1)} %form.1), channel_id=1, replica_groups={{0,2,4,6},{1,3,5,7},{8,10,12,14},{9,11,13,15},{16,18,20,22},{17,19,21,2..., dimensions={0} | all-to-all | bytes 24576 | tf_op jit(solution)/shard_map/all_to_all | solution.py:242
  79.4 0.1 broadcast_in_dim.2
  79.4 15.1 %all_to_all.21 = f32[32,1,768]{2,1,0:T(1,128)S(1)} all-to-all(f32[32,1,768]{2,1,0:T(1,128)S(1)} %broadcast_in_dim.2), channel_id=1, replica_groups=mesh['fac'=32,'scn'=8] {'fac'}, dimensions={0} | all-to-all | bytes 196608 | tf_op jit(solution)/shard_map/all_to_all | solution.py:246
  94.5 0.7 reduce_sum.29
  (3 shorter events, 0.0 us)
Async XLA Ops:
  0.0 16.2 %copy-start = (bf16[512,768]{1,0:T(8,128)(2,1)S(1)}, bf16[512,768]{1,0:T(8,128)(2,1)}, u32[]{:S(2)}) copy-start(bf16[512,768]{1,0:T(8,128)(2,1)} %here.1) | copy-start | bytes 2359300
  0.0 44.8 %copy-start.3 = (bf16[16,16,128]{2,1,0:T(8,128)(2,1)S(1)}, bf16[16,16,128]{2,1,0:T(8,128)(2,1)}, u32[]{:S(2)}) copy-start(bf16[16,16,128]{2,1,0:T(8,128)(2,1)} %gamma.1) | copy-start | bytes 196612
  4.8 40.0 %all-to-all-start = ((bf16[64,16,512]{2,1,0:T(8,128)(2,1)}), bf16[64,16,512]{2,1,0:T(8,128)(2,1)S(1)}, u32[]{:S(2)}, u32[]{:S(2)}) async-start(bf16[64,16,512]{2,1,0:T(8,128)(2,1)} %get-tuple-element.10), calls=%async_computation | async-start | bytes 2097152 | tf_op jit(solution)/shard_map/all_to_all | solution.py:204
  16.2 34.9 %collective-permute-start.1 = (bf16[512,768]{1,0:T(8,128)(2,1)S(1)}, bf16[512,768]{1,0:T(8,128)(2,1)S(1)}, u32[]{:S(2)}, u32[]{:S(2)}) collective-permute-start(bf16[512,768]{1,0:T(8,128)(2,1)S(1)} %copy-done), channel_id=1, source_target_pairs={{0,2},{1,3},{2,4},{3,5},{4,6},{5,7},{6,0},{7,1},{8,10},{9,11},{10,... | collective-permute-start | bytes 2359304 | tf_op jit(solution)/shard_map/ppermute | solution.py:172
  17.4 35.6 %collective-permute-start.2 = (bf16[512,768]{1,0:T(8,128)(2,1)S(1)}, bf16[512,768]{1,0:T(8,128)(2,1)S(1)}, u32[]{:S(2)}, u32[]{:S(2)}) collective-permute-start(bf16[512,768]{1,0:T(8,128)(2,1)S(1)} %copy-done), channel_id=1, source_target_pairs={{0,6},{1,7},{2,0},{3,1},{4,2},{5,3},{6,4},{7,5},{8,14},{9,15},{10,... | collective-permute-start | bytes 2359304 | tf_op jit(solution)/shard_map/ppermute | solution.py:173
  46.3 13.0 %all-to-all-start.1 = ((bf16[8,18,16,128]{3,2,1,0:T(8,128)(2,1)}), bf16[8,18,16,128]{3,2,1,0:T(8,128)(2,1)S(1)}, u32[]{:S(2)}, u32[]{:S(2)}) async-start(bf16[8,18,16,128]{3,2,1,0:T(8,128)(2,1)} %regroup.1), calls=%async_computation.1 | async-start | bytes 1179648 | tf_op jit(solution)/shard_map/all_to_all | solution.py:218
  51.9 15.6 %collective-permute-start.3 = (bf16[256,768]{1,0:T(8,128)(2,1)}, bf16[256,768]{1,0:T(8,128)(2,1)}, u32[]{:S(2)}, u32[]{:S(2)}) collective-permute-start(bf16[256,768]{1,0:T(8,128)(2,1)} %slice.8), channel_id=1, source_target_pairs={{0,2},{1,3},{2,4},{3,5},{4,6},{5,7},{6,0},{7,1},{8,10},{9,11},{10,... | collective-permute-start | bytes 1179656 | tf_op jit(solution)/shard_map/ppermute | solution.py:174
  53.8 14.5 %collective-permute-start.4 = (bf16[256,768]{1,0:T(8,128)(2,1)}, bf16[256,768]{1,0:T(8,128)(2,1)}, u32[]{:S(2)}, u32[]{:S(2)}) collective-permute-start(bf16[256,768]{1,0:T(8,128)(2,1)} %slice.9), channel_id=1, source_target_pairs={{0,6},{1,7},{2,0},{3,1},{4,2},{5,3},{6,4},{7,5},{8,14},{9,15},{10,... | collective-permute-start | bytes 1179656 | tf_op jit(solution)/shard_map/ppermute | solution.py:175
  60.0 0.9 copy-start.1
  60.9 7.4 %collective-permute-start = (bf16[3,256,256]{2,1,0:T(8,128)(2,1)S(1)}, bf16[3,256,256]{2,1,0:T(8,128)(2,1)S(1)}, u32[]{:S(2)}, u32[]{:S(2)}) collective-permute-start(bf16[3,256,256]{2,1,0:T(8,128)(2,1)S(1)} %get-tuple-element.12), channel_id=1, source_target_pairs={{0,1},{1,0},{2,3},{3,2},{4,5},{5,4},{6,7},{7,6},{8,9},{9,8},{10,11... | collective-permute-start | bytes 1179656 | tf_op jit(solution)/shard_map/ppermute | solution.py:227
  68.3 1.1 %copy-start.2 = (f32[3,256,256]{2,1,0:T(8,128)S(1)}, f32[3,256,256]{2,1,0:T(8,128)}, u32[]{:S(2)}) copy-start(f32[3,256,256]{2,1,0:T(8,128)} %copy-done.1) | copy-start | bytes 2359300

commit v8 on v7

--- a/solution.py
+++ b/solution.py
@@ -131,7 +131,9 @@
         sent[k] = out[k].astype(BF16)
 
 
-def form_kernel(own, other, here, left, right, top_far, low_far, slope, out, far_top, far_low, sems):
+def form_kernel(
+    own, other, here, left_top, left_low, right_top, right_low, top_far, low_far, slope, out, far_top, far_low, sems
+):
     first_half = pltpu.make_async_copy(top_far, far_top, sems.at[0])
     second_half = pltpu.make_async_copy(low_far, far_low, sems.at[1])
     first_half.start()
@@ -150,12 +152,14 @@
     top = jnp.concatenate([first, parts[:, :WIDE]], axis=0)
     low = jnp.concatenate([cross, parts[:, WIDE:], last], axis=0)
     extra = WIDE + parts.shape[0]
-    for step, group in ((0, here), (1, right), (3, left), (2, None)):
-        if group is None:
+    whole = (here.at[:WIDE, :], here.at[WIDE:, :])
+    groups = ((0, whole), (1, (right_top, right_low)), (3, (left_top, left_low)), (2, (far_top, far_low)))
+    for step, halves in groups:
+        if step == 2:
             first_half.wait()
             second_half.wait()
-        upper = far_top[...] if group is None else group[:WIDE, :]
-        lower = far_low[...] if group is None else group[WIDE:, :]
+        upper = halves[0][...]
+        lower = halves[1][...]
         image = jnp.dot(low, lower, preferred_element_type=F32)
         more = image[:extra] + jnp.dot(top, upper, preferred_element_type=F32)
         total = jnp.sum(more[:WIDE] * upper.astype(F32) + image[extra:] * lower.astype(F32), axis=0, keepdims=True)
@@ -169,10 +173,13 @@
 def body(loadings, draws, delta, gamma, pair_rows, pair_cols, pair_count):
     columns = draws.shape[1]
     depth = loadings.shape[1]
-    left = lax.ppermute(draws, "scn", ring(2))
-    right = lax.ppermute(draws, "scn", ring(-2))
-    far_top = lax.ppermute(left[: depth // 2], "scn", ring(2))
-    far_low = lax.ppermute(right[depth // 2 :], "scn", ring(-2))
+    upper, lower = draws[: depth // 2], draws[depth // 2 :]
+    left_top = lax.ppermute(upper, "scn", ring(2))
+    right_low = lax.ppermute(lower, "scn", ring(-2))
+    left_low = lax.ppermute(lower, "scn", ring(2))
+    right_top = lax.ppermute(upper, "scn", ring(-2))
+    far_top = lax.ppermute(left_top, "scn", ring(2))
+    far_low = lax.ppermute(right_low, "scn", ring(-2))
     outgoing, table = pl.pallas_call(
         pick_kernel,
         out_shape=(
@@ -228,7 +235,7 @@
     spread = pl.pallas_call(
         form_kernel,
         out_shape=pltpu.VMEM((PARTS // 2, 1, columns), F32),
-        in_specs=[VMEM] * 5 + [HBM, HBM, VMEM],
+        in_specs=[VMEM] * 7 + [HBM, HBM, VMEM],
         out_specs=VMEM,
         scratch_shapes=[
             pltpu.VMEM((depth // 2, columns), BF16),
@@ -237,7 +244,7 @@
         ],
         compiler_params=GRANT,
         name="form",
-    )(near(own), near(other), draws, near(left), near(right), away(far_top), away(far_low), slope.reshape(1, depth))
+    )(near(own), near(other), draws, near(left_top), near(left_low), near(right_top), near(right_low), away(far_top), away(far_low), slope.reshape(1, depth))
     chips = [[c + 2 * x for x in range(PARTS // 2)] for c in range(2)]
     along = lax.all_to_all(
         spread, "scn", split_axis=0, concat_axis=0, tiled=True, axis_index_groups=chips

time: 96.8 us -> 113 us (1.17)
  blocking collectives: 22.6 us -> 62.6 us
  waiting for transfers between devices: 35.9 us -> 23 us
  starting transfers between devices: 20.4 us -> 10.9 us
  local copies, waits for them, and re-layouts: 4.46 us -> 1.78 us
  Pallas kernels: 9.31 us -> 10.5 us
    all_to_all x0 -> x1, blocking collectives: none -> 40 us  [body(): lax.all_to_all(outgoing, 'fac', split_axis=0, concat_axis=0, tiled=True)]
    all_to_all x1 -> x0, waiting for transfers between devices: 26.5 us -> none  [body(): lax.all_to_all(outgoing, 'fac', split_axis=0, concat_axis=0, tiled=True)]
    ppermute x4 -> x6, waiting for transfers between devices: 4.84 us -> 23 us  [the longest x1 11.6 us: body(): left_top = lax.ppermute(upper, 'scn', ring(2))]
    all_to_all x1 -> x0, starting transfers between devices: 11.4 us -> none  [body(): lax.all_to_all(outgoing, 'fac', split_axis=0, concat_axis=0, tiled=True)]
    all_to_all x1, waiting for transfers between devices: 4.53 us -> 0.01 us  [body(): lax.all_to_all(grouped, 'scn', split_axis=0, concat_axis=0, tiled=True)]
    unnamed x8 -> x4, local copies, waits for them, and re-layouts: 2.03 us -> 0.01 us
    ppermute x4 -> x6, starting transfers between devices: 4.13 us -> 6.08 us  [the longest x1 1.98 us: body(): far_top = lax.ppermute(left_top, 'scn', ring(2))]
  transfers between devices with their start and end apart: 7 -> 8, of which waited for: 4 -> 5; matrix products, arithmetic and copies ran while one was open for 4% -> 3% of each run, Pallas kernels for 2% -> 1%
where the time goes in v8:
time: 113 us; the launch traced here: 111 us
  blocking collectives  62.6 us (55%)
  waiting for transfers between devices  23 us (20%)
  starting transfers between devices  10.9 us (10%)
  Pallas kernels  10.5 us (9%)
  other arithmetic  2.48 us (2%)
  local copies, waits for them, and re-layouts  1.78 us (2%)
    all_to_all x1, blocking collectives, body(): lax.all_to_all(outgoing, 'fac', split_axis=0, concat_axis=0, tiled=True)  40 us
    all_to_all x1, blocking collectives, body(): every = lax.all_to_all(mine, 'fac', split_axis=0, concat_axis=0, tiled=True)  15.1 us
    ppermute x1, waiting for transfers between devices, body(): left_top = lax.ppermute(upper, 'scn', ring(2))  11.6 us
    all_to_all x1, blocking collectives, body(): lax.all_to_all(spread, 'scn', split_axis=0, concat_axis=0, tiled=True, ax...  7.55 us
    ppermute x1, waiting for transfers between devices, body(): far_top = lax.ppermute(left_top, 'scn', ring(2))  7.03 us
    all_to_all x1, starting transfers between devices, body(): lax.all_to_all(grouped, 'scn', split_axis=0, concat_axis=0, tiled=True)  4.8 us
    pallas_call x1, Pallas kernels, body(): pl.pallas_call(pick_kernel, out_shape=(pltpu.VMEM((2 * OWNERS, SLICE, dep...  4.32 us
    pallas_call x1, Pallas kernels, body(): pl.pallas_call(form_kernel, out_shape=pltpu.VMEM((PARTS // 2, 1, columns)...  3.24 us
  transfers between devices with their start and end apart: 8, of which 5 were waited for; matrix products, arithmetic and copies ran while one was open for 3% of the time, Pallas kernels for 1%

profile of v8, /device:TPU:4, one launch (start us, length us, event | category | flops | bytes accessed | tf_op | source)
XLA Modules:
  0.0 111.3 jit_solution(16022105710876572596)
XLA Ops:
  0.0 0.0 copy-start.1
  0.0 4.3 %pick.1 = (bf16[64,16,512]{2,1,0:T(8,128)(2,1)S(1)}, s32[48]{0:T(128)S(1)}) custom-call(s32[4,128]{1,0:T(4,128)} %bitcast.4, s32[4,128]{1,0:T(4,128)} %bitcast.5, s32[32]{0:T(128)} %count.1, bf16[6144,512]{1,0:T(8,128)(2,1)} %loadings.1), custom_call_target="tpu_custom_call" | custom-call | tf_op jit(solution)/shard_map/pick/pallas_call | solution.py:183
  4.3 0.0 copy-start
  4.3 40.0 %all_to_all.20.recv = bf16[64,16,512]{2,1,0:T(8,128)(2,1)S(1)} all-to-all(bf16[64,16,512]{2,1,0:T(8,128)(2,1)S(1)} %get-tuple-element.10), channel_id=1, replica_groups=mesh['fac'=32,'scn'=8] {'fac'}, dimensions={0} | all-to-all | bytes 2097152 | tf_op jit(solution)/shard_map/all_to_all | solution.py:211
  44.3 0.0 copy-done.1
  44.3 1.5 %regroup.1 = bf16[8,18,16,128]{3,2,1,0:T(8,128)(2,1)} custom-call(s32[48]{0:T(128)S(1)} %get-tuple-element.9.table, bf16[64,16,512]{2,1,0:T(8,128)(2,1)S(1)} %all_to_all.20.recv, bf16[16,16,128]{2,1,0:T(8,128)(2,1)S(1)} %copy-done.1), custom_call_target="tpu_custom_call" | custom-call | tf_op jit(solution)/shard_map/regroup/pallas_call | solution.py:217
  45.8 4.8 %all-to-all-start.1 = ((bf16[8,18,16,128]{3,2,1,0:T(8,128)(2,1)}), bf16[8,18,16,128]{3,2,1,0:T(8,128)(2,1)S(1)}, u32[]{:S(2)}, u32[]{:S(2)}) async-start(bf16[8,18,16,128]{3,2,1,0:T(8,128)(2,1)} %regroup.1), calls=%async_computation.1 | async-start | bytes 1179648 | tf_op jit(solution)/shard_map/all_to_all | solution.py:225
  50.6 0.0 copy-done
  50.6 0.9 fusion
  51.5 1.2 %collective-permute-start.1 = (bf16[256,768]{1,0:T(8,128)(2,1)}, bf16[256,768]{1,0:T(8,128)(2,1)S(1)}, u32[]{:S(2)}, u32[]{:S(2)}) collective-permute-start(bf16[256,768]{1,0:T(8,128)(2,1)} %get-tuple-element.14), channel_id=1, source_target_pairs={{0,2},{1,3},{2,4},{3,5},{4,6},{5,7},{6,0},{7,1},{8,10},{9,11},{10,... | collective-permute-start | bytes 1179656 | tf_op jit(solution)/shard_map/ppermute | solution.py:177
  52.7 0.9 collective-permute-start.4
  53.5 1.2 %collective-permute-start.2 = (bf16[256,768]{1,0:T(8,128)(2,1)}, bf16[256,768]{1,0:T(8,128)(2,1)S(1)}, u32[]{:S(2)}, u32[]{:S(2)}) collective-permute-start(bf16[256,768]{1,0:T(8,128)(2,1)} %get-tuple-element.13), channel_id=1, source_target_pairs={{0,2},{1,3},{2,4},{3,5},{4,6},{5,7},{6,0},{7,1},{8,10},{9,11},{10,... | collective-permute-start | bytes 1179656 | tf_op jit(solution)/shard_map/ppermute | solution.py:179
  54.7 0.9 collective-permute-start.3
  55.6 11.6 %collective-permute-done.1.left_top = bf16[256,768]{1,0:T(8,128)(2,1)S(1)} collective-permute-done((bf16[256,768]{1,0:T(8,128)(2,1)}, bf16[256,768]{1,0:T(8,128)(2,1)S(1)}, u32[]{:S(2)}, u32[]{:S(2)}) %collective-permute-start.1) | collective-permute-done | bytes 393248 | tf_op jit(solution)/shard_map/ppermute | solution.py:177
  67.1 2.0 %collective-permute-start.5 = (bf16[256,768]{1,0:T(8,128)(2,1)S(1)}, bf16[256,768]{1,0:T(8,128)(2,1)}, u32[]{:S(2)}, u32[]{:S(2)}) collective-permute-start(bf16[256,768]{1,0:T(8,128)(2,1)S(1)} %collective-permute-done.1.left_top), channel_id=1, source_target_pairs={{0,2},{1,3},{2,4},{3,5},{4,6},{5,7},{6,0},{7,1},{8,10},{9,11},{10,... | collective-permute-start | bytes 1179656 | tf_op jit(solution)/shard_map/ppermute | solution.py:181
  69.1 0.0 collective-permute-done.4.right_low
  69.1 0.0 collective-permute-start.6
  69.2 0.0 all-to-all-done.1.recv
  69.2 1.5 %pair.1 = (f32[3,256,256]{2,1,0:T(8,128)S(1)}, bf16[3,256,256]{2,1,0:T(8,128)(2,1)}) custom-call(bf16[8,18,16,128]{3,2,1,0:T(8,128)(2,1)S(1)} %all-to-all-done.1.recv), custom_call_target="tpu_custom_call" | custom-call | tf_op jit(solution)/shard_map/pair/pallas_call | solution.py:226
  70.7 0.0 collective-permute-start
  70.7 0.8 dynamic_slice.6
  71.5 1.8 %multiply_reduce_fusion = f32[512]{0:T(512)S(1)} fusion(bf16[6144,512]{1,0:T(8,128)(2,1)} %loadings.1, s32[]{:T(128)S(6)} %select_n.10, f32[1536]{0:T(1024)S(1)} %dynamic_slice.6), kind=kLoop, calls=%fused_computation | loop fusion | flops 2358784 | bytes 1581060 | tf_op jit(solution)/shard_map/reduce_sum | solution.py:216
  73.3 2.3 %collective-permute-done.2.left_low = bf16[256,768]{1,0:T(8,128)(2,1)S(1)} collective-permute-done((bf16[256,768]{1,0:T(8,128)(2,1)}, bf16[256,768]{1,0:T(8,128)(2,1)S(1)}, u32[]{:S(2)}, u32[]{:S(2)}) %collective-permute-start.2) | collective-permute-done | bytes 393248 | tf_op jit(solution)/shard_map/ppermute | solution.py:179
  75.6 1.2 %collective-permute-done.3.right_top = bf16[256,768]{1,0:T(8,128)(2,1)} collective-permute-done((bf16[256,768]{1,0:T(8,128)(2,1)}, bf16[256,768]{1,0:T(8,128)(2,1)}, u32[]{:S(2)}, u32[]{:S(2)}) %collective-permute-start.3) | collective-permute-done | bytes 393248 | tf_op jit(solution)/shard_map/ppermute | solution.py:180
  76.8 7.0 %collective-permute-done.5.top_far = bf16[256,768]{1,0:T(8,128)(2,1)} collective-permute-done((bf16[256,768]{1,0:T(8,128)(2,1)S(1)}, bf16[256,768]{1,0:T(8,128)(2,1)}, u32[]{:S(2)}, u32[]{:S(2)}) %collective-permute-start.5) | collective-permute-done | bytes 393248 | tf_op jit(solution)/shard_map/ppermute | solution.py:181
  83.8 0.8 collective-permute-done.6.low_far
  84.7 0.0 collective-permute-done.other
  84.7 3.2 %form.1 = f32[4,1,768]{2,1,0:T(1,128)S(1)} custom-call(f32[3,256,256]{2,1,0:T(8,128)S(1)} %get-tuple-element.11.own, bf16[3,256,256]{2,1,0:T(8,128)(2,1)S(1)} %collective-permute-done.other, bf16[512,768]{1,0:T(8,128)(2,1)S(1)} %copy-done, bf16[256,768]{1,0:T(8,128)(2,1)S(1)} %collective-permute-done.1.left_top, ...), custom_call_target="tpu_custom_call" | custom-call | tf_op jit(solution)/shard_map/form/pallas_call | solution.py:235
  87.9 7.5 %all_to_all.21 = f32[4,1,768]{2,1,0:T(1,128)S(1)} all-to-all(f32[4,1,768]{2,1,0:T(1,128)S(1)} %form.1), channel_id=1, replica_groups={{0,2,4,6},{1,3,5,7},{8,10,12,14},{9,11,13,15},{16,18,20,22},{17,19,21,2..., dimensions={0} | all-to-all | bytes 24576 | tf_op jit(solution)/shard_map/all_to_all | solution.py:249
  95.5 0.1 broadcast_in_dim.2
  95.5 15.1 %all_to_all.22 = f32[32,1,768]{2,1,0:T(1,128)S(1)} all-to-all(f32[32,1,768]{2,1,0:T(1,128)S(1)} %broadcast_in_dim.2), channel_id=1, replica_groups=mesh['fac'=32,'scn'=8] {'fac'}, dimensions={0} | all-to-all | bytes 196608 | tf_op jit(solution)/shard_map/all_to_all | solution.py:253
  110.6 0.7 reduce_sum.29
  (1 shorter events, 0.0 us)
Async XLA Ops:
  0.0 44.3 %copy-start.1 = (bf16[16,16,128]{2,1,0:T(8,128)(2,1)S(1)}, bf16[16,16,128]{2,1,0:T(8,128)(2,1)}, u32[]{:S(2)}) copy-start(bf16[16,16,128]{2,1,0:T(8,128)(2,1)} %gamma.1) | copy-start | bytes 196612
  4.3 46.2 %copy-start = (bf16[512,768]{1,0:T(8,128)(2,1)S(1)}, bf16[512,768]{1,0:T(8,128)(2,1)}, u32[]{:S(2)}) copy-start(bf16[512,768]{1,0:T(8,128)(2,1)} %here.1) | copy-start | bytes 2359300
  45.8 23.4 %all-to-all-start.1 = ((bf16[8,18,16,128]{3,2,1,0:T(8,128)(2,1)}), bf16[8,18,16,128]{3,2,1,0:T(8,128)(2,1)S(1)}, u32[]{:S(2)}, u32[]{:S(2)}) async-start(bf16[8,18,16,128]{3,2,1,0:T(8,128)(2,1)} %regroup.1), calls=%async_computation.1 | async-start | bytes 1179648 | tf_op jit(solution)/shard_map/all_to_all | solution.py:225
  51.5 15.6 %collective-permute-start.1 = (bf16[256,768]{1,0:T(8,128)(2,1)}, bf16[256,768]{1,0:T(8,128)(2,1)S(1)}, u32[]{:S(2)}, u32[]{:S(2)}) collective-permute-start(bf16[256,768]{1,0:T(8,128)(2,1)} %get-tuple-element.14), channel_id=1, source_target_pairs={{0,2},{1,3},{2,4},{3,5},{4,6},{5,7},{6,0},{7,1},{8,10},{9,11},{10,... | collective-permute-start | bytes 1179656 | tf_op jit(solution)/shard_map/ppermute | solution.py:177
  52.7 16.5 %collective-permute-start.4 = (bf16[256,768]{1,0:T(8,128)(2,1)}, bf16[256,768]{1,0:T(8,128)(2,1)S(1)}, u32[]{:S(2)}, u32[]{:S(2)}) collective-permute-start(bf16[256,768]{1,0:T(8,128)(2,1)} %get-tuple-element.13), channel_id=1, source_target_pairs={{0,6},{1,7},{2,0},{3,1},{4,2},{5,3},{6,4},{7,5},{8,14},{9,15},{10,... | collective-permute-start | bytes 1179656 | tf_op jit(solution)/shard_map/ppermute | solution.py:178
  53.5 22.0 %collective-permute-start.2 = (bf16[256,768]{1,0:T(8,128)(2,1)}, bf16[256,768]{1,0:T(8,128)(2,1)S(1)}, u32[]{:S(2)}, u32[]{:S(2)}) collective-permute-start(bf16[256,768]{1,0:T(8,128)(2,1)} %get-tuple-element.13), channel_id=1, source_target_pairs={{0,2},{1,3},{2,4},{3,5},{4,6},{5,7},{6,0},{7,1},{8,10},{9,11},{10,... | collective-permute-start | bytes 1179656 | tf_op jit(solution)/shard_map/ppermute | solution.py:179
  54.7 22.1 %collective-permute-start.3 = (bf16[256,768]{1,0:T(8,128)(2,1)}, bf16[256,768]{1,0:T(8,128)(2,1)}, u32[]{:S(2)}, u32[]{:S(2)}) collective-permute-start(bf16[256,768]{1,0:T(8,128)(2,1)} %get-tuple-element.14), channel_id=1, source_target_pairs={{0,6},{1,7},{2,0},{3,1},{4,2},{5,3},{6,4},{7,5},{8,14},{9,15},{10,... | collective-permute-start | bytes 1179656 | tf_op jit(solution)/shard_map/ppermute | solution.py:180
  67.1 16.7 %collective-permute-start.5 = (bf16[256,768]{1,0:T(8,128)(2,1)S(1)}, bf16[256,768]{1,0:T(8,128)(2,1)}, u32[]{:S(2)}, u32[]{:S(2)}) collective-permute-start(bf16[256,768]{1,0:T(8,128)(2,1)S(1)} %collective-permute-done.1.left_top), channel_id=1, source_target_pairs={{0,2},{1,3},{2,4},{3,5},{4,6},{5,7},{6,0},{7,1},{8,10},{9,11},{10,... | collective-permute-start | bytes 1179656 | tf_op jit(solution)/shard_map/ppermute | solution.py:181
  69.1 15.5 %collective-permute-start.6 = (bf16[256,768]{1,0:T(8,128)(2,1)S(1)}, bf16[256,768]{1,0:T(8,128)(2,1)}, u32[]{:S(2)}, u32[]{:S(2)}) collective-permute-start(bf16[256,768]{1,0:T(8,128)(2,1)S(1)} %collective-permute-done.4.right_low), channel_id=1, source_target_pairs={{0,6},{1,7},{2,0},{3,1},{4,2},{5,3},{6,4},{7,5},{8,14},{9,15},{10,... | collective-permute-start | bytes 1179656 | tf_op jit(solution)/shard_map/ppermute | solution.py:182
  70.7 14.0 %collective-permute-start = (bf16[3,256,256]{2,1,0:T(8,128)(2,1)}, bf16[3,256,256]{2,1,0:T(8,128)(2,1)S(1)}, u32[]{:S(2)}, u32[]{:S(2)}) collective-permute-start(bf16[3,256,256]{2,1,0:T(8,128)(2,1)} %get-tuple-element.12), channel_id=1, source_target_pairs={{0,1},{1,0},{2,3},{3,2},{4,5},{5,4},{6,7},{7,6},{8,9},{9,8},{10,11... | collective-permute-start | bytes 1179656 | tf_op jit(solution)/shard_map/ppermute | solution.py:234

commit v9 on v8

--- a/solution.py
+++ b/solution.py
@@ -36,7 +36,7 @@
 
 def pick_kernel(
     rows, cols, count, loadings, out, table,
-    rows_v, cols_v, rows_s, cols_s, count_s, keys_v, keys_s, seen, sems, small,
+    rows_v, cols_v, rows_s, cols_s, count_s, seen, sems, small,
 ):
     me = lax.axis_index("fac")
     part = lax.axis_index("scn")
@@ -59,10 +59,6 @@
     keys = jnp.concatenate([jnp.minimum(low_r, low_c), jnp.minimum(high_r, high_c)], axis=0)
     for shift in (1, 2, 4, 8):
         keys = jnp.minimum(keys, pltpu.roll(keys, LANES - shift, 1))
-    keys_v[...] = keys
-    copy = pltpu.make_async_copy(keys_v, keys_s, small.at[5])
-    copy.start()
-    copy.wait()
 
     def fetch(slot, offset):
         start = pl.multiple_of(offset * LANES + part * SLICE, SLICE)
@@ -70,8 +66,8 @@
 
     for o in range(OWNERS):
         row, col = o // 8, (o % 8) * CAP
-        fetch(2 * o, jnp.minimum(keys_s[row, col] & 63, BLOCKS_DEV - 1)).start()
-        fetch(2 * o + 1, jnp.minimum((-keys_s[4 + row, col]) & 63, BLOCKS_DEV - 1)).start()
+        fetch(2 * o, jnp.minimum(keys[row, col] & 63, BLOCKS_DEV - 1)).start()
+        fetch(2 * o + 1, jnp.minimum((-keys[4 + row, col]) & 63, BLOCKS_DEV - 1)).start()
     for move in moves[2:]:
         move.wait()
     for h in range(OWNERS):
@@ -194,11 +190,9 @@
             pltpu.SMEM((4, LANES), jnp.int32),
             pltpu.SMEM((4, LANES), jnp.int32),
             pltpu.SMEM((OWNERS,), jnp.int32),
-            pltpu.VMEM((8, LANES), jnp.int32),
-            pltpu.SMEM((8, LANES), jnp.int32),
             pltpu.SMEM((OWNERS,), jnp.int32),
             pltpu.SemaphoreType.DMA((2 * OWNERS,)),
-            pltpu.SemaphoreType.DMA((6,)),
+            pltpu.SemaphoreType.DMA((5,)),
         ],
         compiler_params=GRANT,
         name="pick",

time: 113 us -> 112 us (level)
  no operation moved by 1% of the time
where the time goes in v9:
time: 112 us; the launch traced here: 111 us
  blocking collectives  62.5 us (56%)
  waiting for transfers between devices  23 us (21%)
  starting transfers between devices  10.9 us (10%)
  Pallas kernels  10 us (9%)
  other arithmetic  2.48 us (2%)
  local copies, waits for them, and re-layouts  1.78 us (2%)
    all_to_all x1, blocking collectives, body(): lax.all_to_all(outgoing, 'fac', split_axis=0, concat_axis=0, tiled=True)  39.9 us
    all_to_all x1, blocking collectives, body(): every = lax.all_to_all(mine, 'fac', split_axis=0, concat_axis=0, tiled=True)  15 us
    ppermute x1, waiting for transfers between devices, body(): left_top = lax.ppermute(upper, 'scn', ring(2))  11.6 us
    all_to_all x1, blocking collectives, body(): lax.all_to_all(spread, 'scn', split_axis=0, concat_axis=0, tiled=True, ax...  7.55 us
    ppermute x1, waiting for transfers between devices, body(): far_top = lax.ppermute(left_top, 'scn', ring(2))  7.03 us
    all_to_all x1, starting transfers between devices, body(): lax.all_to_all(grouped, 'scn', split_axis=0, concat_axis=0, tiled=True)  4.8 us
    pallas_call x1, Pallas kernels, body(): pl.pallas_call(pick_kernel, out_shape=(pltpu.VMEM((2 * OWNERS, SLICE, dep...  3.82 us
    pallas_call x1, Pallas kernels, body(): pl.pallas_call(form_kernel, out_shape=pltpu.VMEM((PARTS // 2, 1, columns)...  3.24 us
  transfers between devices with their start and end apart: 8, of which 5 were waited for; matrix products, arithmetic and copies ran while one was open for 3% of the time, Pallas kernels for 1%

profile of v9, /device:TPU:4, one launch (start us, length us, event | category | flops | bytes accessed | tf_op | source)
XLA Modules:
  0.0 110.7 jit_solution(9175725461207066877)
XLA Ops:
  0.0 0.0 copy-start.1
  0.0 3.8 %pick.1 = (bf16[64,16,512]{2,1,0:T(8,128)(2,1)S(1)}, s32[48]{0:T(128)S(1)}) custom-call(s32[4,128]{1,0:T(4,128)} %bitcast.4, s32[4,128]{1,0:T(4,128)} %bitcast.5, s32[32]{0:T(128)} %count.1, bf16[6144,512]{1,0:T(8,128)(2,1)} %loadings.1), custom_call_target="tpu_custom_call" | custom-call | tf_op jit(solution)/shard_map/pick/pallas_call | solution.py:179
  3.8 0.0 copy-start
  3.8 39.9 %all_to_all.20.recv = bf16[64,16,512]{2,1,0:T(8,128)(2,1)S(1)} all-to-all(bf16[64,16,512]{2,1,0:T(8,128)(2,1)S(1)} %get-tuple-element.10), channel_id=1, replica_groups=mesh['fac'=32,'scn'=8] {'fac'}, dimensions={0} | all-to-all | bytes 2097152 | tf_op jit(solution)/shard_map/all_to_all | solution.py:205
  43.8 0.0 copy-done.1
  43.8 1.5 %regroup.1 = bf16[8,18,16,128]{3,2,1,0:T(8,128)(2,1)} custom-call(s32[48]{0:T(128)S(1)} %get-tuple-element.9.table, bf16[64,16,512]{2,1,0:T(8,128)(2,1)S(1)} %all_to_all.20.recv, bf16[16,16,128]{2,1,0:T(8,128)(2,1)S(1)} %copy-done.1), custom_call_target="tpu_custom_call" | custom-call | tf_op jit(solution)/shard_map/regroup/pallas_call | solution.py:211
  45.2 4.8 %all-to-all-start.1 = ((bf16[8,18,16,128]{3,2,1,0:T(8,128)(2,1)}), bf16[8,18,16,128]{3,2,1,0:T(8,128)(2,1)S(1)}, u32[]{:S(2)}, u32[]{:S(2)}) async-start(bf16[8,18,16,128]{3,2,1,0:T(8,128)(2,1)} %regroup.1), calls=%async_computation.1 | async-start | bytes 1179648 | tf_op jit(solution)/shard_map/all_to_all | solution.py:219
  50.0 0.0 copy-done
  50.0 0.9 fusion
  51.0 1.2 %collective-permute-start.1 = (bf16[256,768]{1,0:T(8,128)(2,1)}, bf16[256,768]{1,0:T(8,128)(2,1)S(1)}, u32[]{:S(2)}, u32[]{:S(2)}) collective-permute-start(bf16[256,768]{1,0:T(8,128)(2,1)} %get-tuple-element.14), channel_id=1, source_target_pairs={{0,2},{1,3},{2,4},{3,5},{4,6},{5,7},{6,0},{7,1},{8,10},{9,11},{10,... | collective-permute-start | bytes 1179656 | tf_op jit(solution)/shard_map/ppermute | solution.py:173
  52.1 0.9 collective-permute-start.4
  53.0 1.2 %collective-permute-start.2 = (bf16[256,768]{1,0:T(8,128)(2,1)}, bf16[256,768]{1,0:T(8,128)(2,1)S(1)}, u32[]{:S(2)}, u32[]{:S(2)}) collective-permute-start(bf16[256,768]{1,0:T(8,128)(2,1)} %get-tuple-element.13), channel_id=1, source_target_pairs={{0,2},{1,3},{2,4},{3,5},{4,6},{5,7},{6,0},{7,1},{8,10},{9,11},{10,... | collective-permute-start | bytes 1179656 | tf_op jit(solution)/shard_map/ppermute | solution.py:175
  54.2 0.9 collective-permute-start.3
  55.0 11.6 %collective-permute-done.1.left_top = bf16[256,768]{1,0:T(8,128)(2,1)S(1)} collective-permute-done((bf16[256,768]{1,0:T(8,128)(2,1)}, bf16[256,768]{1,0:T(8,128)(2,1)S(1)}, u32[]{:S(2)}, u32[]{:S(2)}) %collective-permute-start.1) | collective-permute-done | bytes 393248 | tf_op jit(solution)/shard_map/ppermute | solution.py:173
  66.6 2.0 %collective-permute-start.5 = (bf16[256,768]{1,0:T(8,128)(2,1)S(1)}, bf16[256,768]{1,0:T(8,128)(2,1)}, u32[]{:S(2)}, u32[]{:S(2)}) collective-permute-start(bf16[256,768]{1,0:T(8,128)(2,1)S(1)} %collective-permute-done.1.left_top), channel_id=1, source_target_pairs={{0,2},{1,3},{2,4},{3,5},{4,6},{5,7},{6,0},{7,1},{8,10},{9,11},{10,... | collective-permute-start | bytes 1179656 | tf_op jit(solution)/shard_map/ppermute | solution.py:177
  68.6 0.0 collective-permute-done.4.right_low
  68.6 0.0 collective-permute-start.6
  68.6 0.0 all-to-all-done.1.recv
  68.7 1.5 %pair.1 = (f32[3,256,256]{2,1,0:T(8,128)S(1)}, bf16[3,256,256]{2,1,0:T(8,128)(2,1)}) custom-call(bf16[8,18,16,128]{3,2,1,0:T(8,128)(2,1)S(1)} %all-to-all-done.1.recv), custom_call_target="tpu_custom_call" | custom-call | tf_op jit(solution)/shard_map/pair/pallas_call | solution.py:220
  70.2 0.0 collective-permute-start
  70.2 0.8 dynamic_slice.6
  71.0 1.8 %multiply_reduce_fusion = f32[512]{0:T(512)S(1)} fusion(bf16[6144,512]{1,0:T(8,128)(2,1)} %loadings.1, s32[]{:T(128)S(6)} %select_n.10, f32[1536]{0:T(1024)S(1)} %dynamic_slice.6), kind=kLoop, calls=%fused_computation | loop fusion | flops 2358784 | bytes 1581060 | tf_op jit(solution)/shard_map/reduce_sum | solution.py:210
  72.7 2.3 %collective-permute-done.2.left_low = bf16[256,768]{1,0:T(8,128)(2,1)S(1)} collective-permute-done((bf16[256,768]{1,0:T(8,128)(2,1)}, bf16[256,768]{1,0:T(8,128)(2,1)S(1)}, u32[]{:S(2)}, u32[]{:S(2)}) %collective-permute-start.2) | collective-permute-done | bytes 393248 | tf_op jit(solution)/shard_map/ppermute | solution.py:175
  75.0 1.2 %collective-permute-done.3.right_top = bf16[256,768]{1,0:T(8,128)(2,1)} collective-permute-done((bf16[256,768]{1,0:T(8,128)(2,1)}, bf16[256,768]{1,0:T(8,128)(2,1)}, u32[]{:S(2)}, u32[]{:S(2)}) %collective-permute-start.3) | collective-permute-done | bytes 393248 | tf_op jit(solution)/shard_map/ppermute | solution.py:176
  76.3 7.0 %collective-permute-done.5.top_far = bf16[256,768]{1,0:T(8,128)(2,1)} collective-permute-done((bf16[256,768]{1,0:T(8,128)(2,1)S(1)}, bf16[256,768]{1,0:T(8,128)(2,1)}, u32[]{:S(2)}, u32[]{:S(2)}) %collective-permute-start.5) | collective-permute-done | bytes 393248 | tf_op jit(solution)/shard_map/ppermute | solution.py:177
  83.3 0.8 collective-permute-done.6.low_far
  84.1 0.0 collective-permute-done.other
  84.1 3.2 %form.1 = f32[4,1,768]{2,1,0:T(1,128)S(1)} custom-call(f32[3,256,256]{2,1,0:T(8,128)S(1)} %get-tuple-element.11.own, bf16[3,256,256]{2,1,0:T(8,128)(2,1)S(1)} %collective-permute-done.other, bf16[512,768]{1,0:T(8,128)(2,1)S(1)} %copy-done, bf16[256,768]{1,0:T(8,128)(2,1)S(1)} %collective-permute-done.1.left_top, ...), custom_call_target="tpu_custom_call" | custom-call | tf_op jit(solution)/shard_map/form/pallas_call | solution.py:229
  87.4 7.5 %all_to_all.21 = f32[4,1,768]{2,1,0:T(1,128)S(1)} all-to-all(f32[4,1,768]{2,1,0:T(1,128)S(1)} %form.1), channel_id=1, replica_groups={{0,2,4,6},{1,3,5,7},{8,10,12,14},{9,11,13,15},{16,18,20,22},{17,19,21,2..., dimensions={0} | all-to-all | bytes 24576 | tf_op jit(solution)/shard_map/all_to_all | solution.py:243
  94.9 0.1 broadcast_in_dim.2
  95.0 15.0 %all_to_all.22 = f32[32,1,768]{2,1,0:T(1,128)S(1)} all-to-all(f32[32,1,768]{2,1,0:T(1,128)S(1)} %broadcast_in_dim.2), channel_id=1, replica_groups=mesh['fac'=32,'scn'=8] {'fac'}, dimensions={0} | all-to-all | bytes 196608 | tf_op jit(solution)/shard_map/all_to_all | solution.py:247
  110.1 0.7 reduce_sum.29
  (1 shorter events, 0.0 us)
Async XLA Ops:
  0.0 43.8 %copy-start.1 = (bf16[16,16,128]{2,1,0:T(8,128)(2,1)S(1)}, bf16[16,16,128]{2,1,0:T(8,128)(2,1)}, u32[]{:S(2)}) copy-start(bf16[16,16,128]{2,1,0:T(8,128)(2,1)} %gamma.1) | copy-start | bytes 196612
  3.8 46.2 %copy-start = (bf16[512,768]{1,0:T(8,128)(2,1)S(1)}, bf16[512,768]{1,0:T(8,128)(2,1)}, u32[]{:S(2)}) copy-start(bf16[512,768]{1,0:T(8,128)(2,1)} %here.1) | copy-start | bytes 2359300
  45.2 23.4 %all-to-all-start.1 = ((bf16[8,18,16,128]{3,2,1,0:T(8,128)(2,1)}), bf16[8,18,16,128]{3,2,1,0:T(8,128)(2,1)S(1)}, u32[]{:S(2)}, u32[]{:S(2)}) async-start(bf16[8,18,16,128]{3,2,1,0:T(8,128)(2,1)} %regroup.1), calls=%async_computation.1 | async-start | bytes 1179648 | tf_op jit(solution)/shard_map/all_to_all | solution.py:219
  51.0 15.6 %collective-permute-start.1 = (bf16[256,768]{1,0:T(8,128)(2,1)}, bf16[256,768]{1,0:T(8,128)(2,1)S(1)}, u32[]{:S(2)}, u32[]{:S(2)}) collective-permute-start(bf16[256,768]{1,0:T(8,128)(2,1)} %get-tuple-element.14), channel_id=1, source_target_pairs={{0,2},{1,3},{2,4},{3,5},{4,6},{5,7},{6,0},{7,1},{8,10},{9,11},{10,... | collective-permute-start | bytes 1179656 | tf_op jit(solution)/shard_map/ppermute | solution.py:173
  52.1 16.5 %collective-permute-start.4 = (bf16[256,768]{1,0:T(8,128)(2,1)}, bf16[256,768]{1,0:T(8,128)(2,1)S(1)}, u32[]{:S(2)}, u32[]{:S(2)}) collective-permute-start(bf16[256,768]{1,0:T(8,128)(2,1)} %get-tuple-element.13), channel_id=1, source_target_pairs={{0,6},{1,7},{2,0},{3,1},{4,2},{5,3},{6,4},{7,5},{8,14},{9,15},{10,... | collective-permute-start | bytes 1179656 | tf_op jit(solution)/shard_map/ppermute | solution.py:174
  53.0 22.0 %collective-permute-start.2 = (bf16[256,768]{1,0:T(8,128)(2,1)}, bf16[256,768]{1,0:T(8,128)(2,1)S(1)}, u32[]{:S(2)}, u32[]{:S(2)}) collective-permute-start(bf16[256,768]{1,0:T(8,128)(2,1)} %get-tuple-element.13), channel_id=1, source_target_pairs={{0,2},{1,3},{2,4},{3,5},{4,6},{5,7},{6,0},{7,1},{8,10},{9,11},{10,... | collective-permute-start | bytes 1179656 | tf_op jit(solution)/shard_map/ppermute | solution.py:175
  54.2 22.1 %collective-permute-start.3 = (bf16[256,768]{1,0:T(8,128)(2,1)}, bf16[256,768]{1,0:T(8,128)(2,1)}, u32[]{:S(2)}, u32[]{:S(2)}) collective-permute-start(bf16[256,768]{1,0:T(8,128)(2,1)} %get-tuple-element.14), channel_id=1, source_target_pairs={{0,6},{1,7},{2,0},{3,1},{4,2},{5,3},{6,4},{7,5},{8,14},{9,15},{10,... | collective-permute-start | bytes 1179656 | tf_op jit(solution)/shard_map/ppermute | solution.py:176
  66.6 16.7 %collective-permute-start.5 = (bf16[256,768]{1,0:T(8,128)(2,1)S(1)}, bf16[256,768]{1,0:T(8,128)(2,1)}, u32[]{:S(2)}, u32[]{:S(2)}) collective-permute-start(bf16[256,768]{1,0:T(8,128)(2,1)S(1)} %collective-permute-done.1.left_top), channel_id=1, source_target_pairs={{0,2},{1,3},{2,4},{3,5},{4,6},{5,7},{6,0},{7,1},{8,10},{9,11},{10,... | collective-permute-start | bytes 1179656 | tf_op jit(solution)/shard_map/ppermute | solution.py:177
  68.6 15.5 %collective-permute-start.6 = (bf16[256,768]{1,0:T(8,128)(2,1)S(1)}, bf16[256,768]{1,0:T(8,128)(2,1)}, u32[]{:S(2)}, u32[]{:S(2)}) collective-permute-start(bf16[256,768]{1,0:T(8,128)(2,1)S(1)} %collective-permute-done.4.right_low), channel_id=1, source_target_pairs={{0,6},{1,7},{2,0},{3,1},{4,2},{5,3},{6,4},{7,5},{8,14},{9,15},{10,... | collective-permute-start | bytes 1179656 | tf_op jit(solution)/shard_map/ppermute | solution.py:178
  70.2 14.0 %collective-permute-start = (bf16[3,256,256]{2,1,0:T(8,128)(2,1)}, bf16[3,256,256]{2,1,0:T(8,128)(2,1)S(1)}, u32[]{:S(2)}, u32[]{:S(2)}) collective-permute-start(bf16[3,256,256]{2,1,0:T(8,128)(2,1)} %get-tuple-element.12), channel_id=1, source_target_pairs={{0,1},{1,0},{2,3},{3,2},{4,5},{5,4},{6,7},{7,6},{8,9},{9,8},{10,11... | collective-permute-start | bytes 1179656 | tf_op jit(solution)/shard_map/ppermute | solution.py:228

commit v10 on v9

--- a/solution.py
+++ b/solution.py
@@ -128,7 +128,8 @@
 
 
 def form_kernel(
-    own, other, here, left_top, left_low, right_top, right_low, top_far, low_far, slope, out, far_top, far_low, sems
+    own, other, here, left_top, left_low, right_top, right_low, top_far, low_far, slope,
+    mine, across, sent, out, far_top, far_low, sems,
 ):
     first_half = pltpu.make_async_copy(top_far, far_top, sems.at[0])
     second_half = pltpu.make_async_copy(low_far, far_low, sems.at[1])
@@ -159,7 +160,14 @@
         image = jnp.dot(low, lower, preferred_element_type=F32)
         more = image[:extra] + jnp.dot(top, upper, preferred_element_type=F32)
         total = jnp.sum(more[:WIDE] * upper.astype(F32) + image[extra:] * lower.astype(F32), axis=0, keepdims=True)
-        out[(chip + step) & 3] = total + jnp.sum(more[WIDE:], axis=0, keepdims=True)
+        group = (chip + step) & 3
+        beside = group == (chip ^ 1)
+        place = jnp.where(group == 3 - chip, 1, jnp.where(beside, 2, 3)) if step else 0
+        out[place] = total + jnp.sum(more[WIDE:], axis=0, keepdims=True)
+    mine[...] = out[0]
+    across[...] = out[1]
+    sent[0] = out[2]
+    sent[1] = out[3]
 
 
 def ring(step):
@@ -226,12 +234,17 @@
         name="pair",
     )(near(pairs))
     other = lax.ppermute(sent, "scn", [(i, i ^ 1) for i in range(PARTS)])
-    spread = pl.pallas_call(
+    mine, across, send = pl.pallas_call(
         form_kernel,
-        out_shape=pltpu.VMEM((PARTS // 2, 1, columns), F32),
+        out_shape=(
+            pltpu.VMEM((1, columns), F32),
+            pltpu.VMEM((1, columns), F32),
+            pltpu.VMEM((2, 1, columns), F32),
+        ),
         in_specs=[VMEM] * 7 + [HBM, HBM, VMEM],
-        out_specs=VMEM,
+        out_specs=(VMEM, VMEM, VMEM),
         scratch_shapes=[
+            pltpu.VMEM((4, 1, columns), F32),
             pltpu.VMEM((depth // 2, columns), BF16),
             pltpu.VMEM((depth // 2, columns), BF16),
             pltpu.SemaphoreType.DMA((2,)),
@@ -239,12 +252,12 @@
         compiler_params=GRANT,
         name="form",
     )(near(own), near(other), draws, near(left_top), near(left_low), near(right_top), near(right_low), away(far_top), away(far_low), slope.reshape(1, depth))
-    chips = [[c + 2 * x for x in range(PARTS // 2)] for c in range(2)]
-    along = lax.all_to_all(
-        spread, "scn", split_axis=0, concat_axis=0, tiled=True, axis_index_groups=chips
-    )
-    mine = jnp.broadcast_to(jnp.sum(along, axis=0)[None], (OWNERS, 1, columns))
-    every = lax.all_to_all(mine, "fac", split_axis=0, concat_axis=0, tiled=True)
+    near_sum = lax.ppermute(send, "scn", [(i, i ^ 2) for i in range(PARTS)])
+    across = across + near_sum[1]
+    over = lax.ppermute(across, "scn", [(i, 6 - i + 2 * (i % 2)) for i in range(PARTS)])
+    total = mine + near_sum[0] + over
+    spread = jnp.broadcast_to(total[None], (OWNERS, 1, columns))
+    every = lax.all_to_all(spread, "fac", split_axis=0, concat_axis=0, tiled=True)
     return jnp.sum(every, axis=0).reshape(-1)
 
 

time: 112 us -> 113 us (level)
  the two profiles are of different devices: /device:TPU:4 before, /device:TPU:32 now
where the time goes in v10:
time: 113 us
  blocking collectives  54.2 us (48%)
  waiting for transfers between devices  28.6 us (25%)
  starting transfers between devices  15.2 us (13%)
  Pallas kernels  10.2 us (9%)
  other arithmetic  2.48 us (2%)
  local copies, waits for them, and re-layouts  1.77 us (2%)
    all_to_all x1, blocking collectives, body(): lax.all_to_all(outgoing, 'fac', split_axis=0, concat_axis=0, tiled=True)  39.8 us
    all_to_all x1, blocking collectives, body(): lax.all_to_all(spread, 'fac', split_axis=0, concat_axis=0, tiled=True)  14.5 us
    ppermute x1, waiting for transfers between devices, body(): left_top = lax.ppermute(upper, 'scn', ring(2))  12.1 us
    ppermute x1, waiting for transfers between devices, body(): far_top = lax.ppermute(left_top, 'scn', ring(2))  8.14 us
    all_to_all x1, starting transfers between devices, body(): lax.all_to_all(grouped, 'scn', split_axis=0, concat_axis=0, tiled=True)  4.27 us
    ppermute x1, waiting for transfers between devices, body(): lax.ppermute(across, 'scn', [(i, 6 - i + 2 * (i % 2)) for i in range(PART...  3.89 us
    pallas_call x1, Pallas kernels, body(): pl.pallas_call(pick_kernel, out_shape=(pltpu.VMEM((2 * OWNERS, SLICE, dep...  3.76 us
    pallas_call x1, Pallas kernels, body(): pl.pallas_call(form_kernel, out_shape=(pltpu.VMEM((1, columns), F32), plt...  3.48 us
  transfers between devices with their start and end apart: 10, of which 5 were waited for; matrix products, arithmetic and copies ran while one was open for 3% of the time, Pallas kernels for 1%

profile of v10, /device:TPU:32, one launch (start us, length us, event | category | flops | bytes accessed | tf_op | source)
XLA Modules:
  0.0 112.6 jit_solution(8417491546160333866)
XLA Ops:
  0.0 3.8 %pick.1 = (bf16[64,16,512]{2,1,0:T(8,128)(2,1)S(1)}, s32[48]{0:T(128)S(1)}) custom-call(s32[4,128]{1,0:T(4,128)} %bitcast.16, s32[4,128]{1,0:T(4,128)} %bitcast.17, s32[32]{0:T(128)} %count.1, bf16[6144,512]{1,0:T(8,128)(2,1)} %loadings.1), custom_call_target="tpu_custom_call" | custom-call | tf_op jit(solution)/shard_map/pick/pallas_call | solution.py:187
  3.8 0.0 copy-start
  3.8 39.8 %all_to_all.15.recv = bf16[64,16,512]{2,1,0:T(8,128)(2,1)S(1)} all-to-all(bf16[64,16,512]{2,1,0:T(8,128)(2,1)S(1)} %get-tuple-element.13), channel_id=1, replica_groups=mesh['fac'=32,'scn'=8] {'fac'}, dimensions={0} | all-to-all | bytes 2097152 | tf_op jit(solution)/shard_map/all_to_all | solution.py:213
  43.6 1.5 %regroup.1 = bf16[8,18,16,128]{3,2,1,0:T(8,128)(2,1)} custom-call(s32[48]{0:T(128)S(1)} %get-tuple-element.12.table, bf16[64,16,512]{2,1,0:T(8,128)(2,1)S(1)} %all_to_all.15.recv, bf16[16,16,128]{2,1,0:T(8,128)(2,1)S(1)} %copy-done.1), custom_call_target="tpu_custom_call" | custom-call | tf_op jit(solution)/shard_map/regroup/pallas_call | solution.py:219
  45.0 4.3 %all-to-all-start.1 = ((bf16[8,18,16,128]{3,2,1,0:T(8,128)(2,1)}), bf16[8,18,16,128]{3,2,1,0:T(8,128)(2,1)S(1)}, u32[]{:S(2)}, u32[]{:S(2)}) async-start(bf16[8,18,16,128]{3,2,1,0:T(8,128)(2,1)} %regroup.1), calls=%async_computation.1 | async-start | bytes 1179648 | tf_op jit(solution)/shard_map/all_to_all | solution.py:227
  49.3 0.9 fusion.4
  50.2 2.0 %collective-permute-start.1 = (bf16[256,768]{1,0:T(8,128)(2,1)}, bf16[256,768]{1,0:T(8,128)(2,1)S(1)}, u32[]{:S(2)}, u32[]{:S(2)}) collective-permute-start(bf16[256,768]{1,0:T(8,128)(2,1)} %get-tuple-element.20), channel_id=1, source_target_pairs={{0,2},{1,3},{2,4},{3,5},{4,6},{5,7},{6,0},{7,1},{8,10},{9,11},{10,... | collective-permute-start | bytes 1179656 | tf_op jit(solution)/shard_map/ppermute | solution.py:181
  52.2 1.2 %collective-permute-start.4 = (bf16[256,768]{1,0:T(8,128)(2,1)}, bf16[256,768]{1,0:T(8,128)(2,1)S(1)}, u32[]{:S(2)}, u32[]{:S(2)}) collective-permute-start(bf16[256,768]{1,0:T(8,128)(2,1)} %get-tuple-element.19), channel_id=1, source_target_pairs={{0,6},{1,7},{2,0},{3,1},{4,2},{5,3},{6,4},{7,5},{8,14},{9,15},{10,... | collective-permute-start | bytes 1179656 | tf_op jit(solution)/shard_map/ppermute | solution.py:182
  53.4 0.8 collective-permute-start.2
  54.2 2.4 %collective-permute-start.3 = (bf16[256,768]{1,0:T(8,128)(2,1)}, bf16[256,768]{1,0:T(8,128)(2,1)}, u32[]{:S(2)}, u32[]{:S(2)}) collective-permute-start(bf16[256,768]{1,0:T(8,128)(2,1)} %get-tuple-element.20), channel_id=1, source_target_pairs={{0,6},{1,7},{2,0},{3,1},{4,2},{5,3},{6,4},{7,5},{8,14},{9,15},{10,... | collective-permute-start | bytes 1179656 | tf_op jit(solution)/shard_map/ppermute | solution.py:184
  56.7 12.1 %collective-permute-done.1.left_top = bf16[256,768]{1,0:T(8,128)(2,1)S(1)} collective-permute-done((bf16[256,768]{1,0:T(8,128)(2,1)}, bf16[256,768]{1,0:T(8,128)(2,1)S(1)}, u32[]{:S(2)}, u32[]{:S(2)}) %collective-permute-start.1) | collective-permute-done | bytes 393248 | tf_op jit(solution)/shard_map/ppermute | solution.py:181
  68.8 0.0 collective-permute-start.5
  68.8 0.0 collective-permute-done.4.right_low
  68.8 3.2 %collective-permute-start.6 = (bf16[256,768]{1,0:T(8,128)(2,1)S(1)}, bf16[256,768]{1,0:T(8,128)(2,1)}, u32[]{:S(2)}, u32[]{:S(2)}) collective-permute-start(bf16[256,768]{1,0:T(8,128)(2,1)S(1)} %collective-permute-done.4.right_low), channel_id=1, source_target_pairs={{0,6},{1,7},{2,0},{3,1},{4,2},{5,3},{6,4},{7,5},{8,14},{9,15},{10,... | collective-permute-start | bytes 1179656 | tf_op jit(solution)/shard_map/ppermute | solution.py:186
  72.1 0.0 all-to-all-done.1.recv
  72.1 1.5 %pair.1 = (f32[3,256,256]{2,1,0:T(8,128)S(1)}, bf16[3,256,256]{2,1,0:T(8,128)(2,1)}) custom-call(bf16[8,18,16,128]{3,2,1,0:T(8,128)(2,1)S(1)} %all-to-all-done.1.recv), custom_call_target="tpu_custom_call" | custom-call | tf_op jit(solution)/shard_map/pair/pallas_call | solution.py:228
  73.6 0.0 collective-permute-start
  73.6 0.8 dynamic_slice.6
  74.4 1.8 %multiply_reduce_fusion = f32[512]{0:T(512)S(1)} fusion(bf16[6144,512]{1,0:T(8,128)(2,1)} %loadings.1, s32[]{:T(128)S(6)} %select_n.10, f32[1536]{0:T(1024)S(1)} %dynamic_slice.6), kind=kLoop, calls=%fused_computation | loop fusion | flops 2358784 | bytes 1581060 | tf_op jit(solution)/shard_map/reduce_sum | solution.py:218
  76.1 1.1 collective-permute-done.2.left_low
  77.2 0.0 collective-permute-done.3.right_top
  77.2 8.1 %collective-permute-done.5.top_far = bf16[256,768]{1,0:T(8,128)(2,1)} collective-permute-done((bf16[256,768]{1,0:T(8,128)(2,1)S(1)}, bf16[256,768]{1,0:T(8,128)(2,1)}, u32[]{:S(2)}, u32[]{:S(2)}) %collective-permute-start.5) | collective-permute-done | bytes 393248 | tf_op jit(solution)/shard_map/ppermute | solution.py:185
  85.4 0.0 collective-permute-done.6.low_far
  85.4 0.0 collective-permute-done.other
  85.4 3.5 %form.1 = (f32[1,768]{1,0:T(1,128)S(1)}, f32[1,768]{1,0:T(1,128)S(1)}, f32[2,1,768]{2,1,0:T(1,128)S(1)}) custom-call(f32[3,256,256]{2,1,0:T(8,128)S(1)} %get-tuple-element.14.own, bf16[3,256,256]{2,1,0:T(8,128)(2,1)S(1)} %collective-permute-done.other, bf16[512,768]{1,0:T(8,128)(2,1)S(1)} %copy-done, bf16[256,768]{1,0:T(8,128)(2,1)S(1)} %collective-permute-done.1.left_top, ...), custom_call_target="tpu_custom_call" | custom-call | tf_op jit(solution)/shard_map/form/pallas_call | solution.py:237
  88.9 0.3 collective-permute-start.7
  89.2 3.4 %collective-permute-done.7 = f32[2,1,768]{2,1,0:T(1,128)S(1)} collective-permute-done((f32[2,1,768]{2,1,0:T(1,128)S(1)}, f32[2,1,768]{2,1,0:T(1,128)S(1)}, u32[]{:S(2)}, u32[]{:S(2)}) %collective-permute-start.7) | collective-permute-done | bytes 6176 | tf_op jit(solution)/shard_map/ppermute | solution.py:255
  92.6 0.9 collective-permute-start.8
  93.5 3.9 %collective-permute-done.8 = f32[1,768]{1,0:T(1,128)S(1)} collective-permute-done((f32[1,768]{1,0:T(1,128)S(1)}, f32[1,768]{1,0:T(1,128)S(1)}, u32[]{:S(2)}, u32[]{:S(2)}) %collective-permute-start.8) | collective-permute-done | bytes 3104 | tf_op jit(solution)/shard_map/ppermute | solution.py:257
  97.4 0.1 broadcast_in_dim.10
  97.5 14.5 %all_to_all.16 = f32[32,1,768]{2,1,0:T(1,128)S(1)} all-to-all(f32[32,1,768]{2,1,0:T(1,128)S(1)} %broadcast_in_dim.10), channel_id=1, replica_groups=mesh['fac'=32,'scn'=8] {'fac'}, dimensions={0} | all-to-all | bytes 196608 | tf_op jit(solution)/shard_map/all_to_all | solution.py:260
  111.9 0.7 reduce_sum.19
  (5 shorter events, 0.0 us)
Async XLA Ops:
  0.0 43.6 %copy-start.1 = (bf16[16,16,128]{2,1,0:T(8,128)(2,1)S(1)}, bf16[16,16,128]{2,1,0:T(8,128)(2,1)}, u32[]{:S(2)}) copy-start(bf16[16,16,128]{2,1,0:T(8,128)(2,1)} %gamma.1) | copy-start | bytes 196612
  3.8 45.5 %copy-start = (bf16[512,768]{1,0:T(8,128)(2,1)S(1)}, bf16[512,768]{1,0:T(8,128)(2,1)}, u32[]{:S(2)}) copy-start(bf16[512,768]{1,0:T(8,128)(2,1)} %here.1) | copy-start | bytes 2359300
  45.0 27.1 %all-to-all-start.1 = ((bf16[8,18,16,128]{3,2,1,0:T(8,128)(2,1)}), bf16[8,18,16,128]{3,2,1,0:T(8,128)(2,1)S(1)}, u32[]{:S(2)}, u32[]{:S(2)}) async-start(bf16[8,18,16,128]{3,2,1,0:T(8,128)(2,1)} %regroup.1), calls=%async_computation.1 | async-start | bytes 1179648 | tf_op jit(solution)/shard_map/all_to_all | solution.py:227
  50.2 18.6 %collective-permute-start.1 = (bf16[256,768]{1,0:T(8,128)(2,1)}, bf16[256,768]{1,0:T(8,128)(2,1)S(1)}, u32[]{:S(2)}, u32[]{:S(2)}) collective-permute-start(bf16[256,768]{1,0:T(8,128)(2,1)} %get-tuple-element.20), channel_id=1, source_target_pairs={{0,2},{1,3},{2,4},{3,5},{4,6},{5,7},{6,0},{7,1},{8,10},{9,11},{10,... | collective-permute-start | bytes 1179656 | tf_op jit(solution)/shard_map/ppermute | solution.py:181
  52.2 16.6 %collective-permute-start.4 = (bf16[256,768]{1,0:T(8,128)(2,1)}, bf16[256,768]{1,0:T(8,128)(2,1)S(1)}, u32[]{:S(2)}, u32[]{:S(2)}) collective-permute-start(bf16[256,768]{1,0:T(8,128)(2,1)} %get-tuple-element.19), channel_id=1, source_target_pairs={{0,6},{1,7},{2,0},{3,1},{4,2},{5,3},{6,4},{7,5},{8,14},{9,15},{10,... | collective-permute-start | bytes 1179656 | tf_op jit(solution)/shard_map/ppermute | solution.py:182
  53.4 23.8 %collective-permute-start.2 = (bf16[256,768]{1,0:T(8,128)(2,1)}, bf16[256,768]{1,0:T(8,128)(2,1)S(1)}, u32[]{:S(2)}, u32[]{:S(2)}) collective-permute-start(bf16[256,768]{1,0:T(8,128)(2,1)} %get-tuple-element.19), channel_id=1, source_target_pairs={{0,2},{1,3},{2,4},{3,5},{4,6},{5,7},{6,0},{7,1},{8,10},{9,11},{10,... | collective-permute-start | bytes 1179656 | tf_op jit(solution)/shard_map/ppermute | solution.py:183
  54.2 23.0 %collective-permute-start.3 = (bf16[256,768]{1,0:T(8,128)(2,1)}, bf16[256,768]{1,0:T(8,128)(2,1)}, u32[]{:S(2)}, u32[]{:S(2)}) collective-permute-start(bf16[256,768]{1,0:T(8,128)(2,1)} %get-tuple-element.20), channel_id=1, source_target_pairs={{0,6},{1,7},{2,0},{3,1},{4,2},{5,3},{6,4},{7,5},{8,14},{9,15},{10,... | collective-permute-start | bytes 1179656 | tf_op jit(solution)/shard_map/ppermute | solution.py:184
  68.8 16.6 %collective-permute-start.5 = (bf16[256,768]{1,0:T(8,128)(2,1)S(1)}, bf16[256,768]{1,0:T(8,128)(2,1)}, u32[]{:S(2)}, u32[]{:S(2)}) collective-permute-start(bf16[256,768]{1,0:T(8,128)(2,1)S(1)} %collective-permute-done.1.left_top), channel_id=1, source_target_pairs={{0,2},{1,3},{2,4},{3,5},{4,6},{5,7},{6,0},{7,1},{8,10},{9,11},{10,... | collective-permute-start | bytes 1179656 | tf_op jit(solution)/shard_map/ppermute | solution.py:185
  68.8 16.6 %collective-permute-start.6 = (bf16[256,768]{1,0:T(8,128)(2,1)S(1)}, bf16[256,768]{1,0:T(8,128)(2,1)}, u32[]{:S(2)}, u32[]{:S(2)}) collective-permute-start(bf16[256,768]{1,0:T(8,128)(2,1)S(1)} %collective-permute-done.4.right_low), channel_id=1, source_target_pairs={{0,6},{1,7},{2,0},{3,1},{4,2},{5,3},{6,4},{7,5},{8,14},{9,15},{10,... | collective-permute-start | bytes 1179656 | tf_op jit(solution)/shard_map/ppermute | solution.py:186
  73.6 11.8 %collective-permute-start = (bf16[3,256,256]{2,1,0:T(8,128)(2,1)}, bf16[3,256,256]{2,1,0:T(8,128)(2,1)S(1)}, u32[]{:S(2)}, u32[]{:S(2)}) collective-permute-start(bf16[3,256,256]{2,1,0:T(8,128)(2,1)} %get-tuple-element.15), channel_id=1, source_target_pairs={{0,1},{1,0},{2,3},{3,2},{4,5},{5,4},{6,7},{7,6},{8,9},{9,8},{10,11... | collective-permute-start | bytes 1179656 | tf_op jit(solution)/shard_map/ppermute | solution.py:236
  88.9 3.7 %collective-permute-start.7 = (f32[2,1,768]{2,1,0:T(1,128)S(1)}, f32[2,1,768]{2,1,0:T(1,128)S(1)}, u32[]{:S(2)}, u32[]{:S(2)}) collective-permute-start(f32[2,1,768]{2,1,0:T(1,128)S(1)} %get-tuple-element.17), channel_id=1, source_target_pairs={{0,2},{1,3},{2,0},{3,1},{4,6},{5,7},{6,4},{7,5},{8,10},{9,11},{10,... | collective-permute-start | bytes 18440 | tf_op jit(solution)/shard_map/ppermute | solution.py:255
  92.6 4.8 %collective-permute-start.8 = (f32[1,768]{1,0:T(1,128)S(1)}, f32[1,768]{1,0:T(1,128)S(1)}, u32[]{:S(2)}, u32[]{:S(2)}) collective-permute-start(f32[1,768]{1,0:T(1,128)S(1)} %fusion), channel_id=1, source_target_pairs={{0,6},{1,7},{2,4},{3,5},{4,2},{5,3},{6,0},{7,1},{8,14},{9,15},{10,... | collective-permute-start | bytes 9224 | tf_op jit(solution)/shard_map/ppermute | solution.py:257

commit v11 on v9

--- a/solution.py
+++ b/solution.py
@@ -1,3 +1,5 @@
+import functools
+
 import jax
 import jax.numpy as jnp
 from jax import lax
@@ -36,7 +38,7 @@
 
 def pick_kernel(
     rows, cols, count, loadings, out, table,
-    rows_v, cols_v, rows_s, cols_s, count_s, seen, sems, small,
+    rows_v, cols_v, rows_s, cols_s, count_s, seen, held, sems, out_sems, small,
 ):
     me = lax.axis_index("fac")
     part = lax.axis_index("scn")
@@ -62,12 +64,23 @@
 
     def fetch(slot, offset):
         start = pl.multiple_of(offset * LANES + part * SLICE, SLICE)
-        return pltpu.make_async_copy(loadings.at[pl.ds(start, SLICE), :], out.at[slot], sems.at[slot])
-
+        return pltpu.make_async_copy(loadings.at[pl.ds(start, SLICE), :], held.at[slot], sems.at[slot])
+
+    def push(slot):
+        return pltpu.make_async_copy(held.at[slot], out.at[slot], out_sems.at[slot])
+
+    named = []
     for o in range(OWNERS):
         row, col = o // 8, (o % 8) * CAP
-        fetch(2 * o, jnp.minimum(keys[row, col] & 63, BLOCKS_DEV - 1)).start()
-        fetch(2 * o + 1, jnp.minimum((-keys[4 + row, col]) & 63, BLOCKS_DEV - 1)).start()
+        first = keys[row, col]
+        last = -keys[4 + row, col]
+        named += [(first < 1 << 20, first), ((first < 1 << 20) & (last != first), last)]
+
+    def each(act):
+        for slot, (wanted, key) in enumerate(named):
+            pl.when(wanted)(functools.partial(act, slot, key))
+
+    each(lambda slot, key: fetch(slot, jnp.minimum(key & 63, BLOCKS_DEV - 1)).start())
     for move in moves[2:]:
         move.wait()
     for h in range(OWNERS):
@@ -83,8 +96,13 @@
     for p in range(CAP):
         weight = jnp.where(rows_s[row, col + p] == cols_s[row, col + p], 1, 2)
         table[2 * CAP + p] = jnp.where(p < live, weight, 0)
-    for slot in range(2 * OWNERS):
+
+    def forward(slot, key):
         fetch(slot, 0).wait()
+        push(slot).start()
+
+    each(forward)
+    each(lambda slot, key: push(slot).wait())
 
 
 def regroup_kernel(table, recv, gamma, out):
@@ -179,11 +197,11 @@
     outgoing, table = pl.pallas_call(
         pick_kernel,
         out_shape=(
-            pltpu.VMEM((2 * OWNERS, SLICE, depth), BF16),
+            jax.ShapeDtypeStruct((2 * OWNERS, SLICE, depth), BF16),
             jax.ShapeDtypeStruct((3 * CAP,), jnp.int32),
         ),
         in_specs=[HBM, HBM, HBM, HBM],
-        out_specs=(VMEM, SMEM),
+        out_specs=(HBM, SMEM),
         scratch_shapes=[
             pltpu.VMEM((4, LANES), jnp.int32),
             pltpu.VMEM((4, LANES), jnp.int32),
@@ -191,6 +209,8 @@
             pltpu.SMEM((4, LANES), jnp.int32),
             pltpu.SMEM((OWNERS,), jnp.int32),
             pltpu.SMEM((OWNERS,), jnp.int32),
+            pltpu.VMEM((2 * OWNERS, SLICE, depth), BF16),
+            pltpu.SemaphoreType.DMA((2 * OWNERS,)),
             pltpu.SemaphoreType.DMA((2 * OWNERS,)),
             pltpu.SemaphoreType.DMA((5,)),
         ],

time: 112 us -> 114 us (1.018)
  Pallas kernels: 10 us -> 11.4 us
    pallas_call x1, Pallas kernels: 3.82 us -> 5.19 us  [body(): pl.pallas_call(pick_kernel, out_shape=(jax.ShapeDtypeStruct((2 * OWNERS,...]
where the time goes in v11:
time: 114 us; the launch traced here: 112 us
  blocking collectives  62.6 us (55%)
  waiting for transfers between devices  23 us (20%)
  Pallas kernels  11.4 us (10%)
  starting transfers between devices  10.9 us (10%)
  other arithmetic  2.48 us (2%)
  local copies, waits for them, and re-layouts  1.78 us (2%)
    all_to_all x1, blocking collectives, body(): lax.all_to_all(outgoing, 'fac', split_axis=0, concat_axis=0, tiled=True)  40 us
    all_to_all x1, blocking collectives, body(): every = lax.all_to_all(mine, 'fac', split_axis=0, concat_axis=0, tiled=True)  15.1 us
    ppermute x1, waiting for transfers between devices, body(): left_top = lax.ppermute(upper, 'scn', ring(2))  11.6 us
    all_to_all x1, blocking collectives, body(): lax.all_to_all(spread, 'scn', split_axis=0, concat_axis=0, tiled=True, ax...  7.55 us
    ppermute x1, waiting for transfers between devices, body(): far_top = lax.ppermute(left_top, 'scn', ring(2))  7.03 us
    pallas_call x1, Pallas kernels, body(): pl.pallas_call(pick_kernel, out_shape=(jax.ShapeDtypeStruct((2 * OWNERS,...  5.19 us
    all_to_all x1, starting transfers between devices, body(): lax.all_to_all(grouped, 'scn', split_axis=0, concat_axis=0, tiled=True)  4.8 us
    pallas_call x1, Pallas kernels, body(): pl.pallas_call(form_kernel, out_shape=pltpu.VMEM((PARTS // 2, 1, columns)...  3.24 us
  transfers between devices with their start and end apart: 8, of which 5 were waited for; matrix products, arithmetic and copies ran while one was open for 3% of the time, Pallas kernels for 1%

profile of v11, /device:TPU:4, one launch (start us, length us, event | category | flops | bytes accessed | tf_op | source)
XLA Modules:
  0.0 112.2 jit_solution(6925402209568938320)
XLA Ops:
  0.0 0.0 copy-start.1
  0.0 5.2 %pick.1 = (bf16[64,16,512]{2,1,0:T(8,128)(2,1)S(1)}, s32[48]{0:T(128)S(1)}) custom-call(s32[4,128]{1,0:T(4,128)} %bitcast.4, s32[4,128]{1,0:T(4,128)} %bitcast.5, s32[32]{0:T(128)} %count.1, bf16[6144,512]{1,0:T(8,128)(2,1)} %loadings.1), custom_call_target="tpu_custom_call" | custom-call | tf_op jit(solution)/shard_map/pick/pallas_call | solution.py:197
  5.2 0.0 copy-start
  5.2 40.0 %all_to_all.20.recv = bf16[64,16,512]{2,1,0:T(8,128)(2,1)S(1)} all-to-all(bf16[64,16,512]{2,1,0:T(8,128)(2,1)S(1)} %get-tuple-element.10), channel_id=1, replica_groups=mesh['fac'=32,'scn'=8] {'fac'}, dimensions={0} | all-to-all | bytes 2097152 | tf_op jit(solution)/shard_map/all_to_all | solution.py:225
  45.2 0.0 copy-done.1
  45.2 1.5 %regroup.1 = bf16[8,18,16,128]{3,2,1,0:T(8,128)(2,1)} custom-call(s32[48]{0:T(128)S(1)} %get-tuple-element.9.table, bf16[64,16,512]{2,1,0:T(8,128)(2,1)S(1)} %all_to_all.20.recv, bf16[16,16,128]{2,1,0:T(8,128)(2,1)S(1)} %copy-done.1), custom_call_target="tpu_custom_call" | custom-call | tf_op jit(solution)/shard_map/regroup/pallas_call | solution.py:231
  46.7 4.8 %all-to-all-start.1 = ((bf16[8,18,16,128]{3,2,1,0:T(8,128)(2,1)}), bf16[8,18,16,128]{3,2,1,0:T(8,128)(2,1)S(1)}, u32[]{:S(2)}, u32[]{:S(2)}) async-start(bf16[8,18,16,128]{3,2,1,0:T(8,128)(2,1)} %regroup.1), calls=%async_computation.1 | async-start | bytes 1179648 | tf_op jit(solution)/shard_map/all_to_all | solution.py:239
  51.5 0.0 copy-done
  51.5 0.9 fusion
  52.4 1.2 %collective-permute-start.1 = (bf16[256,768]{1,0:T(8,128)(2,1)}, bf16[256,768]{1,0:T(8,128)(2,1)S(1)}, u32[]{:S(2)}, u32[]{:S(2)}) collective-permute-start(bf16[256,768]{1,0:T(8,128)(2,1)} %get-tuple-element.14), channel_id=1, source_target_pairs={{0,2},{1,3},{2,4},{3,5},{4,6},{5,7},{6,0},{7,1},{8,10},{9,11},{10,... | collective-permute-start | bytes 1179656 | tf_op jit(solution)/shard_map/ppermute | solution.py:191
  53.6 0.9 collective-permute-start.4
  54.5 1.2 %collective-permute-start.2 = (bf16[256,768]{1,0:T(8,128)(2,1)}, bf16[256,768]{1,0:T(8,128)(2,1)S(1)}, u32[]{:S(2)}, u32[]{:S(2)}) collective-permute-start(bf16[256,768]{1,0:T(8,128)(2,1)} %get-tuple-element.13), channel_id=1, source_target_pairs={{0,2},{1,3},{2,4},{3,5},{4,6},{5,7},{6,0},{7,1},{8,10},{9,11},{10,... | collective-permute-start | bytes 1179656 | tf_op jit(solution)/shard_map/ppermute | solution.py:193
  55.6 0.9 collective-permute-start.3
  56.5 11.6 %collective-permute-done.1.left_top = bf16[256,768]{1,0:T(8,128)(2,1)S(1)} collective-permute-done((bf16[256,768]{1,0:T(8,128)(2,1)}, bf16[256,768]{1,0:T(8,128)(2,1)S(1)}, u32[]{:S(2)}, u32[]{:S(2)}) %collective-permute-start.1) | collective-permute-done | bytes 393248 | tf_op jit(solution)/shard_map/ppermute | solution.py:191
  68.1 2.0 %collective-permute-start.5 = (bf16[256,768]{1,0:T(8,128)(2,1)S(1)}, bf16[256,768]{1,0:T(8,128)(2,1)}, u32[]{:S(2)}, u32[]{:S(2)}) collective-permute-start(bf16[256,768]{1,0:T(8,128)(2,1)S(1)} %collective-permute-done.1.left_top), channel_id=1, source_target_pairs={{0,2},{1,3},{2,4},{3,5},{4,6},{5,7},{6,0},{7,1},{8,10},{9,11},{10,... | collective-permute-start | bytes 1179656 | tf_op jit(solution)/shard_map/ppermute | solution.py:195
  70.0 0.0 collective-permute-done.4.right_low
  70.0 0.0 collective-permute-start.6
  70.1 0.0 all-to-all-done.1.recv
  70.1 1.5 %pair.1 = (f32[3,256,256]{2,1,0:T(8,128)S(1)}, bf16[3,256,256]{2,1,0:T(8,128)(2,1)}) custom-call(bf16[8,18,16,128]{3,2,1,0:T(8,128)(2,1)S(1)} %all-to-all-done.1.recv), custom_call_target="tpu_custom_call" | custom-call | tf_op jit(solution)/shard_map/pair/pallas_call | solution.py:240
  71.6 0.0 collective-permute-start
  71.6 0.8 dynamic_slice.6
  72.4 1.8 %multiply_reduce_fusion = f32[512]{0:T(512)S(1)} fusion(bf16[6144,512]{1,0:T(8,128)(2,1)} %loadings.1, s32[]{:T(128)S(6)} %select_n.10, f32[1536]{0:T(1024)S(1)} %dynamic_slice.6), kind=kLoop, calls=%fused_computation | loop fusion | flops 2358784 | bytes 1581060 | tf_op jit(solution)/shard_map/reduce_sum | solution.py:230
  74.2 2.3 %collective-permute-done.2.left_low = bf16[256,768]{1,0:T(8,128)(2,1)S(1)} collective-permute-done((bf16[256,768]{1,0:T(8,128)(2,1)}, bf16[256,768]{1,0:T(8,128)(2,1)S(1)}, u32[]{:S(2)}, u32[]{:S(2)}) %collective-permute-start.2) | collective-permute-done | bytes 393248 | tf_op jit(solution)/shard_map/ppermute | solution.py:193
  76.5 1.2 %collective-permute-done.3.right_top = bf16[256,768]{1,0:T(8,128)(2,1)} collective-permute-done((bf16[256,768]{1,0:T(8,128)(2,1)}, bf16[256,768]{1,0:T(8,128)(2,1)}, u32[]{:S(2)}, u32[]{:S(2)}) %collective-permute-start.3) | collective-permute-done | bytes 393248 | tf_op jit(solution)/shard_map/ppermute | solution.py:194
  77.7 7.0 %collective-permute-done.5.top_far = bf16[256,768]{1,0:T(8,128)(2,1)} collective-permute-done((bf16[256,768]{1,0:T(8,128)(2,1)S(1)}, bf16[256,768]{1,0:T(8,128)(2,1)}, u32[]{:S(2)}, u32[]{:S(2)}) %collective-permute-start.5) | collective-permute-done | bytes 393248 | tf_op jit(solution)/shard_map/ppermute | solution.py:195
  84.8 0.8 collective-permute-done.6.low_far
  85.6 0.0 collective-permute-done.other
  85.6 3.2 %form.1 = f32[4,1,768]{2,1,0:T(1,128)S(1)} custom-call(f32[3,256,256]{2,1,0:T(8,128)S(1)} %get-tuple-element.11.own, bf16[3,256,256]{2,1,0:T(8,128)(2,1)S(1)} %collective-permute-done.other, bf16[512,768]{1,0:T(8,128)(2,1)S(1)} %copy-done, bf16[256,768]{1,0:T(8,128)(2,1)S(1)} %collective-permute-done.1.left_top, ...), custom_call_target="tpu_custom_call" | custom-call | tf_op jit(solution)/shard_map/form/pallas_call | solution.py:249
  88.8 7.5 %all_to_all.21 = f32[4,1,768]{2,1,0:T(1,128)S(1)} all-to-all(f32[4,1,768]{2,1,0:T(1,128)S(1)} %form.1), channel_id=1, replica_groups={{0,2,4,6},{1,3,5,7},{8,10,12,14},{9,11,13,15},{16,18,20,22},{17,19,21,2..., dimensions={0} | all-to-all | bytes 24576 | tf_op jit(solution)/shard_map/all_to_all | solution.py:263
  96.4 0.1 broadcast_in_dim.2
  96.5 15.1 %all_to_all.22 = f32[32,1,768]{2,1,0:T(1,128)S(1)} all-to-all(f32[32,1,768]{2,1,0:T(1,128)S(1)} %broadcast_in_dim.2), channel_id=1, replica_groups=mesh['fac'=32,'scn'=8] {'fac'}, dimensions={0} | all-to-all | bytes 196608 | tf_op jit(solution)/shard_map/all_to_all | solution.py:267
  111.5 0.7 reduce_sum.29
  (1 shorter events, 0.0 us)
Async XLA Ops:
  0.0 45.2 %copy-start.1 = (bf16[16,16,128]{2,1,0:T(8,128)(2,1)S(1)}, bf16[16,16,128]{2,1,0:T(8,128)(2,1)}, u32[]{:S(2)}) copy-start(bf16[16,16,128]{2,1,0:T(8,128)(2,1)} %gamma.1) | copy-start | bytes 196612
  5.2 46.3 %copy-start = (bf16[512,768]{1,0:T(8,128)(2,1)S(1)}, bf16[512,768]{1,0:T(8,128)(2,1)}, u32[]{:S(2)}) copy-start(bf16[512,768]{1,0:T(8,128)(2,1)} %here.1) | copy-start | bytes 2359300
  46.7 23.4 %all-to-all-start.1 = ((bf16[8,18,16,128]{3,2,1,0:T(8,128)(2,1)}), bf16[8,18,16,128]{3,2,1,0:T(8,128)(2,1)S(1)}, u32[]{:S(2)}, u32[]{:S(2)}) async-start(bf16[8,18,16,128]{3,2,1,0:T(8,128)(2,1)} %regroup.1), calls=%async_computation.1 | async-start | bytes 1179648 | tf_op jit(solution)/shard_map/all_to_all | solution.py:239
  52.4 15.6 %collective-permute-start.1 = (bf16[256,768]{1,0:T(8,128)(2,1)}, bf16[256,768]{1,0:T(8,128)(2,1)S(1)}, u32[]{:S(2)}, u32[]{:S(2)}) collective-permute-start(bf16[256,768]{1,0:T(8,128)(2,1)} %get-tuple-element.14), channel_id=1, source_target_pairs={{0,2},{1,3},{2,4},{3,5},{4,6},{5,7},{6,0},{7,1},{8,10},{9,11},{10,... | collective-permute-start | bytes 1179656 | tf_op jit(solution)/shard_map/ppermute | solution.py:191
  53.6 16.5 %collective-permute-start.4 = (bf16[256,768]{1,0:T(8,128)(2,1)}, bf16[256,768]{1,0:T(8,128)(2,1)S(1)}, u32[]{:S(2)}, u32[]{:S(2)}) collective-permute-start(bf16[256,768]{1,0:T(8,128)(2,1)} %get-tuple-element.13), channel_id=1, source_target_pairs={{0,6},{1,7},{2,0},{3,1},{4,2},{5,3},{6,4},{7,5},{8,14},{9,15},{10,... | collective-permute-start | bytes 1179656 | tf_op jit(solution)/shard_map/ppermute | solution.py:192
  54.5 22.0 %collective-permute-start.2 = (bf16[256,768]{1,0:T(8,128)(2,1)}, bf16[256,768]{1,0:T(8,128)(2,1)S(1)}, u32[]{:S(2)}, u32[]{:S(2)}) collective-permute-start(bf16[256,768]{1,0:T(8,128)(2,1)} %get-tuple-element.13), channel_id=1, source_target_pairs={{0,2},{1,3},{2,4},{3,5},{4,6},{5,7},{6,0},{7,1},{8,10},{9,11},{10,... | collective-permute-start | bytes 1179656 | tf_op jit(solution)/shard_map/ppermute | solution.py:193
  55.6 22.1 %collective-permute-start.3 = (bf16[256,768]{1,0:T(8,128)(2,1)}, bf16[256,768]{1,0:T(8,128)(2,1)}, u32[]{:S(2)}, u32[]{:S(2)}) collective-permute-start(bf16[256,768]{1,0:T(8,128)(2,1)} %get-tuple-element.14), channel_id=1, source_target_pairs={{0,6},{1,7},{2,0},{3,1},{4,2},{5,3},{6,4},{7,5},{8,14},{9,15},{10,... | collective-permute-start | bytes 1179656 | tf_op jit(solution)/shard_map/ppermute | solution.py:194
  68.1 16.7 %collective-permute-start.5 = (bf16[256,768]{1,0:T(8,128)(2,1)S(1)}, bf16[256,768]{1,0:T(8,128)(2,1)}, u32[]{:S(2)}, u32[]{:S(2)}) collective-permute-start(bf16[256,768]{1,0:T(8,128)(2,1)S(1)} %collective-permute-done.1.left_top), channel_id=1, source_target_pairs={{0,2},{1,3},{2,4},{3,5},{4,6},{5,7},{6,0},{7,1},{8,10},{9,11},{10,... | collective-permute-start | bytes 1179656 | tf_op jit(solution)/shard_map/ppermute | solution.py:195
  70.0 15.5 %collective-permute-start.6 = (bf16[256,768]{1,0:T(8,128)(2,1)S(1)}, bf16[256,768]{1,0:T(8,128)(2,1)}, u32[]{:S(2)}, u32[]{:S(2)}) collective-permute-start(bf16[256,768]{1,0:T(8,128)(2,1)S(1)} %collective-permute-done.4.right_low), channel_id=1, source_target_pairs={{0,6},{1,7},{2,0},{3,1},{4,2},{5,3},{6,4},{7,5},{8,14},{9,15},{10,... | collective-permute-start | bytes 1179656 | tf_op jit(solution)/shard_map/ppermute | solution.py:196
  71.6 14.0 %collective-permute-start = (bf16[3,256,256]{2,1,0:T(8,128)(2,1)}, bf16[3,256,256]{2,1,0:T(8,128)(2,1)S(1)}, u32[]{:S(2)}, u32[]{:S(2)}) collective-permute-start(bf16[3,256,256]{2,1,0:T(8,128)(2,1)} %get-tuple-element.12), channel_id=1, source_target_pairs={{0,1},{1,0},{2,3},{3,2},{4,5},{5,4},{6,7},{7,6},{8,9},{9,8},{10,11... | collective-permute-start | bytes 1179656 | tf_op jit(solution)/shard_map/ppermute | solution.py:248

commit v12 on v10

--- a/solution.py
+++ b/solution.py
@@ -162,7 +162,7 @@
         total = jnp.sum(more[:WIDE] * upper.astype(F32) + image[extra:] * lower.astype(F32), axis=0, keepdims=True)
         group = (chip + step) & 3
         beside = group == (chip ^ 1)
-        place = jnp.where(group == 3 - chip, 1, jnp.where(beside, 2, 3)) if step else 0
+        place = jnp.where(beside, 1, jnp.where(group == 3 - chip, 2, 3)) if step else 0
         out[place] = total + jnp.sum(more[WIDE:], axis=0, keepdims=True)
     mine[...] = out[0]
     across[...] = out[1]
@@ -252,9 +252,9 @@
         compiler_params=GRANT,
         name="form",
     )(near(own), near(other), draws, near(left_top), near(left_low), near(right_top), near(right_low), away(far_top), away(far_low), slope.reshape(1, depth))
-    near_sum = lax.ppermute(send, "scn", [(i, i ^ 2) for i in range(PARTS)])
+    near_sum = lax.ppermute(send, "scn", [(i, 6 - i + 2 * (i % 2)) for i in range(PARTS)])
     across = across + near_sum[1]
-    over = lax.ppermute(across, "scn", [(i, 6 - i + 2 * (i % 2)) for i in range(PARTS)])
+    over = lax.ppermute(across, "scn", [(i, i ^ 2) for i in range(PARTS)])
     total = mine + near_sum[0] + over
     spread = jnp.broadcast_to(total[None], (OWNERS, 1, columns))
     every = lax.all_to_all(spread, "fac", split_axis=0, concat_axis=0, tiled=True)

time: 113 us -> 113 us (level)
  no operation moved by 1% of the time
where the time goes in v12:
time: 113 us
  blocking collectives  54.2 us (48%)
  waiting for transfers between devices  28.9 us (26%)
  starting transfers between devices  15 us (13%)
  Pallas kernels  10.2 us (9%)
  other arithmetic  2.48 us (2%)
  local copies, waits for them, and re-layouts  1.77 us (2%)
    all_to_all x1, blocking collectives, body(): lax.all_to_all(outgoing, 'fac', split_axis=0, concat_axis=0, tiled=True)  39.8 us
    all_to_all x1, blocking collectives, body(): lax.all_to_all(spread, 'fac', split_axis=0, concat_axis=0, tiled=True)  14.5 us
    ppermute x1, waiting for transfers between devices, body(): left_top = lax.ppermute(upper, 'scn', ring(2))  12.1 us
    ppermute x1, waiting for transfers between devices, body(): far_top = lax.ppermute(left_top, 'scn', ring(2))  8.14 us
    all_to_all x1, starting transfers between devices, body(): lax.all_to_all(grouped, 'scn', split_axis=0, concat_axis=0, tiled=True)  4.27 us
    ppermute x1, waiting for transfers between devices, body(): lax.ppermute(send, 'scn', [(i, 6 - i + 2 * (i % 2)) for i in range(PARTS)])  3.93 us
    pallas_call x1, Pallas kernels, body(): pl.pallas_call(pick_kernel, out_shape=(pltpu.VMEM((2 * OWNERS, SLICE, dep...  3.76 us
    ppermute x1, waiting for transfers between devices, body(): over = lax.ppermute(across, 'scn', [(i, i ^ 2) for i in range(PARTS)])  3.59 us
  transfers between devices with their start and end apart: 10, of which 5 were waited for; matrix products, arithmetic and copies ran while one was open for 3% of the time, Pallas kernels for 1%

profile of v12, /device:TPU:32, one launch (start us, length us, event | category | flops | bytes accessed | tf_op | source)
XLA Modules:
  0.0 112.6 jit_solution(5661824024627590271)
XLA Ops:
  0.0 3.8 %pick.1 = (bf16[64,16,512]{2,1,0:T(8,128)(2,1)S(1)}, s32[48]{0:T(128)S(1)}) custom-call(s32[4,128]{1,0:T(4,128)} %bitcast.16, s32[4,128]{1,0:T(4,128)} %bitcast.17, s32[32]{0:T(128)} %count.1, bf16[6144,512]{1,0:T(8,128)(2,1)} %loadings.1), custom_call_target="tpu_custom_call" | custom-call | tf_op jit(solution)/shard_map/pick/pallas_call | solution.py:187
  3.8 0.0 copy-start
  3.8 39.8 %all_to_all.15.recv = bf16[64,16,512]{2,1,0:T(8,128)(2,1)S(1)} all-to-all(bf16[64,16,512]{2,1,0:T(8,128)(2,1)S(1)} %get-tuple-element.13), channel_id=1, replica_groups=mesh['fac'=32,'scn'=8] {'fac'}, dimensions={0} | all-to-all | bytes 2097152 | tf_op jit(solution)/shard_map/all_to_all | solution.py:213
  43.6 1.5 %regroup.1 = bf16[8,18,16,128]{3,2,1,0:T(8,128)(2,1)} custom-call(s32[48]{0:T(128)S(1)} %get-tuple-element.12.table, bf16[64,16,512]{2,1,0:T(8,128)(2,1)S(1)} %all_to_all.15.recv, bf16[16,16,128]{2,1,0:T(8,128)(2,1)S(1)} %copy-done.1), custom_call_target="tpu_custom_call" | custom-call | tf_op jit(solution)/shard_map/regroup/pallas_call | solution.py:219
  45.0 4.3 %all-to-all-start.1 = ((bf16[8,18,16,128]{3,2,1,0:T(8,128)(2,1)}), bf16[8,18,16,128]{3,2,1,0:T(8,128)(2,1)S(1)}, u32[]{:S(2)}, u32[]{:S(2)}) async-start(bf16[8,18,16,128]{3,2,1,0:T(8,128)(2,1)} %regroup.1), calls=%async_computation.1 | async-start | bytes 1179648 | tf_op jit(solution)/shard_map/all_to_all | solution.py:227
  49.3 0.9 fusion.4
  50.2 2.0 %collective-permute-start.1 = (bf16[256,768]{1,0:T(8,128)(2,1)}, bf16[256,768]{1,0:T(8,128)(2,1)S(1)}, u32[]{:S(2)}, u32[]{:S(2)}) collective-permute-start(bf16[256,768]{1,0:T(8,128)(2,1)} %get-tuple-element.20), channel_id=1, source_target_pairs={{0,2},{1,3},{2,4},{3,5},{4,6},{5,7},{6,0},{7,1},{8,10},{9,11},{10,... | collective-permute-start | bytes 1179656 | tf_op jit(solution)/shard_map/ppermute | solution.py:181
  52.2 1.2 %collective-permute-start.4 = (bf16[256,768]{1,0:T(8,128)(2,1)}, bf16[256,768]{1,0:T(8,128)(2,1)S(1)}, u32[]{:S(2)}, u32[]{:S(2)}) collective-permute-start(bf16[256,768]{1,0:T(8,128)(2,1)} %get-tuple-element.19), channel_id=1, source_target_pairs={{0,6},{1,7},{2,0},{3,1},{4,2},{5,3},{6,4},{7,5},{8,14},{9,15},{10,... | collective-permute-start | bytes 1179656 | tf_op jit(solution)/shard_map/ppermute | solution.py:182
  53.4 0.8 collective-permute-start.2
  54.2 2.4 %collective-permute-start.3 = (bf16[256,768]{1,0:T(8,128)(2,1)}, bf16[256,768]{1,0:T(8,128)(2,1)}, u32[]{:S(2)}, u32[]{:S(2)}) collective-permute-start(bf16[256,768]{1,0:T(8,128)(2,1)} %get-tuple-element.20), channel_id=1, source_target_pairs={{0,6},{1,7},{2,0},{3,1},{4,2},{5,3},{6,4},{7,5},{8,14},{9,15},{10,... | collective-permute-start | bytes 1179656 | tf_op jit(solution)/shard_map/ppermute | solution.py:184
  56.7 12.1 %collective-permute-done.1.left_top = bf16[256,768]{1,0:T(8,128)(2,1)S(1)} collective-permute-done((bf16[256,768]{1,0:T(8,128)(2,1)}, bf16[256,768]{1,0:T(8,128)(2,1)S(1)}, u32[]{:S(2)}, u32[]{:S(2)}) %collective-permute-start.1) | collective-permute-done | bytes 393248 | tf_op jit(solution)/shard_map/ppermute | solution.py:181
  68.8 0.0 collective-permute-start.5
  68.8 0.0 collective-permute-done.4.right_low
  68.8 3.2 %collective-permute-start.6 = (bf16[256,768]{1,0:T(8,128)(2,1)S(1)}, bf16[256,768]{1,0:T(8,128)(2,1)}, u32[]{:S(2)}, u32[]{:S(2)}) collective-permute-start(bf16[256,768]{1,0:T(8,128)(2,1)S(1)} %collective-permute-done.4.right_low), channel_id=1, source_target_pairs={{0,6},{1,7},{2,0},{3,1},{4,2},{5,3},{6,4},{7,5},{8,14},{9,15},{10,... | collective-permute-start | bytes 1179656 | tf_op jit(solution)/shard_map/ppermute | solution.py:186
  72.1 0.0 all-to-all-done.1.recv
  72.1 1.5 %pair.1 = (f32[3,256,256]{2,1,0:T(8,128)S(1)}, bf16[3,256,256]{2,1,0:T(8,128)(2,1)}) custom-call(bf16[8,18,16,128]{3,2,1,0:T(8,128)(2,1)S(1)} %all-to-all-done.1.recv), custom_call_target="tpu_custom_call" | custom-call | tf_op jit(solution)/shard_map/pair/pallas_call | solution.py:228
  73.6 0.0 collective-permute-start
  73.6 0.8 dynamic_slice.6
  74.4 1.8 %multiply_reduce_fusion = f32[512]{0:T(512)S(1)} fusion(bf16[6144,512]{1,0:T(8,128)(2,1)} %loadings.1, s32[]{:T(128)S(6)} %select_n.10, f32[1536]{0:T(1024)S(1)} %dynamic_slice.6), kind=kLoop, calls=%fused_computation | loop fusion | flops 2358784 | bytes 1581060 | tf_op jit(solution)/shard_map/reduce_sum | solution.py:218
  76.1 1.1 collective-permute-done.2.left_low
  77.2 0.0 collective-permute-done.3.right_top
  77.2 8.1 %collective-permute-done.5.top_far = bf16[256,768]{1,0:T(8,128)(2,1)} collective-permute-done((bf16[256,768]{1,0:T(8,128)(2,1)S(1)}, bf16[256,768]{1,0:T(8,128)(2,1)}, u32[]{:S(2)}, u32[]{:S(2)}) %collective-permute-start.5) | collective-permute-done | bytes 393248 | tf_op jit(solution)/shard_map/ppermute | solution.py:185
  85.4 0.0 collective-permute-done.6.low_far
  85.4 0.0 collective-permute-done.other
  85.4 3.5 %form.1 = (f32[1,768]{1,0:T(1,128)S(1)}, f32[1,768]{1,0:T(1,128)S(1)}, f32[2,1,768]{2,1,0:T(1,128)S(1)}) custom-call(f32[3,256,256]{2,1,0:T(8,128)S(1)} %get-tuple-element.14.own, bf16[3,256,256]{2,1,0:T(8,128)(2,1)S(1)} %collective-permute-done.other, bf16[512,768]{1,0:T(8,128)(2,1)S(1)} %copy-done, bf16[256,768]{1,0:T(8,128)(2,1)S(1)} %collective-permute-done.1.left_top, ...), custom_call_target="tpu_custom_call" | custom-call | tf_op jit(solution)/shard_map/form/pallas_call | solution.py:237
  88.9 1.0 collective-permute-start.7
  89.9 3.9 %collective-permute-done.7 = f32[2,1,768]{2,1,0:T(1,128)S(1)} collective-permute-done((f32[2,1,768]{2,1,0:T(1,128)S(1)}, f32[2,1,768]{2,1,0:T(1,128)S(1)}, u32[]{:S(2)}, u32[]{:S(2)}) %collective-permute-start.7) | collective-permute-done | bytes 6176 | tf_op jit(solution)/shard_map/ppermute | solution.py:255
  93.8 0.0 collective-permute-start.8
  93.8 3.6 %collective-permute-done.8 = f32[1,768]{1,0:T(1,128)S(1)} collective-permute-done((f32[1,768]{1,0:T(1,128)S(1)}, f32[1,768]{1,0:T(1,128)S(1)}, u32[]{:S(2)}, u32[]{:S(2)}) %collective-permute-start.8) | collective-permute-done | bytes 3104 | tf_op jit(solution)/shard_map/ppermute | solution.py:257
  97.4 0.1 broadcast_in_dim.10
  97.5 14.5 %all_to_all.16 = f32[32,1,768]{2,1,0:T(1,128)S(1)} all-to-all(f32[32,1,768]{2,1,0:T(1,128)S(1)} %broadcast_in_dim.10), channel_id=1, replica_groups=mesh['fac'=32,'scn'=8] {'fac'}, dimensions={0} | all-to-all | bytes 196608 | tf_op jit(solution)/shard_map/all_to_all | solution.py:260
  111.9 0.7 reduce_sum.19
  (5 shorter events, 0.0 us)
Async XLA Ops:
  0.0 43.6 %copy-start.1 = (bf16[16,16,128]{2,1,0:T(8,128)(2,1)S(1)}, bf16[16,16,128]{2,1,0:T(8,128)(2,1)}, u32[]{:S(2)}) copy-start(bf16[16,16,128]{2,1,0:T(8,128)(2,1)} %gamma.1) | copy-start | bytes 196612
  3.8 45.5 %copy-start = (bf16[512,768]{1,0:T(8,128)(2,1)S(1)}, bf16[512,768]{1,0:T(8,128)(2,1)}, u32[]{:S(2)}) copy-start(bf16[512,768]{1,0:T(8,128)(2,1)} %here.1) | copy-start | bytes 2359300
  45.0 27.1 %all-to-all-start.1 = ((bf16[8,18,16,128]{3,2,1,0:T(8,128)(2,1)}), bf16[8,18,16,128]{3,2,1,0:T(8,128)(2,1)S(1)}, u32[]{:S(2)}, u32[]{:S(2)}) async-start(bf16[8,18,16,128]{3,2,1,0:T(8,128)(2,1)} %regroup.1), calls=%async_computation.1 | async-start | bytes 1179648 | tf_op jit(solution)/shard_map/all_to_all | solution.py:227
  50.2 18.6 %collective-permute-start.1 = (bf16[256,768]{1,0:T(8,128)(2,1)}, bf16[256,768]{1,0:T(8,128)(2,1)S(1)}, u32[]{:S(2)}, u32[]{:S(2)}) collective-permute-start(bf16[256,768]{1,0:T(8,128)(2,1)} %get-tuple-element.20), channel_id=1, source_target_pairs={{0,2},{1,3},{2,4},{3,5},{4,6},{5,7},{6,0},{7,1},{8,10},{9,11},{10,... | collective-permute-start | bytes 1179656 | tf_op jit(solution)/shard_map/ppermute | solution.py:181
  52.2 16.6 %collective-permute-start.4 = (bf16[256,768]{1,0:T(8,128)(2,1)}, bf16[256,768]{1,0:T(8,128)(2,1)S(1)}, u32[]{:S(2)}, u32[]{:S(2)}) collective-permute-start(bf16[256,768]{1,0:T(8,128)(2,1)} %get-tuple-element.19), channel_id=1, source_target_pairs={{0,6},{1,7},{2,0},{3,1},{4,2},{5,3},{6,4},{7,5},{8,14},{9,15},{10,... | collective-permute-start | bytes 1179656 | tf_op jit(solution)/shard_map/ppermute | solution.py:182
  53.4 23.8 %collective-permute-start.2 = (bf16[256,768]{1,0:T(8,128)(2,1)}, bf16[256,768]{1,0:T(8,128)(2,1)S(1)}, u32[]{:S(2)}, u32[]{:S(2)}) collective-permute-start(bf16[256,768]{1,0:T(8,128)(2,1)} %get-tuple-element.19), channel_id=1, source_target_pairs={{0,2},{1,3},{2,4},{3,5},{4,6},{5,7},{6,0},{7,1},{8,10},{9,11},{10,... | collective-permute-start | bytes 1179656 | tf_op jit(solution)/shard_map/ppermute | solution.py:183
  54.2 23.0 %collective-permute-start.3 = (bf16[256,768]{1,0:T(8,128)(2,1)}, bf16[256,768]{1,0:T(8,128)(2,1)}, u32[]{:S(2)}, u32[]{:S(2)}) collective-permute-start(bf16[256,768]{1,0:T(8,128)(2,1)} %get-tuple-element.20), channel_id=1, source_target_pairs={{0,6},{1,7},{2,0},{3,1},{4,2},{5,3},{6,4},{7,5},{8,14},{9,15},{10,... | collective-permute-start | bytes 1179656 | tf_op jit(solution)/shard_map/ppermute | solution.py:184
  68.8 16.6 %collective-permute-start.5 = (bf16[256,768]{1,0:T(8,128)(2,1)S(1)}, bf16[256,768]{1,0:T(8,128)(2,1)}, u32[]{:S(2)}, u32[]{:S(2)}) collective-permute-start(bf16[256,768]{1,0:T(8,128)(2,1)S(1)} %collective-permute-done.1.left_top), channel_id=1, source_target_pairs={{0,2},{1,3},{2,4},{3,5},{4,6},{5,7},{6,0},{7,1},{8,10},{9,11},{10,... | collective-permute-start | bytes 1179656 | tf_op jit(solution)/shard_map/ppermute | solution.py:185
  68.8 16.6 %collective-permute-start.6 = (bf16[256,768]{1,0:T(8,128)(2,1)S(1)}, bf16[256,768]{1,0:T(8,128)(2,1)}, u32[]{:S(2)}, u32[]{:S(2)}) collective-permute-start(bf16[256,768]{1,0:T(8,128)(2,1)S(1)} %collective-permute-done.4.right_low), channel_id=1, source_target_pairs={{0,6},{1,7},{2,0},{3,1},{4,2},{5,3},{6,4},{7,5},{8,14},{9,15},{10,... | collective-permute-start | bytes 1179656 | tf_op jit(solution)/shard_map/ppermute | solution.py:186
  73.6 11.8 %collective-permute-start = (bf16[3,256,256]{2,1,0:T(8,128)(2,1)}, bf16[3,256,256]{2,1,0:T(8,128)(2,1)S(1)}, u32[]{:S(2)}, u32[]{:S(2)}) collective-permute-start(bf16[3,256,256]{2,1,0:T(8,128)(2,1)} %get-tuple-element.15), channel_id=1, source_target_pairs={{0,1},{1,0},{2,3},{3,2},{4,5},{5,4},{6,7},{7,6},{8,9},{9,8},{10,11... | collective-permute-start | bytes 1179656 | tf_op jit(solution)/shard_map/ppermute | solution.py:236
  88.9 4.9 %collective-permute-start.7 = (f32[2,1,768]{2,1,0:T(1,128)S(1)}, f32[2,1,768]{2,1,0:T(1,128)S(1)}, u32[]{:S(2)}, u32[]{:S(2)}) collective-permute-start(f32[2,1,768]{2,1,0:T(1,128)S(1)} %get-tuple-element.17), channel_id=1, source_target_pairs={{0,6},{1,7},{2,4},{3,5},{4,2},{5,3},{6,0},{7,1},{8,14},{9,15},{10,... | collective-permute-start | bytes 18440 | tf_op jit(solution)/shard_map/ppermute | solution.py:255
  93.8 3.6 %collective-permute-start.8 = (f32[1,768]{1,0:T(1,128)S(1)}, f32[1,768]{1,0:T(1,128)S(1)}, u32[]{:S(2)}, u32[]{:S(2)}) collective-permute-start(f32[1,768]{1,0:T(1,128)S(1)} %fusion), channel_id=1, source_target_pairs={{0,2},{1,3},{2,0},{3,1},{4,6},{5,7},{6,4},{7,5},{8,10},{9,11},{10,... | collective-permute-start | bytes 9224 | tf_op jit(solution)/shard_map/ppermute | solution.py:257
